TPU v7x, 32 devices: a whole 2x2x4 slice. The times are simulated.
32 devices in a mesh: dp: 8 (over y, x, core), seq: 4 (over z).
Axes of the slice: x: 2, y: 2, z: 4, core: 2. Of those that a mesh axis runs over, the one named last changes fastest.
Arguments:
- tokens: bfloat16 [16, 1024, 1536], P('dp', 'seq'), may hold values from -6 to 6
- cotangent: bfloat16 [16, 1024, 1536], P('dp', 'seq'), may hold values from -6 to 6
- parents: int32 [16, 8], P('dp'), may hold values from 0 to 7, as said below
- adapter_ids: int32 [16], P('dp'), may hold values from 0 to 7
- attention_gain: float32 [1536], replicated, may hold values from 0.5 to 1.5
- mixer_weight: bfloat16 [1536, 6144], P('dp'), may hold values from -0.15625 to 0.15625
- forget_weight: bfloat16 [1536, 24], P('dp'), may hold values from -0.15625 to 0.15625
- forget_bias: float32 [24], replicated, may hold values from 1.5 to 8
- output_weight: bfloat16 [1536, 1536], P('dp'), may hold values from -1.75 to 1.75
- feedforward_gain: float32 [1536], replicated, may hold values from 0.5 to 1.5
- swiglu_weight: bfloat16 [1536, 8192], P('dp'), may hold values from -0.15625 to 0.15625
- down_weight: bfloat16 [4096, 1536], P('dp'), may hold values from -0.09375 to 0.09375
- adapter_inner: bfloat16 [8, 1536, 128], P(None, 'dp'), may hold values from -0.15625 to 0.15625
- adapter_hidden: bfloat16 [8, 4096, 16], P(None, 'dp'), may hold values from -0.09375 to 0.09375
- adapter_model: bfloat16 [8, 80, 1536], P(None, None, 'dp'), may hold values from -1.5 to 1.5
- adapter_project: bfloat16 [8, 16, 1536], P(None, None, 'dp'), may hold values from -4 to 4
- adapter_swiglu: bfloat16 [8, 32, 4096], P(None, None, 'dp'), may hold values from -1.5 to 1.5
- adapter_forget: bfloat16 [128, 24], P('dp'), may hold values from -1.5 to 1.5
Outputs:
- block_output: bfloat16 [16, 1024, 1536], P('dp', 'seq')
- tokens_grad: float32 [16, 1024, 1536], P('dp', 'seq')
- inner_grad: float32 [8, 1536, 128], P(None, 'dp')
- hidden_grad: float32 [8, 4096, 16], P(None, 'dp')
- model_grad: float32 [8, 80, 1536], P(None, None, 'dp')
- project_grad: float32 [8, 16, 1536], P(None, None, 'dp')
- swiglu_grad: float32 [8, 32, 4096], P(None, None, 'dp')
- forget_grad: float32 [128, 24], P('dp')
Inputs may be any that keep to these rules, and one draw needn't show every extreme that they name: `parents`: in every row, entries 0 to 3 are 0, 0, 1, 2. Of blocks 4 to 7, two have parent 3, and each of the other two has one of those two as parent, a different one.
All inputs are finite; a program needn't handle non-finite values.
Results may differ from a plain program's by a relative error of at most 0.02.
Values may be sent and summed in bfloat16 or wider, within the bound.
A program may use at most 216 MiB of HBM per device.

v0:
```python
import jax
import jax.numpy as jnp
from jax import lax
from jax.sharding import PartitionSpec as P

D = 1536
H = 24
HD = 64
FF = 4096
RANK = 16
ADAPTERS = 8
BLOCK = 128
TREE_LEN = 1024


highest = lax.Precision.HIGHEST
epsilon = 1e-06


def linear(left, right):
    return jnp.dot(left, right, preferred_element_type=jnp.float32)


def linear_back(left, right):
    return lax.dot_general(
        left, right, (((1,), (1,)), ((), ())), preferred_element_type=jnp.float32
    )


def linear_grad(left, right):
    return lax.dot_general(
        left, right, (((0,), (0,)), ((), ())), preferred_element_type=jnp.float32
    )


def rms_scale(values):
    return lax.rsqrt(jnp.mean(values * values, axis=-1, keepdims=True) + epsilon)


def norm_back(values, gain, upstream):
    scale_rows = rms_scale(values)
    unit = values * scale_rows
    inner = upstream * gain
    return scale_rows * (inner - unit * jnp.mean(inner * unit, axis=-1, keepdims=True))


def ancestry(parent_row):
    blocks = jnp.arange(8, dtype=jnp.int32)
    step_up = ((parent_row[:, None] == blocks[None, :]) & (blocks[:, None] != 0)).astype(
        jnp.float32
    )
    reach = jnp.eye(8, dtype=jnp.float32)
    power = reach
    for level in range(7):
        power = jnp.dot(power, step_up, precision=highest)
        reach = reach + power
    return reach


def add_at(total, piece, which):
    current = lax.dynamic_index_in_dim(total, which, 0, keepdims=False)
    return lax.dynamic_update_index_in_dim(total, current + piece, which, 0)


def to_owners(grads):
    return (
        lax.psum_scatter(grads[0], "dp", scatter_dimension=1, tiled=True),
        lax.psum_scatter(grads[1], "dp", scatter_dimension=1, tiled=True),
        lax.psum_scatter(grads[2], "dp", scatter_dimension=2, tiled=True),
        lax.psum_scatter(grads[3], "dp", scatter_dimension=2, tiled=True),
        lax.psum_scatter(grads[4], "dp", scatter_dimension=2, tiled=True),
        lax.psum_scatter(grads[5], "dp", scatter_dimension=0, tiled=True),
    )


def body(
    tokens,
    cotangent,
    parents,
    adapter_ids,
    attention_gain,
    mixer_weight,
    forget_weight,
    forget_bias,
    output_weight,
    feedforward_gain,
    swiglu_weight,
    down_weight,
    adapter_inner,
    adapter_hidden,
    adapter_model,
    adapter_project,
    adapter_swiglu,
    adapter_forget,
):
    owned = (
        mixer_weight,
        forget_weight,
        output_weight,
        swiglu_weight,
        down_weight,
        adapter_inner,
        adapter_hidden,
        adapter_model,
        adapter_project,
        adapter_swiglu,
        adapter_forget,
    )
    rows = tokens.shape[1]
    seq_start = lax.axis_index("seq") * rows
    query_pos = seq_start + jnp.arange(rows, dtype=jnp.int32)
    key_pos = jnp.arange(TREE_LEN, dtype=jnp.int32)
    block_ids = jnp.arange(8, dtype=jnp.int32)
    scale = HD ** (-0.5)
    eye_blocks = jnp.eye(8, dtype=jnp.float32)

    def one_tree(tree_index, state):
        outputs, input_grads, accum = state
        full = (
            lax.all_gather(owned[0], "dp", axis=0, tiled=True),
            lax.all_gather(owned[1], "dp", axis=0, tiled=True),
            lax.all_gather(owned[2], "dp", axis=0, tiled=True),
            lax.all_gather(owned[3], "dp", axis=0, tiled=True),
            lax.all_gather(owned[4], "dp", axis=0, tiled=True),
            lax.all_gather(owned[5], "dp", axis=1, tiled=True),
            lax.all_gather(owned[6], "dp", axis=1, tiled=True),
            lax.all_gather(owned[7], "dp", axis=2, tiled=True),
            lax.all_gather(owned[8], "dp", axis=2, tiled=True),
            lax.all_gather(owned[9], "dp", axis=2, tiled=True),
            lax.all_gather(owned[10], "dp", axis=0, tiled=True),
        )
        (
            w_mix,
            w_forget,
            w_out,
            w_swiglu,
            w_down,
            a_inner,
            a_hidden,
            b_model,
            b_project,
            b_swiglu,
            b_forget,
        ) = full
        which = lax.dynamic_index_in_dim(adapter_ids, tree_index, 0, keepdims=False)
        parent_row = lax.dynamic_index_in_dim(parents, tree_index, 0, keepdims=False)
        inner_sel = lax.dynamic_index_in_dim(a_inner, which, 0, keepdims=False)
        hidden_sel = lax.dynamic_index_in_dim(a_hidden, which, 0, keepdims=False)
        model_sel = lax.dynamic_index_in_dim(b_model, which, 0, keepdims=False)
        project_sel = lax.dynamic_index_in_dim(b_project, which, 0, keepdims=False)
        swiglu_sel = lax.dynamic_index_in_dim(b_swiglu, which, 0, keepdims=False)
        forget_sel = lax.dynamic_slice_in_dim(b_forget, which * RANK, RANK, 0)
        inputs = lax.dynamic_index_in_dim(tokens, tree_index, 0, keepdims=False).astype(jnp.float32)
        upstream = lax.dynamic_index_in_dim(cotangent, tree_index, 0, keepdims=False).astype(
            jnp.float32
        )
        first_norm = (inputs * rms_scale(inputs) * attention_gain).astype(jnp.bfloat16)
        inner_low = linear(first_norm, inner_sel[:, : 5 * RANK]).astype(jnp.bfloat16)
        side = jnp.einsum(
            "tpr,prd->tpd",
            inner_low[:, : 4 * RANK].reshape(rows, 4, RANK),
            model_sel[: 4 * RANK].reshape(4, RANK, D),
            preferred_element_type=jnp.float32,
        )
        mix = linear(first_norm, w_mix) + side.reshape(rows, 4 * D)
        queries = mix[:, :D].astype(jnp.bfloat16)
        keys_mine = mix[:, D : 2 * D].astype(jnp.bfloat16)
        values_mine = mix[:, 2 * D : 3 * D].astype(jnp.bfloat16)
        gate_logit = mix[:, 3 * D :]
        forget_logit = (
            linear(first_norm, w_forget)
            + linear(inner_low[:, 4 * RANK :], forget_sel)
            + forget_bias
        ).astype(jnp.bfloat16)
        keys_all, values_all, forget_all = (
            lax.all_gather(keys_mine, "seq", axis=0, tiled=True),
            lax.all_gather(values_mine, "seq", axis=0, tiled=True),
            lax.all_gather(forget_logit, "seq", axis=0, tiled=True),
        )
        reach = ancestry(parent_row)
        strict = reach - eye_blocks
        log_forget = jax.nn.log_sigmoid(forget_all.astype(jnp.float32)).T.reshape(H, 8, BLOCK)
        within = jnp.cumsum(log_forget, axis=2)
        offsets = jnp.dot(within[:, :, BLOCK - 1], strict.T, precision=highest)
        path_sum = (within + offsets[:, :, None]).reshape(H, TREE_LEN)
        mine_sum = lax.dynamic_slice_in_dim(path_sum, seq_start, rows, 1)
        query_blk = query_pos // BLOCK
        key_blk = key_pos // BLOCK
        pick_query = (query_blk[:, None] == block_ids[None, :]).astype(jnp.float32)
        pick_key = (key_blk[:, None] == block_ids[None, :]).astype(jnp.float32)
        linked = jnp.dot(
            jnp.dot(pick_query, reach, precision=highest), pick_key.T, precision=highest
        )
        allowed = (linked > 0.5) & (
            (query_blk[:, None] != key_blk[None, :]) | (key_pos[None, :] <= query_pos[:, None])
        )
        query_heads = queries.reshape(rows, H, HD)
        key_heads = keys_all.reshape(TREE_LEN, H, HD)
        value_heads = values_all.reshape(TREE_LEN, H, HD)

        def scores_of():
            raw = (
                jnp.einsum(
                    "thd,shd->hts", query_heads, key_heads, preferred_element_type=jnp.float32
                )
                * scale
            )
            raw = raw + mine_sum[:, :, None] - path_sum[:, None, :]
            return jnp.where(allowed[None], raw, -1e30)

        scores = scores_of()
        peak = jnp.max(scores, axis=2, keepdims=True)
        expo = jnp.exp(scores - peak)
        totals = jnp.sum(expo, axis=2, keepdims=True)
        log_total = peak + jnp.log(totals)
        attended = jnp.einsum(
            "hts,shd->thd",
            (expo / totals).astype(jnp.bfloat16),
            value_heads,
            preferred_element_type=jnp.float32,
        ).reshape(rows, D)
        gate_open = jax.nn.sigmoid(gate_logit)
        gated = (attended * gate_open).astype(jnp.bfloat16)
        project_low = linear(gated, inner_sel[:, 5 * RANK : 6 * RANK]).astype(jnp.bfloat16)
        middle = inputs + linear(gated, w_out) + linear(project_low, project_sel)
        second_norm = (middle * rms_scale(middle) * feedforward_gain).astype(jnp.bfloat16)
        swiglu_low = linear(second_norm, inner_sel[:, 6 * RANK :]).astype(jnp.bfloat16)
        lifted_side = jnp.einsum(
            "tpr,prf->tpf",
            swiglu_low.reshape(rows, 2, RANK),
            swiglu_sel.reshape(2, RANK, FF),
            preferred_element_type=jnp.float32,
        )
        lifted = linear(second_norm, w_swiglu) + lifted_side.reshape(rows, 2 * FF)
        gate_part = lifted[:, :FF]
        up_part = lifted[:, FF:]
        activated = (jax.nn.silu(gate_part) * up_part).astype(jnp.bfloat16)
        hidden_low = linear(activated, hidden_sel).astype(jnp.bfloat16)
        result = middle + linear(activated, w_down) + linear(hidden_low, model_sel[4 * RANK :])
        outputs = lax.dynamic_update_index_in_dim(
            outputs, result.astype(jnp.bfloat16), tree_index, 0
        )
        feed_grad = upstream.astype(jnp.bfloat16)
        hidden_low_grad = linear_back(feed_grad, model_sel[4 * RANK :]).astype(jnp.bfloat16)
        activated_grad = linear_back(feed_grad, w_down) + linear_back(hidden_low_grad, hidden_sel)
        sig_gate = jax.nn.sigmoid(gate_part)
        gate_grad = activated_grad * up_part * sig_gate * (1.0 + gate_part * (1.0 - sig_gate))
        up_grad = activated_grad * gate_part * sig_gate
        lifted_grad = jnp.concatenate([gate_grad, up_grad], axis=1).astype(jnp.bfloat16)
        swiglu_low_grad = (
            jnp.einsum(
                "tpf,prf->tpr",
                lifted_grad.reshape(rows, 2, FF),
                swiglu_sel.reshape(2, RANK, FF),
                preferred_element_type=jnp.float32,
            )
            .reshape(rows, 2 * RANK)
            .astype(jnp.bfloat16)
        )
        second_grad = linear_back(lifted_grad, w_swiglu) + linear_back(
            swiglu_low_grad, inner_sel[:, 6 * RANK :]
        )
        middle_grad = upstream + norm_back(middle, feedforward_gain, second_grad)
        branch_grad = middle_grad.astype(jnp.bfloat16)
        project_low_grad = linear_back(branch_grad, project_sel).astype(jnp.bfloat16)
        gated_grad = linear_back(branch_grad, w_out) + linear_back(
            project_low_grad, inner_sel[:, 5 * RANK : 6 * RANK]
        )
        attended_grad = (gated_grad * gate_open).astype(jnp.bfloat16)
        gate_logit_grad = gated_grad * attended * gate_open * (1.0 - gate_open)
        grad_heads = attended_grad.reshape(rows, H, HD)
        probs = jnp.exp(scores_of() - log_total)
        prob_grad = jnp.einsum(
            "thd,shd->hts", grad_heads, value_heads, preferred_element_type=jnp.float32
        )
        row_dot = jnp.sum(probs * prob_grad, axis=2, keepdims=True)
        score_grad = (probs * (prob_grad - row_dot)).astype(jnp.bfloat16)
        low_probs = probs.astype(jnp.bfloat16)
        query_grad = (
            jnp.einsum(
                "hts,shd->thd", score_grad, key_heads, preferred_element_type=jnp.float32
            ).reshape(rows, D)
            * scale
        )
        key_part = (
            jnp.einsum(
                "hts,thd->shd", score_grad, query_heads, preferred_element_type=jnp.float32
            ).reshape(rows * lax.axis_size("seq"), D)
            * scale
        )
        value_part = jnp.einsum(
            "hts,thd->shd", low_probs, grad_heads, preferred_element_type=jnp.float32
        ).reshape(rows * lax.axis_size("seq"), D)
        kv_grad = lax.psum_scatter(
            jnp.concatenate([key_part, value_part], axis=1).astype(jnp.bfloat16),
            "seq",
            scatter_dimension=0,
            tiled=True,
        ).astype(jnp.float32)
        key_decay = -jnp.sum(score_grad, axis=1, dtype=jnp.float32)
        query_decay = jnp.sum(score_grad, axis=2, dtype=jnp.float32)
        own_decay = lax.dynamic_slice_in_dim(key_decay, seq_start, rows, 1) + query_decay
        decay_term = lax.dynamic_update_slice_in_dim(key_decay, own_decay, seq_start, 1)
        decay_all = lax.psum(decay_term, "seq").reshape(H, 8, BLOCK)
        below = jnp.dot(jnp.sum(decay_all, axis=2), strict, precision=highest)
        suffix = jnp.flip(jnp.cumsum(jnp.flip(decay_all, 2), axis=2), 2) + below[:, :, None]
        logf_grad = lax.dynamic_slice_in_dim(suffix.reshape(H, TREE_LEN), seq_start, rows, 1).T
        forget_grad_low = (logf_grad * jax.nn.sigmoid(-forget_logit.astype(jnp.float32))).astype(
            jnp.bfloat16
        )
        mix_grad = jnp.concatenate(
            [query_grad, kv_grad[:, :D], kv_grad[:, D:], gate_logit_grad], axis=1
        ).astype(jnp.bfloat16)
        mix_low_grad = jnp.einsum(
            "tpd,prd->tpr",
            mix_grad.reshape(rows, 4, D),
            model_sel[: 4 * RANK].reshape(4, RANK, D),
            preferred_element_type=jnp.float32,
        ).reshape(rows, 4 * RANK)
        inner_low_grad = jnp.concatenate(
            [mix_low_grad, linear_back(forget_grad_low, forget_sel)], axis=1
        ).astype(jnp.bfloat16)
        first_grad = (
            linear_back(mix_grad, w_mix)
            + linear_back(forget_grad_low, w_forget)
            + linear_back(inner_low_grad, inner_sel[:, : 5 * RANK])
        )
        input_grad = middle_grad + norm_back(inputs, attention_gain, first_grad)
        input_grads = lax.dynamic_update_index_in_dim(input_grads, input_grad, tree_index, 0)
        inner_piece = jnp.concatenate(
            [
                linear_grad(first_norm, inner_low_grad),
                linear_grad(gated, project_low_grad),
                linear_grad(second_norm, swiglu_low_grad),
            ],
            axis=1,
        )
        hidden_piece = linear_grad(activated, hidden_low_grad)
        model_mix = jnp.einsum(
            "tpr,tpd->prd",
            inner_low[:, : 4 * RANK].reshape(rows, 4, RANK),
            mix_grad.reshape(rows, 4, D),
            preferred_element_type=jnp.float32,
        ).reshape(4 * RANK, D)
        model_piece = jnp.concatenate([model_mix, linear_grad(hidden_low, feed_grad)], axis=0)
        project_piece = linear_grad(project_low, branch_grad)
        swiglu_piece = jnp.einsum(
            "tpr,tpf->prf",
            swiglu_low.reshape(rows, 2, RANK),
            lifted_grad.reshape(rows, 2, FF),
            preferred_element_type=jnp.float32,
        ).reshape(2 * RANK, FF)
        forget_piece = linear_grad(inner_low[:, 4 * RANK :], forget_grad_low)
        inner_total, hidden_total, model_total, project_total, swiglu_total, forget_total = accum
        forget_now = lax.dynamic_slice_in_dim(forget_total, which * RANK, RANK, 0)
        accum = (
            add_at(inner_total, inner_piece, which),
            add_at(hidden_total, hidden_piece, which),
            add_at(model_total, model_piece, which),
            add_at(project_total, project_piece, which),
            add_at(swiglu_total, swiglu_piece, which),
            lax.dynamic_update_slice_in_dim(
                forget_total, forget_now + forget_piece, which * RANK, 0
            ),
        )
        return (outputs, input_grads, accum)

    zeros = (
        jnp.zeros((ADAPTERS, D, 8 * RANK), jnp.float32),
        jnp.zeros((ADAPTERS, FF, RANK), jnp.float32),
        jnp.zeros((ADAPTERS, 5 * RANK, D), jnp.float32),
        jnp.zeros((ADAPTERS, RANK, D), jnp.float32),
        jnp.zeros((ADAPTERS, 2 * RANK, FF), jnp.float32),
        jnp.zeros((ADAPTERS * RANK, H), jnp.float32),
    )
    start_state = (
        jnp.zeros(tokens.shape, jnp.bfloat16),
        jnp.zeros(tokens.shape, jnp.float32),
        zeros,
    )
    outputs, input_grads, accum = lax.fori_loop(0, tokens.shape[0], one_tree, start_state)
    summed = (
        lax.psum(accum[0].astype(jnp.bfloat16), "seq").astype(jnp.float32),
        lax.psum(accum[1].astype(jnp.bfloat16), "seq").astype(jnp.float32),
        lax.psum(accum[2].astype(jnp.bfloat16), "seq").astype(jnp.float32),
        lax.psum(accum[3].astype(jnp.bfloat16), "seq").astype(jnp.float32),
        lax.psum(accum[4].astype(jnp.bfloat16), "seq").astype(jnp.float32),
        lax.psum(accum[5].astype(jnp.bfloat16), "seq").astype(jnp.float32),
    )
    owned_grads = to_owners(summed)
    return (
        outputs,
        input_grads,
        owned_grads[0],
        owned_grads[1],
        owned_grads[2],
        owned_grads[3],
        owned_grads[4],
        owned_grads[5],
    )


def solution(mesh):
    placed = (
        P("dp", "seq", None),
        P("dp", "seq", None),
        P("dp", None),
        P("dp"),
        P(),
        P("dp", None),
        P("dp", None),
        P(),
        P("dp", None),
        P(),
        P("dp", None),
        P("dp", None),
        P(None, "dp", None),
        P(None, "dp", None),
        P(None, None, "dp"),
        P(None, None, "dp"),
        P(None, None, "dp"),
        P("dp", None),
    )
    return jax.shard_map(
        body,
        mesh=mesh,
        in_specs=placed,
        out_specs=(
            P("dp", "seq", None),
            P("dp", "seq", None),
            P(None, "dp", None),
            P(None, "dp", None),
            P(None, None, "dp"),
            P(None, None, "dp"),
            P(None, None, "dp"),
            P("dp", None),
        ),
        check_vma=False,
    )
```

profile of v0, /device:TPU:0, one launch (start us, length us, event | category | flops | bytes accessed | tf_op | source)
XLA Modules:
  0.0 2411.1 jit_solution(10180221446027901801)
XLA Ops:
  22.8 1763.2 %while.33 = (s32[]{:T(128)}, bf16[2,256,1536]{2,1,0:T(8,128)(2,1)}, f32[2,256,1536]{2,1,0:T(8,128)}, f32[8,1536,128]{2,1,0:T(8,128)}, f32[8,4096,16]{1,2,0:T(8,1...) while((s32[]{:T(128)}, bf16[2,256,1536]{2,1,0:T(8,128)(2,1)}, ...), condition=%wide.region_15.16_spmd.clone.clone.clone, body=%wide.region_0.15_spmd.clone.clone.clone.sunk | while | flops 37383176192 | bytes 1113380736 | solution.py:381
  30.8 30.5 %all-gather.16.cloned.1.call-done = bf16[8,80,1536]{1,0,2:T(8,128)(2,1)} async-done(((bf16[8,80,192]{1,0,2:T(8,128)(2,1)}), bf16[8,80,1536]{1,0,2:T(8,128)(2,1)}) %all-gather.16.cloned.1.call-update) | async-done | bytes 1966096 | tf_op jit(solution)/shard_map/while/body/eval_jaxpr/all_gather | solution.py:127
  64.1 31.6 %all-gather.18.cloned.1.call-done = bf16[8,1536,128]{2,1,0:T(8,128)(2,1)} async-done(((bf16[8,192,128]{2,1,0:T(8,128)(2,1)}), bf16[8,1536,128]{2,1,0:T(8,128)(2,1)}) %all-gather.18.cloned.1.call-update) | async-done | bytes 3145744 | tf_op jit(solution)/shard_map/while/body/eval_jaxpr/all_gather | solution.py:125
  109.1 87.4 %all-gather.20.cloned.1.call-done = bf16[1536,6144]{1,0:T(8,128)(2,1)} async-done(((bf16[192,6144]{1,0:T(8,128)(2,1)}), bf16[1536,6144]{1,0:T(8,128)(2,1)}) %all-gather.20.cloned.1.call-update) | async-done | bytes 18874384 | tf_op jit(solution)/shard_map/while/body/eval_jaxpr/all_gather | solution.py:120
  196.6 12.9 fusion.448
  216.5 9.4 all-gather.4
  227.6 8.4 all_gather.211
  236.1 33.2 %all_gather.215 = bf16[8,16,1536]{1,0,2:T(8,128)(2,1)S(1)} all-gather(bf16[8,16,192]{1,0,2:T(8,128)(2,1)} %get-tuple-element.1594), channel_id=1, replica_groups=mesh['dp'=8,'seq'=4] {'dp'}, dimensions={2}, use_global_device_ids=true | all-gather | bytes 442368 | tf_op jit(solution)/shard_map/while/body/eval_jaxpr/all_gather | solution.py:128
  281.5 13.6 all_gather.212
  303.2 10.5 all-gather.32.cloned.1.call-done
  313.8 10.2 fusion.468
  325.2 53.6 %all-gather.24.cloned.1.call-done = bf16[1024,1536]{1,0:T(8,128)(2,1)} async-done(((bf16[256,1536]{1,0:T(8,128)(2,1)}), bf16[1024,1536]{1,0:T(8,128)(2,1)}) %all-gather.24.cloned.1.call-update) | async-done | bytes 3145744 | tf_op jit(solution)/shard_map/while/body/eval_jaxpr/all_gather | solution.py:176
  382.0 13.5 fusion.464
  395.6 11.1 fusion.465
  407.9 34.8 %all-gather.22.cloned.1.call-done = bf16[1024,1536]{1,0:T(8,128)(2,1)} async-done(((bf16[256,1536]{1,0:T(8,128)(2,1)}), bf16[1024,1536]{1,0:T(8,128)(2,1)}) %all-gather.22.cloned.1.call-update) | async-done | bytes 3145744 | tf_op jit(solution)/shard_map/while/body/eval_jaxpr/all_gather | solution.py:177
  445.9 13.1 fusion.466
  463.8 18.6 all-gather.26.cloned.1.call-done
  493.9 9.4 copy.151
  503.3 106.5 %all-gather.30.cloned.1.call-done = bf16[1536,8192]{1,0:T(8,128)(2,1)} async-done(((bf16[192,8192]{1,0:T(8,128)(2,1)}), bf16[1536,8192]{1,0:T(8,128)(2,1)}) %all-gather.30.cloned.1.call-update) | async-done | bytes 25165840 | tf_op jit(solution)/shard_map/while/body/eval_jaxpr/all_gather | solution.py:123
  609.7 18.6 convolution_add_fusion.21
  646.1 13.0 fusion.470
  671.9 17.7 multiply_reduce_fusion.8
  689.6 13.5 fusion.475
  703.1 17.6 convert_reduce_fusion.3
  766.0 9.6 convolution_multiply_fusion.2
  779.3 13.4 reduce_window_sum.42
  801.9 72.2 %reduce-scatter.24.cloned.1.call-done = bf16[256,3072]{0,1:T(8,128)(2,1)} async-done(((bf16[1024,3072]{0,1:T(8,128)(2,1)}), bf16[256,3072]{0,1:T(8,128)(2,1)}) %reduce-scatter.24.cloned.1.call-update) | async-done | bytes 1572880 | tf_op jit(solution)/shard_map/while/body/eval_jaxpr/reduce_scatter | solution.py:294
  886.5 11.6 fusion.478
  911.1 28.6 %all-gather.16.cloned.1.call-done = bf16[8,80,1536]{1,0,2:T(8,128)(2,1)} async-done(((bf16[8,80,192]{1,0,2:T(8,128)(2,1)}), bf16[8,80,1536]{1,0,2:T(8,128)(2,1)}) %all-gather.16.cloned.1.call-update) | async-done | bytes 1966096 | tf_op jit(solution)/shard_map/while/body/eval_jaxpr/all_gather | solution.py:127
  942.5 31.5 %all-gather.18.cloned.1.call-done = bf16[8,1536,128]{2,1,0:T(8,128)(2,1)} async-done(((bf16[8,192,128]{2,1,0:T(8,128)(2,1)}), bf16[8,1536,128]{2,1,0:T(8,128)(2,1)}) %all-gather.18.cloned.1.call-update) | async-done | bytes 3145744 | tf_op jit(solution)/shard_map/while/body/eval_jaxpr/all_gather | solution.py:125
  987.4 87.3 %all-gather.20.cloned.1.call-done = bf16[1536,6144]{1,0:T(8,128)(2,1)} async-done(((bf16[192,6144]{1,0:T(8,128)(2,1)}), bf16[1536,6144]{1,0:T(8,128)(2,1)}) %all-gather.20.cloned.1.call-update) | async-done | bytes 18874384 | tf_op jit(solution)/shard_map/while/body/eval_jaxpr/all_gather | solution.py:120
  1074.6 12.8 fusion.448
  1094.5 9.4 all-gather.4
  1105.7 8.3 all_gather.211
  1114.0 33.2 %all_gather.215 = bf16[8,16,1536]{1,0,2:T(8,128)(2,1)S(1)} all-gather(bf16[8,16,192]{1,0,2:T(8,128)(2,1)} %get-tuple-element.1594), channel_id=1, replica_groups=mesh['dp'=8,'seq'=4] {'dp'}, dimensions={2}, use_global_device_ids=true | all-gather | bytes 442368 | tf_op jit(solution)/shard_map/while/body/eval_jaxpr/all_gather | solution.py:128
  1159.5 13.6 all_gather.212
  1181.2 10.6 all-gather.32.cloned.1.call-done
  1191.8 10.2 fusion.468
  1203.2 53.6 %all-gather.24.cloned.1.call-done = bf16[1024,1536]{1,0:T(8,128)(2,1)} async-done(((bf16[256,1536]{1,0:T(8,128)(2,1)}), bf16[1024,1536]{1,0:T(8,128)(2,1)}) %all-gather.24.cloned.1.call-update) | async-done | bytes 3145744 | tf_op jit(solution)/shard_map/while/body/eval_jaxpr/all_gather | solution.py:176
  1260.1 13.6 fusion.464
  1273.6 11.1 fusion.465
  1286.0 34.8 %all-gather.22.cloned.1.call-done = bf16[1024,1536]{1,0:T(8,128)(2,1)} async-done(((bf16[256,1536]{1,0:T(8,128)(2,1)}), bf16[1024,1536]{1,0:T(8,128)(2,1)}) %all-gather.22.cloned.1.call-update) | async-done | bytes 3145744 | tf_op jit(solution)/shard_map/while/body/eval_jaxpr/all_gather | solution.py:177
  1323.9 13.1 fusion.466
  1341.8 18.4 all-gather.26.cloned.1.call-done
  1371.8 9.4 copy.151
  1381.1 106.5 %all-gather.30.cloned.1.call-done = bf16[1536,8192]{1,0:T(8,128)(2,1)} async-done(((bf16[192,8192]{1,0:T(8,128)(2,1)}), bf16[1536,8192]{1,0:T(8,128)(2,1)}) %all-gather.30.cloned.1.call-update) | async-done | bytes 25165840 | tf_op jit(solution)/shard_map/while/body/eval_jaxpr/all_gather | solution.py:123
  1487.6 18.6 convolution_add_fusion.21
  1513.3 7.0 multiply_convert_fusion.16
  1524.1 13.0 fusion.470
  1549.9 17.7 multiply_reduce_fusion.8
  1567.6 13.5 fusion.475
  1581.2 17.6 convert_reduce_fusion.3
  1644.0 9.6 convolution_multiply_fusion.2
  1657.3 13.4 reduce_window_sum.42
  1679.9 72.2 %reduce-scatter.24.cloned.1.call-done = bf16[256,3072]{0,1:T(8,128)(2,1)} async-done(((bf16[1024,3072]{0,1:T(8,128)(2,1)}), bf16[256,3072]{0,1:T(8,128)(2,1)}) %reduce-scatter.24.cloned.1.call-update) | async-done | bytes 1572880 | tf_op jit(solution)/shard_map/while/body/eval_jaxpr/reduce_scatter | solution.py:294
  1764.6 11.6 fusion.478
  1800.4 302.5 %all-reduce.4.cloned.1.call-done = (bf16[8,1536,128]{2,1,0:T(8,128)(2,1)}, bf16[8,4096,16]{1,2,0:T(8,128)(2,1)}, bf16[8,80,1536]{2,1,0:T(8,128)(2,1)}, bf16[8,16,1536]{2,1,0:T(8,128)(2,1)}, bf16[8,32,4096]{2,1,0:T(8,128)(2,1)}) async-done(((bf16[8,1536,128]{2,1,0:T(8,128)(2,1)}, bf16[8,4096,16]{1,2,0:T(8,128)(2,1)}, bf16[8,80,1536]{2,1,0:T(8,128)(2,1)}, bf16[8,16,1536]{2,1,0:T(8,128)(2,1)}, ...) | async-done | bytes 8650768 | tf_op jit(solution)/shard_map/psum | solution.py:383
  2116.9 7.1 reshape.643
  2124.8 16.8 psum.62
  2153.8 46.5 %reduce-scatter.20.cloned.1.call-done = f32[192,640]{1,0:T(8,128)} async-done(((f32[1536,640]{1,0:T(8,128)}), f32[192,640]{1,0:T(8,128)}) %reduce-scatter.20.cloned.1.call-update) | async-done | bytes 491536
  2202.9 34.5 %reduce-scatter.18.cloned.1.call-done = f32[16,24]{1,0:T(8,128)} async-done(((f32[128,24]{1,0:T(8,128)}), f32[16,24]{1,0:T(8,128)}) %reduce-scatter.18.cloned.1.call-update) | async-done | bytes 1552 | tf_op jit(solution)/shard_map/reduce_scatter | solution.py:72
  2237.4 45.1 %reduce-scatter.14.cloned.1.call-done = f32[8,512,16]{1,2,0:T(8,128)} async-done(((f32[8,4096,16]{1,2,0:T(8,128)}), f32[8,512,16]{1,2,0:T(8,128)}) %reduce-scatter.14.cloned.1.call-update) | async-done | bytes 262160 | tf_op jit(solution)/shard_map/reduce_scatter | solution.py:68
  2282.4 55.5 %reduce-scatter.16.cloned.1.call-done = f32[8,32,512]{2,1,0:T(8,128)} async-done(((f32[8,32,4096]{2,1,0:T(8,128)}), f32[8,32,512]{2,1,0:T(8,128)}) %reduce-scatter.16.cloned.1.call-update) | async-done | bytes 524304 | tf_op jit(solution)/shard_map/reduce_scatter | solution.py:71
  2337.9 65.4 %reduce-scatter.12.cloned.1.call-done = f32[8,192,128]{2,1,0:T(8,128)} async-done(((f32[8,1536,128]{2,1,0:T(8,128)}), f32[8,192,128]{2,1,0:T(8,128)}) %reduce-scatter.12.cloned.1.call-update) | async-done | bytes 786448 | tf_op jit(solution)/shard_map/reduce_scatter | solution.py:67
  (559 shorter events, 413.6 us)
Async XLA Ops:
  22.8 38.5 %all-gather.16.cloned.1.call-start = ((), (), s32[]{:S(2)}) async-start(), calls=%async_computation.14 | async-start | bytes 3538944 | tf_op jit(solution)/shard_map/while/body/eval_jaxpr/all_gather | solution.py:127
  23.6 72.2 %all-gather.18.cloned.1.call-start = ((), (), s32[]{:S(2)}) async-start(), calls=%async_computation.15 | async-start | bytes 3538944 | tf_op jit(solution)/shard_map/while/body/eval_jaxpr/all_gather | solution.py:125
  24.3 172.2 %all-gather.20.cloned.1.call-start = ((), (), s32[]{:S(2)}) async-start(), calls=%async_computation.16 | async-start | bytes 21233664 | tf_op jit(solution)/shard_map/while/body/eval_jaxpr/all_gather | solution.py:120
  25.1 254.0 %all-gather.28.cloned.1.call-start = ((), (), s32[]{:S(2)}) async-start(), calls=%async_computation.20 | async-start | bytes 2359296 | tf_op jit(solution)/shard_map/while/body/eval_jaxpr/all_gather | solution.py:129
  25.6 288.1 %all-gather.32.cloned.1.call-start = ((), (), s32[]{:S(2)}) async-start(), calls=%async_computation.22 | async-start | bytes 14155776 | tf_op jit(solution)/shard_map/while/body/eval_jaxpr/all_gather | solution.py:124
  26.2 352.6 %all-gather.24.cloned.1.call-start = ((), (), s32[]{:S(2)}) async-start(), calls=%async_computation.18 | async-start | bytes 3932160 | tf_op jit(solution)/shard_map/while/body/eval_jaxpr/all_gather | solution.py:176
  30.8 195.2 %copy-start.50 = (f32[256]{0:T(256)}, f32[256]{0:T(256)S(1)}, u32[]{:S(2)}) copy-start(f32[256]{0:T(256)S(1)} %add_rsqrt_fusion.4) | copy-start | bytes 3076 | tf_op jit(solution)/shard_map/while
  64.1 38.0 %copy-start.13 = (bf16[1,64,1536]{2,1,0:T(8,128)(2,1)}, bf16[1,64,1536]{2,1,0:T(8,128)(2,1)S(1)}, u32[]{:S(2)}) copy-start(bf16[1,64,1536]{2,1,0:T(8,128)(2,1)S(1)} %copy.140) | copy-start | bytes 589828 | tf_op jit(solution)/shard_map/while
  98.4 182.3 %copy-start.45 = (bf16[256,80]{0,1:T(8,128)(2,1)}, bf16[256,80]{0,1:T(8,128)(2,1)S(1)}, u32[]{:S(2)}) copy-start(bf16[256,80]{0,1:T(8,128)(2,1)S(1)} %convolution_convert_fusion.16) | copy-start | bytes 122884 | tf_op jit(solution)/shard_map/while
  210.8 231.9 %all-gather.22.cloned.1.call-start = ((), (), s32[]{:S(2)}) async-start(), calls=%async_computation.17 | async-start | bytes 3932160 | tf_op jit(solution)/shard_map/while/body/eval_jaxpr/all_gather | solution.py:177
  211.6 270.7 %all-gather.26.cloned.1.call-start = ((), (), s32[]{:S(2)}) async-start(), calls=%async_computation.19 | async-start | bytes 5308416 | tf_op jit(solution)/shard_map/while/body/eval_jaxpr/all_gather | solution.py:122
  212.3 397.4 %all-gather.30.cloned.1.call-start = ((), (), s32[]{:S(2)}) async-start(), calls=%async_computation.21 | async-start | bytes 28311552 | tf_op jit(solution)/shard_map/while/body/eval_jaxpr/all_gather | solution.py:123
  213.1 422.2 %all-gather.34.cloned.1.call-start = ((), (), s32[]{:S(2)}) async-start(), calls=%async_computation.23 | async-start | bytes 1179648 | tf_op jit(solution)/shard_map/while/body/eval_jaxpr/all_gather | solution.py:126
  213.7 564.0 %all-reduce.6.cloned.1.call-start = ((), (), s32[]{:S(2)}) async-start(), calls=%async_computation.24 | async-start | bytes 196608 | tf_op jit(solution)/shard_map/while/body/eval_jaxpr/psum | solution.py:304
  215.9 86.4 %copy-start.54 = (f32[8,8]{1,0:T(8,128)}, f32[8,8]{1,0:T(8,128)S(1)}, u32[]{:S(2)}) copy-start(f32[8,8]{1,0:T(8,128)S(1)} %convolution_add_fusion.19) | copy-start | bytes 772 | tf_op jit(solution)/shard_map/while
  236.1 44.7 %copy-start.44 = (bf16[128,24]{1,0:T(8,128)(2,1)}, bf16[128,24]{1,0:T(8,128)(2,1)S(1)}, u32[]{:S(2)}) copy-start(bf16[128,24]{1,0:T(8,128)(2,1)S(1)} %all_gather.211) | copy-start | bytes 18436 | tf_op jit(solution)/shard_map/while
  276.7 47.3 %copy-start.24 = (bf16[1,16,1536]{2,1,0:T(8,128)(2,1)}, bf16[1,16,1536]{2,1,0:T(8,128)(2,1)S(1)}, u32[]{:S(2)}) copy-start(bf16[1,16,1536]{2,1,0:T(8,128)(2,1)S(1)} %copy.152) | copy-start | bytes 147460 | tf_op jit(solution)/shard_map/while
  302.6 21.4 copy-start.32
  460.9 25.4 %copy-start.1 = (f32[256,1536]{1,0:T(8,128)}, f32[256,1536]{1,0:T(8,128)S(1)}, u32[]{:S(2)}) copy-start(f32[256,1536]{1,0:T(8,128)S(1)} %copy.149) | copy-start | bytes 4718596 | tf_op jit(solution)/shard_map/while
  463.3 19.1 copy-start.8
  487.6 122.2 %copy-start.5 = (bf16[256,1536]{1,0:T(8,128)(2,1)}, bf16[256,1536]{1,0:T(8,128)(2,1)S(1)}, u32[]{:S(2)}) copy-start(bf16[256,1536]{1,0:T(8,128)(2,1)S(1)} %multiply_convert_fusion.15) | copy-start | bytes 2359300 | tf_op jit(solution)/shard_map/while
  503.3 132.0 %copy-start.48 = (bf16[256,16]{0,1:T(8,128)(2,1)S(1)}, bf16[256,16]{0,1:T(8,128)(2,1)}, u32[]{:S(2)}) copy-start(bf16[256,16]{0,1:T(8,128)(2,1)} %convolution_convert_fusion.19) | copy-start | bytes 24580 | tf_op jit(solution)/shard_map/while
  628.4 15.9 copy-start.19
  703.1 17.7 copy-start.10
  727.0 147.1 %reduce-scatter.24.cloned.1.call-start = ((), (), s32[]{:S(2)}) async-start(), calls=%async_computation.25 | async-start | bytes 7864320 | tf_op jit(solution)/shard_map/while/body/eval_jaxpr/reduce_scatter | solution.py:294
  766.0 29.3 %copy-start.55 = (f32[8,8]{1,0:T(8,128)S(1)}, f32[8,8]{1,0:T(8,128)}, u32[]{:S(2)}) copy-start(f32[8,8]{1,0:T(8,128)} %copy-done.54) | copy-start | bytes 772 | tf_op jit(solution)/shard_map/while
  775.6 98.4 %copy-start.11 = (bf16[256,1536]{0,1:T(8,128)(2,1)S(1)}, bf16[256,1536]{0,1:T(8,128)(2,1)}, u32[]{:S(2)}) copy-start(bf16[256,1536]{0,1:T(8,128)(2,1)} %copy.156) | copy-start | bytes 2359300 | tf_op jit(solution)/shard_map/while
  903.4 36.4 %all-gather.16.cloned.1.call-start = ((), (), s32[]{:S(2)}) async-start(), calls=%async_computation.14 | async-start | bytes 3538944 | tf_op jit(solution)/shard_map/while/body/eval_jaxpr/all_gather | solution.py:127
  904.1 69.9 %all-gather.18.cloned.1.call-start = ((), (), s32[]{:S(2)}) async-start(), calls=%async_computation.15 | async-start | bytes 3538944 | tf_op jit(solution)/shard_map/while/body/eval_jaxpr/all_gather | solution.py:125
  904.7 169.9 %all-gather.20.cloned.1.call-start = ((), (), s32[]{:S(2)}) async-start(), calls=%async_computation.16 | async-start | bytes 21233664 | tf_op jit(solution)/shard_map/while/body/eval_jaxpr/all_gather | solution.py:120
  905.3 251.7 %all-gather.28.cloned.1.call-start = ((), (), s32[]{:S(2)}) async-start(), calls=%async_computation.20 | async-start | bytes 2359296 | tf_op jit(solution)/shard_map/while/body/eval_jaxpr/all_gather | solution.py:129
  905.9 286.0 %all-gather.32.cloned.1.call-start = ((), (), s32[]{:S(2)}) async-start(), calls=%async_computation.22 | async-start | bytes 14155776 | tf_op jit(solution)/shard_map/while/body/eval_jaxpr/all_gather | solution.py:124
  906.4 350.4 %all-gather.24.cloned.1.call-start = ((), (), s32[]{:S(2)}) async-start(), calls=%async_computation.18 | async-start | bytes 3932160 | tf_op jit(solution)/shard_map/while/body/eval_jaxpr/all_gather | solution.py:176
  911.1 193.0 %copy-start.50 = (f32[256]{0:T(256)}, f32[256]{0:T(256)S(1)}, u32[]{:S(2)}) copy-start(f32[256]{0:T(256)S(1)} %add_rsqrt_fusion.4) | copy-start | bytes 3076 | tf_op jit(solution)/shard_map/while
  942.5 37.8 %copy-start.13 = (bf16[1,64,1536]{2,1,0:T(8,128)(2,1)}, bf16[1,64,1536]{2,1,0:T(8,128)(2,1)S(1)}, u32[]{:S(2)}) copy-start(bf16[1,64,1536]{2,1,0:T(8,128)(2,1)S(1)} %copy.140) | copy-start | bytes 589828 | tf_op jit(solution)/shard_map/while
  976.6 182.1 %copy-start.45 = (bf16[256,80]{0,1:T(8,128)(2,1)}, bf16[256,80]{0,1:T(8,128)(2,1)S(1)}, u32[]{:S(2)}) copy-start(bf16[256,80]{0,1:T(8,128)(2,1)S(1)} %convolution_convert_fusion.16) | copy-start | bytes 122884 | tf_op jit(solution)/shard_map/while
  1088.8 231.9 %all-gather.22.cloned.1.call-start = ((), (), s32[]{:S(2)}) async-start(), calls=%async_computation.17 | async-start | bytes 3932160 | tf_op jit(solution)/shard_map/while/body/eval_jaxpr/all_gather | solution.py:177
  1089.6 270.7 %all-gather.26.cloned.1.call-start = ((), (), s32[]{:S(2)}) async-start(), calls=%async_computation.19 | async-start | bytes 5308416 | tf_op jit(solution)/shard_map/while/body/eval_jaxpr/all_gather | solution.py:122
  1090.2 397.5 %all-gather.30.cloned.1.call-start = ((), (), s32[]{:S(2)}) async-start(), calls=%async_computation.21 | async-start | bytes 28311552 | tf_op jit(solution)/shard_map/while/body/eval_jaxpr/all_gather | solution.py:123
  1090.9 422.4 %all-gather.34.cloned.1.call-start = ((), (), s32[]{:S(2)}) async-start(), calls=%async_computation.23 | async-start | bytes 1179648 | tf_op jit(solution)/shard_map/while/body/eval_jaxpr/all_gather | solution.py:126
  1091.6 564.0 %all-reduce.6.cloned.1.call-start = ((), (), s32[]{:S(2)}) async-start(), calls=%async_computation.24 | async-start | bytes 196608 | tf_op jit(solution)/shard_map/while/body/eval_jaxpr/psum | solution.py:304
  1093.8 86.3 %copy-start.54 = (f32[8,8]{1,0:T(8,128)}, f32[8,8]{1,0:T(8,128)S(1)}, u32[]{:S(2)}) copy-start(f32[8,8]{1,0:T(8,128)S(1)} %convolution_add_fusion.19) | copy-start | bytes 772 | tf_op jit(solution)/shard_map/while
  1114.0 44.7 %copy-start.44 = (bf16[128,24]{1,0:T(8,128)(2,1)}, bf16[128,24]{1,0:T(8,128)(2,1)S(1)}, u32[]{:S(2)}) copy-start(bf16[128,24]{1,0:T(8,128)(2,1)S(1)} %all_gather.211) | copy-start | bytes 18436 | tf_op jit(solution)/shard_map/while
  1154.7 47.4 %copy-start.24 = (bf16[1,16,1536]{2,1,0:T(8,128)(2,1)}, bf16[1,16,1536]{2,1,0:T(8,128)(2,1)S(1)}, u32[]{:S(2)}) copy-start(bf16[1,16,1536]{2,1,0:T(8,128)(2,1)S(1)} %copy.152) | copy-start | bytes 147460 | tf_op jit(solution)/shard_map/while
  1180.5 21.5 copy-start.32
  1260.1 13.6 copy-start.2
  1338.9 25.3 %copy-start.1 = (f32[256,1536]{1,0:T(8,128)}, f32[256,1536]{1,0:T(8,128)S(1)}, u32[]{:S(2)}) copy-start(f32[256,1536]{1,0:T(8,128)S(1)} %copy.149) | copy-start | bytes 4718596 | tf_op jit(solution)/shard_map/while
  1341.3 18.9 copy-start.8
  1365.5 122.2 %copy-start.5 = (bf16[256,1536]{1,0:T(8,128)(2,1)}, bf16[256,1536]{1,0:T(8,128)(2,1)S(1)}, u32[]{:S(2)}) copy-start(bf16[256,1536]{1,0:T(8,128)(2,1)S(1)} %multiply_convert_fusion.15) | copy-start | bytes 2359300 | tf_op jit(solution)/shard_map/while
  1381.1 132.1 %copy-start.48 = (bf16[256,16]{0,1:T(8,128)(2,1)S(1)}, bf16[256,16]{0,1:T(8,128)(2,1)}, u32[]{:S(2)}) copy-start(bf16[256,16]{0,1:T(8,128)(2,1)} %convolution_convert_fusion.19) | copy-start | bytes 24580 | tf_op jit(solution)/shard_map/while
  1506.2 16.1 copy-start.19
  1581.1 17.7 copy-start.10
  1605.0 147.1 %reduce-scatter.24.cloned.1.call-start = ((), (), s32[]{:S(2)}) async-start(), calls=%async_computation.25 | async-start | bytes 7864320 | tf_op jit(solution)/shard_map/while/body/eval_jaxpr/reduce_scatter | solution.py:294
  1644.0 29.3 %copy-start.55 = (f32[8,8]{1,0:T(8,128)S(1)}, f32[8,8]{1,0:T(8,128)}, u32[]{:S(2)}) copy-start(f32[8,8]{1,0:T(8,128)} %copy-done.54) | copy-start | bytes 772 | tf_op jit(solution)/shard_map/while
  1653.7 98.5 %copy-start.11 = (bf16[256,1536]{0,1:T(8,128)(2,1)S(1)}, bf16[256,1536]{0,1:T(8,128)(2,1)}, u32[]{:S(2)}) copy-start(bf16[256,1536]{0,1:T(8,128)(2,1)} %copy.156) | copy-start | bytes 2359300 | tf_op jit(solution)/shard_map/while
  1786.1 316.8 %all-reduce.4.cloned.1.call-start = ((), (), s32[]{:S(2)}) async-start(), calls=%async_computation.13 | async-start | bytes 17301504 | tf_op jit(solution)/shard_map/psum | solution.py:383
  1800.4 351.3 %reduce-scatter.22.cloned.1.call-start = ((), (), s32[]{:S(2)}) async-start(), calls=%async_computation.12 | async-start | bytes 884736
  2113.0 87.2 %reduce-scatter.20.cloned.1.call-start = ((), (), s32[]{:S(2)}) async-start(), calls=%async_computation.11 | async-start | bytes 4423680
  2124.0 18.4 copy-start.43
  2124.0 20.0 copy-start.37
  2124.0 113.3 %reduce-scatter.18.cloned.1.call-start = ((), (), s32[]{:S(2)}) async-start(), calls=%async_computation.10 | async-start | bytes 73728 | tf_op jit(solution)/shard_map/reduce_scatter | solution.py:72
  2142.3 140.1 %reduce-scatter.14.cloned.1.call-start = ((), (), s32[]{:S(2)}) async-start(), calls=%async_computation.8 | async-start | bytes 2359296 | tf_op jit(solution)/shard_map/reduce_scatter | solution.py:68
  2144.0 194.0 %reduce-scatter.16.cloned.1.call-start = ((), (), s32[]{:S(2)}) async-start(), calls=%async_computation.9 | async-start | bytes 4718592 | tf_op jit(solution)/shard_map/reduce_scatter | solution.py:71
  2146.6 256.7 %reduce-scatter.12.cloned.1.call-start = ((), (), s32[]{:S(2)}) async-start(), calls=%async_computation.7 | async-start | bytes 7077888 | tf_op jit(solution)/shard_map/reduce_scatter | solution.py:67
  (88 other events, 459.3 us)
Sparse Core Ops, SparseCore 0:
  26.3 35.0 all-gather.15
  63.4 32.3 all-gather.17
  97.8 98.7 all-gather.19
  198.4 28.5 all-gather.27
  229.0 84.7 all-gather.31
  315.3 63.4 all-gather.23
  380.5 62.1 all-gather.21
  444.7 37.5 all-gather.25
  484.4 125.3 all-gather.29
  611.6 23.5 all-gather.33
  727.1 34.2 all-reduce.5
  763.6 110.4 reduce-scatter.23
  906.8 32.8 all-gather.15
  941.6 32.3 all-gather.17
  975.9 98.7 all-gather.19
  1076.5 28.5 all-gather.27
  1107.0 84.7 all-gather.31
  1193.3 63.4 all-gather.23
  1258.5 62.1 all-gather.21
  1322.6 37.5 all-gather.25
  1362.3 125.3 all-gather.29
  1489.7 23.5 all-gather.33
  1605.1 34.3 all-reduce.5
  1641.6 110.4 reduce-scatter.23
Sparse Core Ops, SparseCore 1:
  1800.5 302.4 all-reduce.3
  2113.1 33.8 reduce-scatter.21
  2150.3 49.9 reduce-scatter.19
  2204.1 33.2 reduce-scatter.17
  2241.2 41.1 reduce-scatter.13
  2286.7 51.1 reduce-scatter.15
  2341.8 61.5 reduce-scatter.11
where the time goes:
time: 2420 us; the launch traced here: 2410 us
  waiting for transfers between devices  1460 us (60%)
  matrix products  416 us (17%)
  local copies, waits for them, and re-layouts  179 us (7%)
  other arithmetic  176 us (7%)
  blocking collectives  146 us (6%)
    psum x1, waiting for transfers between devices, body(): lax.psum(accum[0].astype(jnp.bfloat16), 'seq').astype(jnp.float32)  302 us
    all_gather x2, waiting for transfers between devices, one_tree(): lax.all_gather(owned[3], 'dp', axis=0, tiled=True)  213 us
    all_gather x2, waiting for transfers between devices, one_tree(): lax.all_gather(owned[0], 'dp', axis=0, tiled=True)  175 us
    reduce_scatter x2, waiting for transfers between devices, one_tree(): lax.psum_scatter(jnp.concatenate([key_part, value_part], axis=1).astype(j...  144 us
    dot_general x24, matrix products, linear_back(): lax.dot_general(left, right, (((1,), (1,)), ((), ())), preferred_element_...  116 us
    all_gather x2, waiting for transfers between devices, one_tree(): lax.all_gather(keys_mine, 'seq', axis=0, tiled=True)  107 us
    dot_general x24, matrix products, linear(): return jnp.dot(left, right, preferred_element_type=jnp.float32)  99.3 us
    all_gather x2, waiting for transfers between devices, one_tree(): lax.all_gather(values_mine, 'seq', axis=0, tiled=True)  69.6 us
  transfers between devices with their start and end apart: 31, of which 26 were waited for; matrix products, arithmetic and copies ran while one was open for 20% of the time, Pallas kernels for 0%

commit v1 on v0

v1 whole, which is shorter than its diff:
```python
import functools

import jax
import jax.numpy as jnp
from jax import lax
from jax.experimental import pallas as pl
from jax.experimental.pallas import tpu as pltpu
from jax.sharding import PartitionSpec as P

D = 1536
H = 24
HD = 64
FF = 4096
RANK = 16
ADAPTERS = 8
BLOCK = 128
TREE_LEN = 1024
EXTRA = 128
PAIRS = H // 2

ENTRIES = (2, 4, 6, 6)
FIRST = (0, 2, 6, 12)
TOTAL = 18

highest = lax.Precision.HIGHEST
epsilon = 1e-06
bf16 = jnp.bfloat16
f32 = jnp.float32


def linear(left, right):
    return jnp.dot(left, right, preferred_element_type=f32)


def linear_back(left, right):
    return lax.dot_general(left, right, (((1,), (1,)), ((), ())), preferred_element_type=f32)


def linear_grad(left, right):
    return lax.dot_general(left, right, (((0,), (0,)), ((), ())), preferred_element_type=f32)


def rms_scale(values):
    return lax.rsqrt(jnp.mean(values * values, axis=-1, keepdims=True) + epsilon)


def norm_back(values, gain, upstream):
    scale_rows = rms_scale(values)
    unit = values * scale_rows
    inner = upstream * gain
    return scale_rows * (inner - unit * jnp.mean(inner * unit, axis=-1, keepdims=True))


def attend_kernel(where_ref, q_ref, k_ref, v_ref, k2_ref, v2_ref, bias_ref, o_ref, p_ref, kbuf, vbuf):
    half = 4 * BLOCK
    kbuf[:half] = k_ref[...]
    kbuf[half:] = k2_ref[...]
    vbuf[:half] = v_ref[...]
    vbuf[half:] = v2_ref[...]
    lane = lax.broadcasted_iota(jnp.int32, (BLOCK, BLOCK), 1)
    row = lax.broadcasted_iota(jnp.int32, (BLOCK, BLOCK), 0)
    later = jnp.where(lane > row, f32(-1e30), f32(0.0))
    for place in range(4):
        count, first = ENTRIES[place], FIRST[place]
        queries = q_ref[place * BLOCK : (place + 1) * BLOCK, :]
        spots = [pl.multiple_of(where_ref[first + e] * BLOCK, BLOCK) for e in range(count)]
        keys = jnp.concatenate([kbuf[pl.ds(s, BLOCK), :] for s in spots], axis=0)
        values = jnp.concatenate([vbuf[pl.ds(s, BLOCK), :] for s in spots], axis=0)
        outs = []
        for a in range(2):
            mine = jnp.where((lane < HD) == (a == 0), queries, jnp.zeros_like(queries))
            scores = linear_back(mine, keys) * (HD ** (-0.5))
            scores = scores + bias_ref[a : a + 1, first * BLOCK : (first + count) * BLOCK]
            scores = jnp.concatenate(
                [scores[:, : (count - 1) * BLOCK], scores[:, (count - 1) * BLOCK :] + later], axis=1
            )
            peak = jnp.max(scores, axis=1, keepdims=True)
            expo = jnp.exp(scores - peak)
            total = jnp.sum(expo, axis=1, keepdims=True)
            probs = (expo * (1.0 / total)).astype(bf16)
            p_ref[a, :, first * BLOCK : (first + count) * BLOCK] = probs
            outs.append(linear(probs, values))
        o_ref[place * BLOCK : (place + 1) * BLOCK, :] = jnp.where(lane < HD, outs[0], outs[1])


def attend(where, queries, keys, values, keys2, values2, bias):
    rows = pl.BlockSpec((4 * BLOCK, 2 * HD), lambda g, w: (0, g))
    return pl.pallas_call(
        attend_kernel,
        out_shape=(
            jax.ShapeDtypeStruct((4 * BLOCK, D), f32),
            jax.ShapeDtypeStruct((H, BLOCK, TOTAL * BLOCK), bf16),
        ),
        grid_spec=pltpu.PrefetchScalarGridSpec(
            num_scalar_prefetch=1,
            grid=(PAIRS,),
            in_specs=[rows] * 5 + [pl.BlockSpec((None, 2, TOTAL * BLOCK), lambda g, w: (g, 0, 0))],
            out_specs=(rows, pl.BlockSpec((2, BLOCK, TOTAL * BLOCK), lambda g, w: (g, 0, 0))),
            scratch_shapes=[pltpu.VMEM((8 * BLOCK, 2 * HD), bf16)] * 2,
        ),
        cost_estimate=pl.CostEstimate(flops=8_000_000_000, bytes_accessed=25_000_000, transcendentals=7_000_000),
        name="attend",
    )(where, queries, keys, values, keys2, values2, bias)


def attend_back_kernel(
    where_ref, q_ref, k_ref, v_ref, k2_ref, v2_ref, g_ref, o_ref, p_ref,
    dq_ref, dk_ref, dv_ref, qsum_ref, ksum_ref, kbuf, vbuf, dkbuf, dvbuf,
):
    half = 4 * BLOCK
    pair = pl.program_id(0)
    kbuf[:half] = k_ref[...]
    kbuf[half:] = k2_ref[...]
    vbuf[:half] = v_ref[...]
    vbuf[half:] = v2_ref[...]
    dkbuf[...] = jnp.zeros_like(dkbuf)
    dvbuf[...] = jnp.zeros_like(dvbuf)
    ksum_ref[...] = jnp.zeros_like(ksum_ref)

    @pl.when(pair == 0)
    def _():
        qsum_ref[...] = jnp.zeros_like(qsum_ref)

    lane = lax.broadcasted_iota(jnp.int32, (BLOCK, BLOCK), 1)
    scale = HD ** (-0.5)
    for place in range(4):
        count, first = ENTRIES[place], FIRST[place]
        span = slice(place * BLOCK, (place + 1) * BLOCK)
        queries = q_ref[span, :]
        grads = g_ref[span, :]
        product = grads.astype(f32) * o_ref[span, :]
        spots = [pl.multiple_of(where_ref[first + e] * BLOCK, BLOCK) for e in range(count)]
        keys = jnp.concatenate([kbuf[pl.ds(s, BLOCK), :] for s in spots], axis=0)
        values = jnp.concatenate([vbuf[pl.ds(s, BLOCK), :] for s in spots], axis=0)
        dqs, dks, dvs = [], [], []
        row_sums = qsum_ref[span, :]
        for a in range(2):
            own = (lane < HD) == (a == 0)
            dot_row = jnp.sum(jnp.where(own, product, 0.0), axis=1, keepdims=True)
            mine = jnp.where(own, grads, jnp.zeros_like(grads))
            probs = p_ref[a, :, first * BLOCK : (first + count) * BLOCK]
            prob_grad = linear_back(mine, values)
            score_grad = (probs.astype(f32) * (prob_grad - dot_row)).astype(bf16)
            wide = score_grad.astype(f32)
            col = jnp.sum(wide, axis=0, keepdims=True)
            for e in range(count):
                ksum_ref[where_ref[first + e], a : a + 1, :] += col[:, e * BLOCK : (e + 1) * BLOCK]
            row_sums = row_sums + jnp.where(lane == 2 * pair + a, jnp.sum(wide, axis=1, keepdims=True), 0.0)
            dqs.append(linear(score_grad, keys))
            dks.append(linear_grad(score_grad, queries))
            dvs.append(linear_grad(probs, grads))
        qsum_ref[span, :] = row_sums
        dq_ref[span, :] = (jnp.where(lane < HD, dqs[0], dqs[1]) * scale).astype(bf16)
        for e in range(count):
            part = slice(e * BLOCK, (e + 1) * BLOCK)
            dkbuf[pl.ds(spots[e], BLOCK), :] += jnp.where(lane < HD, dks[0][part], dks[1][part])
            dvbuf[pl.ds(spots[e], BLOCK), :] += jnp.where(lane < HD, dvs[0][part], dvs[1][part])
    dk_ref[...] = (dkbuf[...] * scale).astype(bf16)
    dv_ref[...] = dvbuf[...].astype(bf16)


def attend_back(where, queries, keys, values, keys2, values2, grads, attended, probs):
    rows = pl.BlockSpec((4 * BLOCK, 2 * HD), lambda g, w: (0, g))
    full = pl.BlockSpec((8 * BLOCK, 2 * HD), lambda g, w: (0, g))
    return pl.pallas_call(
        attend_back_kernel,
        out_shape=(
            jax.ShapeDtypeStruct((4 * BLOCK, D), bf16),
            jax.ShapeDtypeStruct((8 * BLOCK, D), bf16),
            jax.ShapeDtypeStruct((8 * BLOCK, D), bf16),
            jax.ShapeDtypeStruct((4 * BLOCK, BLOCK), f32),
            jax.ShapeDtypeStruct((PAIRS, 8, 2, BLOCK), f32),
        ),
        grid_spec=pltpu.PrefetchScalarGridSpec(
            num_scalar_prefetch=1,
            grid=(PAIRS,),
            in_specs=[rows] * 7 + [pl.BlockSpec((2, BLOCK, TOTAL * BLOCK), lambda g, w: (g, 0, 0))],
            out_specs=(
                rows,
                full,
                full,
                pl.BlockSpec((4 * BLOCK, BLOCK), lambda g, w: (0, 0)),
                pl.BlockSpec((None, 8, 2, BLOCK), lambda g, w: (g, 0, 0, 0)),
            ),
            scratch_shapes=[pltpu.VMEM((8 * BLOCK, 2 * HD), bf16)] * 2
            + [pltpu.VMEM((8 * BLOCK, 2 * HD), f32)] * 2,
        ),
        cost_estimate=pl.CostEstimate(flops=16_000_000_000, bytes_accessed=35_000_000, transcendentals=0),
        name="attend_back",
    )(where, queries, keys, values, keys2, values2, grads, attended, probs)


def forward_kernel(x_ref, low_ref, w_ref, e_ref, b_ref, o_ref):
    out = linear(x_ref[...], w_ref[...]) + linear(low_ref[...], e_ref[...])
    o_ref[...] = (out + b_ref[...]).astype(o_ref.dtype)


def forward_mm(x, low, weight, extra, bias, first, count, width, dtype):
    rows, depth = x.shape
    whole = lambda v: pl.BlockSpec(v.shape, lambda j: (0,) * v.ndim)
    cols = lambda height: pl.BlockSpec((height, width), lambda j: (0, first + j))
    return pl.pallas_call(
        forward_kernel,
        out_shape=jax.ShapeDtypeStruct((rows, count * width), dtype),
        grid=(count,),
        in_specs=[whole(x), whole(low), cols(depth), cols(EXTRA), cols(1)],
        out_specs=pl.BlockSpec((rows, width), lambda j: (0, j)),
        cost_estimate=pl.CostEstimate(
            flops=2 * rows * (depth + EXTRA) * count * width,
            bytes_accessed=2 * depth * count * width + 2 * rows * depth,
            transcendentals=0,
        ),
        name="forward_mm",
    )(x, low, weight, extra, bias)


def backward_kernel(g_ref, w_ref, e_ref, acc_ref, acclow_ref, o_ref, low_ref):
    @pl.when(pl.program_id(0) == 0)
    def _():
        o_ref[...] = acc_ref[...]
        low_ref[...] = acclow_ref[...]

    grads = g_ref[...]
    o_ref[...] += linear_back(grads, w_ref[...])
    low_ref[...] += linear_back(grads, e_ref[...])


def backward_mm(g, weight, extra, first, count, width, acc, acc_low):
    rows = g.shape[0]
    depth = weight.shape[0]
    whole = lambda v: pl.BlockSpec(v.shape, lambda j: (0,) * v.ndim)
    cols = lambda height: pl.BlockSpec((height, width), lambda j: (0, first + j))
    return pl.pallas_call(
        backward_kernel,
        out_shape=(jax.ShapeDtypeStruct((rows, depth), f32), jax.ShapeDtypeStruct((rows, EXTRA), f32)),
        grid=(count,),
        in_specs=[
            pl.BlockSpec((rows, width), lambda j: (0, j)), cols(depth), cols(EXTRA), whole(acc), whole(acc_low)
        ],
        out_specs=(whole(acc), whole(acc_low)),
        cost_estimate=pl.CostEstimate(
            flops=2 * rows * (depth + EXTRA) * count * width,
            bytes_accessed=2 * depth * count * width + 8 * rows * depth,
            transcendentals=0,
        ),
        name="backward_mm",
    )(g, weight, extra, acc, acc_low)


def swiglu_kernel(
    x_ref, lowg_ref, lowu_ref, dy_ref, hlg_ref, g_ref, u_ref, bg_ref, bu_ref, dn_ref, ah_ref,
    second_ref, down_ref, slg_ref, slu_ref, hl_ref, pack_ref,
):
    @pl.when(pl.program_id(0) == 0)
    def _():
        for ref in (second_ref, down_ref, slg_ref, slu_ref, hl_ref):
            ref[...] = jnp.zeros_like(ref)

    gate = linear(x_ref[...], g_ref[...]) + linear(lowg_ref[...], bg_ref[...])
    up = linear(x_ref[...], u_ref[...]) + linear(lowu_ref[...], bu_ref[...])
    back = linear_back(dy_ref[...], dn_ref[...]) + linear(hlg_ref[...], ah_ref[...])
    sig = jax.nn.sigmoid(gate)
    silu = gate * sig
    activated = (silu * up).astype(bf16)
    gate_grad = (back * up * (sig * (1.0 + gate * (1.0 - sig)))).astype(bf16)
    up_grad = (back * silu).astype(bf16)
    down_ref[...] += linear(activated, dn_ref[...])
    hl_ref[...] += linear_back(activated, ah_ref[...])
    second_ref[...] += linear_back(gate_grad, g_ref[...]) + linear_back(up_grad, u_ref[...])
    slg_ref[...] += linear_back(gate_grad, bg_ref[...])
    slu_ref[...] += linear_back(up_grad, bu_ref[...])
    pack_ref[:RANK] = linear_grad(hlg_ref[...], activated).astype(bf16)
    pack_ref[RANK : 2 * RANK] = linear_grad(lowg_ref[...], gate_grad).astype(bf16)
    pack_ref[2 * RANK :] = linear_grad(lowu_ref[...], up_grad).astype(bf16)


def swiglu(x, lowg, lowu, dy, hlg, weight, bg, bu, down, ah):
    rows = x.shape[0]
    width = 512
    steps = FF // width
    whole = lambda v: pl.BlockSpec(v.shape, lambda j: (0,) * v.ndim)
    low = pl.BlockSpec((RANK, width), lambda j: (0, j))
    state = [jax.ShapeDtypeStruct((rows, n), f32) for n in (D, D, RANK, RANK, RANK)]
    return pl.pallas_call(
        swiglu_kernel,
        out_shape=tuple(state) + (jax.ShapeDtypeStruct((3 * RANK, FF), bf16),),
        grid=(steps,),
        in_specs=[whole(v) for v in (x, lowg, lowu, dy, hlg)]
        + [
            pl.BlockSpec((D, width), lambda j: (0, j)),
            pl.BlockSpec((D, width), lambda j: (0, steps + j)),
            low,
            low,
            pl.BlockSpec((width, D), lambda j: (j, 0)),
            low,
        ],
        out_specs=tuple(whole(v) for v in state) + (pl.BlockSpec((3 * RANK, width), lambda j: (0, j)),),
        cost_estimate=pl.CostEstimate(
            flops=12 * rows * D * FF, bytes_accessed=6 * D * FF + 24 * rows * D, transcendentals=rows * FF
        ),
        name="swiglu",
    )(x, lowg, lowu, dy, hlg, weight, weight, bg, bu, down, ah)


MESH = pl.DeviceIdType.MESH


def facts_kernel(facts_ref, forget_ref, facts_all, forget_out, send, recv):
    me, z = lax.axis_index("dp"), lax.axis_index("seq")
    barrier = pltpu.get_barrier_semaphore()
    for m in range(1, 8):
        pl.semaphore_signal(barrier, inc=1, device_id=(me ^ m, z), device_id_type=MESH)
    pl.semaphore_wait(barrier, 7)
    copies = []
    for m in range(1, 8):
        for kind, (src, dst) in enumerate(((facts_ref, facts_all), (forget_ref, forget_out))):
            copies.append(
                pltpu.make_async_remote_copy(
                    src_ref=src,
                    dst_ref=dst.at[me],
                    send_sem=send.at[kind, m],
                    recv_sem=recv.at[kind, m],
                    device_id=(me ^ m, z),
                    device_id_type=MESH,
                )
            )
            copies[-1].start()
    local = [
        pltpu.make_async_copy(facts_ref, facts_all.at[me], send.at[0, 0]),
        pltpu.make_async_copy(forget_ref, forget_out.at[me], send.at[1, 0]),
    ]
    for copy in local:
        copy.start()
    for copy in copies + local:
        copy.wait()


def share_facts(facts, forget):
    vmem = pl.BlockSpec(memory_space=pltpu.VMEM)
    return pl.pallas_call(
        facts_kernel,
        out_shape=(
            jax.ShapeDtypeStruct((8,) + facts.shape, facts.dtype),
            jax.ShapeDtypeStruct((8,) + forget.shape, forget.dtype),
        ),
        in_specs=[vmem, vmem],
        out_specs=(vmem, vmem),
        scratch_shapes=[pltpu.SemaphoreType.DMA((2, 8)), pltpu.SemaphoreType.DMA((2, 8))],
        compiler_params=pltpu.CompilerParams(collective_id=0, has_side_effects=True),
        name="share_facts",
    )(facts, forget)


def column_chunks(widths):
    chunks = []
    for index, (total, width) in enumerate(widths):
        for first in range(0, total, width):
            chunks.append((index, first, width))
    return chunks


def shared_rows(count):
    return count // 4


def gather_kernel(chunks, *refs):
    (tok, cot, inner, model, ffp, mix, fg, out, dn, sw) = refs[:10]
    (x_o, dy_o, inner_o, model_o, ff_o, mix_o, fg_o, out_o, dn_o, sw_o) = refs[10:20]
    send, recv, own_sem, small_send, small_recv, row_send, row_recv = refs[20:]
    me, z = lax.axis_index("dp"), lax.axis_index("seq")
    core, odd = me & 1, z & 1
    first_to = me ^ (2 + 2 * core)
    second_to = me ^ (4 - 2 * core)

    barrier = pltpu.get_barrier_semaphore()
    peers = [(me ^ m, z) for m in range(1, 8)] + [(me ^ m, z ^ k) for m in (0, 1) for k in (1, 2, 3)]
    for peer in peers:
        pl.semaphore_signal(barrier, inc=1, device_id=peer, device_id_type=MESH)
    pl.semaphore_wait(barrier, len(peers))

    sources = (mix, fg, out, dn, sw)
    targets = (mix_o, fg_o, out_o, dn_o, sw_o)
    done = []

    def remote(src, dst, s, r, to):
        copy = pltpu.make_async_remote_copy(
            src_ref=src, dst_ref=dst, send_sem=s, recv_sem=r, device_id=to, device_id_type=MESH
        )
        copy.start()
        done.append(copy)
        return copy

    tree_core = z >> 1
    rows = []
    for kind, (src, dst) in enumerate(((tok, x_o), (cot, dy_o))):
        for j in range(2):
            for b in range(2):
                to = ((me & ~1) | (b ^ odd), 2 * core + j)
                self_copy = (to[0] == me) & (to[1] == z)
                spot = dst.at[pl.ds(z * BLOCK, BLOCK)]
                far = pltpu.make_async_remote_copy(
                    src_ref=src.at[j, b],
                    dst_ref=spot,
                    send_sem=row_send.at[kind, 2 * j + b],
                    recv_sem=row_recv.at[kind, z],
                    device_id=to,
                    device_id_type=MESH,
                )
                near = pltpu.make_async_copy(src.at[j, b], spot, row_send.at[kind, 2 * j + b])

                @pl.when(self_copy)
                def _(near=near):
                    near.start()

                @pl.when(jnp.logical_not(self_copy))
                def _(far=far):
                    far.start()

                rows.append((self_copy, near, far))

    small = []
    for kind, (src, dst) in enumerate(((inner, inner_o), (model, model_o), (ffp, ff_o))):
        for m in range(1, 8):
            remote(src.at[me ^ m], dst.at[me], small_send.at[kind, m], small_recv.at[kind, m], (me ^ m, z))
        copy = pltpu.make_async_copy(src.at[me], dst.at[me], small_send.at[kind, 0])
        copy.start()
        small.append(copy)

    own = []
    for i, (index, first, width) in enumerate(chunks):
        src, dst = sources[index], targets[index]
        count = src.shape[0]
        copy = pltpu.make_async_copy(
            src.at[:, pl.ds(first, width)],
            dst.at[pl.ds(pl.multiple_of(me * count, count), count), pl.ds(first, width)],
            own_sem.at[i],
        )
        copy.start()
        own.append(copy)

    partner = (me ^ 1, z)
    above = (me, z ^ 1)
    state = {}

    def piece(i, owner, start, length):
        index, first, width = chunks[i]
        count = sources[index].shape[0]
        return targets[index].at[
            pl.ds(pl.multiple_of(owner * count + start, 16), length), pl.ds(first, width)
        ]

    def go(i, slot, src, dst, to):
        state[i, slot] = remote(src, dst, send.at[i, slot], recv.at[i, slot], to)

    def shape_of(i):
        index, first, width = chunks[i]
        count = sources[index].shape[0]
        shared = shared_rows(count)
        return count, shared, shared * odd, count - shared

    def pass_on(i, slot, owner, start, length, target):
        ref = piece(i, owner, start, length)
        go(i, slot, ref, ref, target)

    total = len(chunks)
    for i in range(total + 3):
        if i < total:
            index, first, width = chunks[i]
            count, shared, low, length = shape_of(i)
            src = sources[index].at[pl.ds(pl.multiple_of(low, 16), length), pl.ds(first, width)]
            go(i, 0, src, piece(i, me, low, length), (first_to, z))
            go(i, 1, src, piece(i, me, low, length), (second_to, z))
            go(i, 6, sources[index].at[:, pl.ds(first, width)], piece(i, me, 0, count), partner)
        k = i - 1
        if 0 <= k < total:
            count, shared, low, length = shape_of(k)
            state[k, 0].wait_recv()
            pass_on(k, 2, first_to, low, length, (second_to, z))
            pass_on(k, 7, first_to, low, length, partner)
            pass_on(k, 3, first_to, odd * (count - shared), shared, above)
            state[k, 1].wait_recv()
            pass_on(k, 8, second_to, low, length, partner)
            pass_on(k, 4, second_to, odd * (count - shared), shared, above)
        k = i - 2
        if 0 <= k < total:
            count, shared, low, length = shape_of(k)
            state[k, 2].wait_recv()
            pass_on(k, 9, me ^ 6, low, length, partner)
            pass_on(k, 5, me ^ 6, odd * (count - shared), shared, above)
        k = i - 3
        if 0 <= k < total:
            count, shared, low, length = shape_of(k)
            for n, owner in enumerate((first_to, second_to, me ^ 6)):
                state[k, 3 + n].wait_recv()
                pass_on(k, 10 + n, owner, (1 - odd) * (count - shared), shared, partner)
    for i in range(total):
        for slot in range(6, 13):
            state[i, slot].wait_recv()
    for copy in done:
        copy.wait_send()
    for kind in range(3):
        for m in range(7):
            done[kind * 7 + m].wait_recv()
    for copy in own + small:
        copy.wait()
    for self_copy, near, far in rows:
        @pl.when(self_copy)
        def _(near=near):
            near.wait()

        @pl.when(jnp.logical_not(self_copy))
        def _(far=far):
            far.wait_send()

    for kind, dst in enumerate((x_o, dy_o)):
        for p in range(4):
            from_me = (p == z) & (core == tree_core)
            arrived = pltpu.make_async_remote_copy(
                src_ref=tok.at[0, 0],
                dst_ref=dst.at[pl.ds(p * BLOCK, BLOCK)],
                send_sem=row_send.at[kind, p],
                recv_sem=row_recv.at[kind, p],
                device_id=(me ^ 1, z),
                device_id_type=MESH,
            )

            @pl.when(jnp.logical_not(from_me))
            def _(arrived=arrived):
                arrived.wait_recv()


def gather_all(tokens, cotangent, inner, model, ffp, mix, fg, out, dn, sw):
    chunks = column_chunks(((4 * D, 1024), (EXTRA, EXTRA), (D, D), (D, 512), (2 * FF, 1024)))
    vmem = pl.BlockSpec(memory_space=pltpu.VMEM)
    hbm = pl.BlockSpec(memory_space=pl.ANY)
    args = (tokens.reshape(2, 2, BLOCK, D), cotangent.reshape(2, 2, BLOCK, D), inner, model, ffp, mix, fg, out, dn, sw)
    n = len(chunks)
    shapes = [jax.ShapeDtypeStruct((4 * BLOCK, D), bf16)] * 2
    shapes += [jax.ShapeDtypeStruct(v.shape, bf16) for v in (inner, model, ffp)]
    shapes += [jax.ShapeDtypeStruct((8 * v.shape[0], v.shape[1]), bf16) for v in (mix, fg, out, dn, sw)]
    dma = pltpu.SemaphoreType.DMA
    return pl.pallas_call(
        functools.partial(gather_kernel, chunks),
        out_shape=tuple(shapes),
        in_specs=[vmem] * len(args),
        out_specs=(hbm,) * len(shapes),
        scratch_shapes=[dma((n, 13)), dma((n, 13)), dma((n,)), dma((3, 8)), dma((3, 8)), dma((2, 4)), dma((2, 4))],
        compiler_params=pltpu.CompilerParams(collective_id=1, has_side_effects=True),
        name="gather_all",
    )(*args)


def body(
    devices,
    tokens,
    cotangent,
    parents,
    adapter_ids,
    attention_gain,
    mixer_weight,
    forget_weight,
    forget_bias,
    output_weight,
    feedforward_gain,
    swiglu_weight,
    down_weight,
    adapter_inner,
    adapter_hidden,
    adapter_model,
    adapter_project,
    adapter_swiglu,
    adapter_forget,
):
    dp, seq = devices
    paired = dp == 8
    me = lax.axis_index("dp")
    z = lax.axis_index("seq")
    core = me & 1
    tree_core, tree_slot = z >> 1, z & 1
    rows = 4 * BLOCK
    wide = D // dp
    tall = FF // dp

    def swap(value, bit):
        return lax.ppermute(value, "dp", [(i, i ^ bit) for i in range(dp)])

    def routes(step):
        high, low = step >> 1, step & 1
        pairs = []
        for d in range(dp):
            for s in range(seq):
                slot = high ^ (s >> 1)
                target = ((d & ~1) | (low ^ (s & 1))) * seq + 2 * (d & 1) + slot
                pairs.append((d * seq + s, target))
        return pairs

    def spread(value):
        cut = value.reshape(2, 2, BLOCK, D)
        got = []
        for step in range(4):
            piece = lax.dynamic_index_in_dim(cut[:, step & 1], (step >> 1) ^ (z >> 1), 0, keepdims=False)
            got.append(lax.ppermute(piece, ("dp", "seq"), routes(step)))
        stacked = jnp.stack(got)
        order = [lax.dynamic_index_in_dim(stacked, p ^ (2 * tree_slot + core), 0, keepdims=False) for p in range(4)]
        return jnp.concatenate(order, axis=0)

    def collect(value):
        cut = value.reshape(4, BLOCK, D)
        got = []
        for step in range(4):
            piece = lax.dynamic_index_in_dim(cut, step ^ (2 * tree_slot + core), 0, keepdims=False)
            got.append(lax.ppermute(piece, ("dp", "seq"), [(b, a) for a, b in routes(step)]))
        stacked = jnp.stack(got).reshape(2, 2 * BLOCK, D)
        order = [lax.dynamic_index_in_dim(stacked, t ^ (z >> 1), 0, keepdims=False) for t in range(2)]
        return jnp.stack(order)

    def gather_small(value):
        bit = 1
        while bit < dp:
            other = swap(value, bit)
            flag = (me & bit) != 0
            value = jnp.concatenate([jnp.where(flag, other, value), jnp.where(flag, value, other)], axis=0)
            bit *= 2
        return value

    facts = jnp.concatenate([parents, adapter_ids[:, None]], axis=1)
    if paired:
        facts, forget_all = share_facts(jnp.pad(facts, ((0, 6), (0, 128 - 9))), jnp.pad(adapter_forget, ((0, 0), (0, EXTRA - H))))
        facts = facts[:, :2, :9].reshape(2 * dp, 9)
        forget_all = forget_all[:, :, :H].reshape(ADAPTERS * RANK, H)
    else:
        facts = gather_small(facts)
        forget_all = gather_small(adapter_forget)
    all_ids = facts[:, 8]
    tree = 2 * ((me & ~1) | tree_core) + tree_slot
    parent_row = lax.dynamic_index_in_dim(facts, tree, 0, keepdims=False)[:8]
    which = lax.dynamic_index_in_dim(all_ids, tree, 0, keepdims=False)

    def to_trees(value):
        sent = []
        for d in range(dp):
            owner_tree = 2 * ((d & ~1) | tree_core) + tree_slot
            chosen = lax.dynamic_index_in_dim(all_ids, owner_tree, 0, keepdims=False)
            sent.append(lax.dynamic_index_in_dim(value, chosen, 0, keepdims=False))
        return jnp.stack(sent)

    got_inner = to_trees(adapter_inner)
    got_model = to_trees(jnp.concatenate([adapter_model, adapter_project], axis=1))
    got_ff = to_trees(jnp.concatenate([jnp.swapaxes(adapter_hidden, 1, 2), adapter_swiglu], axis=1))
    padded_forget = jnp.pad(forget_weight, ((0, 0), (0, EXTRA - H)))
    shards = (mixer_weight, padded_forget, output_weight, down_weight, swiglu_weight)
    if paired:
        gathered = gather_all(tokens, cotangent, got_inner, got_model, got_ff, *shards)
        x, dy, got_inner, got_model, got_ff = gathered[:5]
        w_mix, w_forget, w_out, w_down, w_swiglu = gathered[5:]
    else:
        x, dy = spread(tokens), spread(cotangent)
        got_inner, got_model, got_ff = (
            lax.all_to_all(v, "dp", 0, 0, tiled=True) for v in (got_inner, got_model, got_ff)
        )
        w_mix, w_forget, w_out, w_down, w_swiglu = (lax.all_gather(v, "dp", axis=0, tiled=True) for v in shards)
    inner_sel = got_inner.reshape(D, 8 * RANK)
    model_sel = jnp.swapaxes(got_model, 0, 1).reshape(6 * RANK, D)
    ff_sel = jnp.swapaxes(got_ff, 0, 1).reshape(3 * RANK, FF)
    forget_sel = lax.dynamic_slice_in_dim(forget_all, which * RANK, RANK, 0)

    zero = functools.partial(jnp.zeros, dtype=bf16)
    b_q, b_k, b_v, b_g, b_down, b_project = (model_sel[i * RANK : (i + 1) * RANK] for i in range(6))
    none = zero((RANK, D))
    line = lambda *blocks: jnp.concatenate(blocks, axis=1)
    extra_mix = jnp.concatenate(
        [
            line(b_q, none, none, none),
            line(none, b_k, none, none),
            line(none, none, b_v, none),
            line(none, none, none, b_g),
            zero((EXTRA - 4 * RANK, 4 * D)),
        ],
        axis=0,
    )
    a_in = inner_sel[:, : 5 * RANK]
    a_project = inner_sel[:, 5 * RANK : 6 * RANK]
    a_swiglu = inner_sel[:, 6 * RANK :]
    inputs = x.astype(f32)
    first_norm = (inputs * rms_scale(inputs) * attention_gain).astype(bf16)
    inner_low = linear(first_norm, a_in).astype(bf16)
    group = lambda v, i: v[:, i * RANK : (i + 1) * RANK]
    pad_low = lambda v: jnp.pad(v, ((0, 0), (0, EXTRA - v.shape[1])))
    low_pad = pad_low(inner_low)
    zero_row = jnp.zeros((1, 4 * D), f32)
    mix = lambda first, count, dtype: forward_mm(first_norm, low_pad, w_mix, extra_mix, zero_row, first, count, 512, dtype)
    forget_logit = (
        linear(first_norm, w_forget)[:, :H] + linear(group(inner_low, 4), forget_sel) + forget_bias
    ).astype(bf16)
    kv = mix(3, 6, bf16)
    kv2 = swap(kv, 1)
    forget2 = swap(forget_logit, 1)
    keys, values = kv[:, :D], kv[:, D:]
    keys2, values2 = kv2[:, :D], kv2[:, D:]
    queries = mix(0, 3, bf16)
    gate_logit = mix(9, 3, f32)

    table = jnp.array([[0, 3, 4, 7], [1, 2, 5, 6]], dtype=jnp.int32)
    mine_ids = lax.dynamic_index_in_dim(table, core, 0, keepdims=False)
    ids = jnp.concatenate([mine_ids, lax.dynamic_index_in_dim(table, 1 - core, 0, keepdims=False)])
    block = jnp.arange(8, dtype=jnp.int32)
    trunk = (block[None, :] < 4) & (block[None, :] <= block[:, None])
    reach = trunk | (block[:, None] == block[None, :]) | (
        (block[:, None] >= 4) & (block[None, :] >= 4) & (parent_row[:, None] == block[None, :])
    )
    strict = (reach & (block[:, None] != block[None, :])).astype(f32)
    pick = (ids[:, None] == block[None, :]).astype(f32)
    strict_local = jnp.dot(jnp.dot(pick, strict, precision=highest), pick.T, precision=highest)
    spot_of = jnp.array([0, 4, 5, 1, 2, 6, 7, 3], dtype=jnp.int32) ^ (4 * core)
    first_entries = jnp.where(
        core == 0,
        jnp.array([-1, 0, 0, 1, 2, 3], dtype=jnp.int32),
        jnp.array([0, 1, 0, 1, -1, 2], dtype=jnp.int32),
    )
    tails = []
    for place in (2, 3):
        own = mine_ids[place]
        up = parent_row[own]
        up = jnp.where(up >= 4, up, -1)
        tails.append(jnp.concatenate([jnp.arange(4, dtype=jnp.int32), up[None], own[None]]))
    entries = jnp.concatenate([first_entries] + tails)
    valid = entries >= 0
    where = jnp.where(valid, spot_of[jnp.maximum(entries, 0)], 0).astype(jnp.int32)

    logits_all = jnp.concatenate([forget_logit, forget2], axis=0).astype(f32)
    log_forget = jax.nn.log_sigmoid(logits_all).T.reshape(H, 8, BLOCK)
    upper = (jnp.arange(BLOCK)[:, None] <= jnp.arange(BLOCK)[None, :]).astype(f32)
    within = jnp.dot(log_forget, upper, precision=highest)
    offsets = jnp.dot(within[:, :, BLOCK - 1], strict_local.T, precision=highest)
    path_sum = within + offsets[:, :, None]
    bias = jnp.where(valid[None, :, None], -path_sum[:, where], -1e30)
    bias = bias.reshape(PAIRS, 2, TOTAL * BLOCK)

    attended, probs = attend(where, queries, keys, values, keys2, values2, bias)
    gate_open = jax.nn.sigmoid(gate_logit)
    gated = (attended * gate_open).astype(bf16)
    project_low = linear(gated, a_project).astype(bf16)
    extra_out = jnp.pad(b_project, ((0, EXTRA - RANK), (0, 0)))
    out = forward_mm(gated, pad_low(project_low), w_out, extra_out, zero_row, 0, 3, 512, f32)
    middle = inputs + out
    second_norm = (middle * rms_scale(middle) * feedforward_gain).astype(bf16)
    swiglu_low = linear(second_norm, a_swiglu).astype(bf16)
    lowg, lowu = swiglu_low[:, :RANK], swiglu_low[:, RANK:]

    hidden_low_grad = linear_back(dy, b_down).astype(bf16)
    second_out, down_out, slg, slu, hidden_low, ff_pack = swiglu(
        second_norm, lowg, lowu, dy, hidden_low_grad, w_swiglu,
        ff_sel[RANK : 2 * RANK], ff_sel[2 * RANK :], w_down, ff_sel[:RANK],
    )
    hidden_low = hidden_low.astype(bf16)
    result = (middle + down_out + linear(hidden_low, b_down)).astype(bf16)
    outputs = collect(result)

    swiglu_low_grad = jnp.concatenate([slg, slu], axis=1).astype(bf16)
    second_grad = second_out + linear_back(swiglu_low_grad, a_swiglu)
    middle_grad = dy.astype(f32) + norm_back(middle, feedforward_gain, second_grad)
    branch_grad = middle_grad.astype(bf16)
    project_low_grad = linear_back(branch_grad, b_project).astype(bf16)
    none_low = jnp.zeros((rows, EXTRA), f32)
    gated_grad = backward_mm(
        branch_grad, w_out, zero((EXTRA, D)), 0, 3, 512, linear_back(project_low_grad, a_project), none_low
    )[0]
    attended_grad = (gated_grad * gate_open).astype(bf16)
    gate_logit_grad = (gated_grad * attended * gate_open * (1.0 - gate_open)).astype(bf16)

    first_out, first_low = backward_mm(
        gate_logit_grad, w_mix, extra_mix, 9, 3, 512, jnp.zeros((rows, D), f32), none_low
    )
    dq, dk_all, dv_all, query_sum, key_sum = attend_back(
        where, queries, keys, values, keys2, values2, attended_grad, attended, probs
    )
    theirs = jnp.concatenate([dk_all[rows:], dv_all[rows:]], axis=1)
    back = swap(theirs, 1)
    key_sum = jnp.transpose(key_sum, (0, 2, 1, 3)).reshape(H, 8, BLOCK)
    query_part = query_sum[:, :H].T.reshape(H, 4, BLOCK)
    decay = jnp.concatenate([query_part - key_sum[:, :4], -key_sum[:, 4:]], axis=1)
    other = swap(decay, 1)
    decay = decay + jnp.concatenate([other[:, 4:], other[:, :4]], axis=1)
    suffix = jnp.dot(decay[:, :4], upper.T, precision=highest)
    below = jnp.dot(jnp.sum(decay, axis=2), strict_local[:, :4], precision=highest)
    logf_grad = (suffix + below[:, :, None]).reshape(H, rows).T
    forget_grad_low = (logf_grad * jax.nn.sigmoid(-forget_logit.astype(f32))).astype(bf16)

    first_out, first_low = backward_mm(dq, w_mix, extra_mix, 0, 3, 512, first_out, first_low)
    dk = (dk_all[:rows].astype(f32) + back[:, :D].astype(f32)).astype(bf16)
    dv = (dv_all[:rows].astype(f32) + back[:, D:].astype(f32)).astype(bf16)
    first_out, first_low = backward_mm(
        jnp.concatenate([dk, dv], axis=1), w_mix, extra_mix, 3, 6, 512, first_out, first_low
    )
    inner_low_grad = jnp.concatenate(
        [first_low[:, : 4 * RANK], linear_back(forget_grad_low, forget_sel)], axis=1
    ).astype(bf16)
    first_grad = first_out + linear_back(inner_low_grad, a_in) + linear_back(pad_low(forget_grad_low), w_forget)
    input_grad = middle_grad + norm_back(inputs, attention_gain, first_grad)
    input_grads = collect(input_grad.astype(bf16)).astype(f32)

    def to_owners(value):
        taken = lax.all_to_all(value, "dp", 0, 0, tiled=True)
        trees = jnp.sum(taken.astype(f32).reshape((dp // 2, 2) + value.shape[1:]), axis=1).astype(bf16)
        if seq != 4:
            return lax.all_gather(trees, "seq", axis=0, tiled=True)
        found = [trees]
        for k in (1, 2, 3):
            found.append(lax.ppermute(trees, "seq", [(i, i ^ k) for i in range(4)]))
        return jnp.concatenate(found, axis=0)

    chip = jnp.arange(dp // 2, dtype=jnp.int32)
    at = jnp.arange(seq, dtype=jnp.int32)
    if seq == 4:
        at = at ^ z
    tree_of = 2 * (2 * chip[None, :] + (at >> 1)[:, None]) + (at & 1)[:, None]
    id_of = all_ids[tree_of.reshape(-1)]
    one_hot = (jnp.arange(ADAPTERS, dtype=jnp.int32)[:, None] == id_of[None, :]).astype(bf16)

    def by_adapter(value):
        return jnp.einsum("at,trc->arc", one_hot, value, preferred_element_type=f32)

    ff_pack = jnp.swapaxes(ff_pack.reshape(3 * RANK, dp, tall), 0, 1)
    ff_sum = by_adapter(to_owners(ff_pack))

    early_lhs = jnp.concatenate(
        [
            linear_grad(gated, project_low_grad),
            linear_grad(second_norm, swiglu_low_grad),
            linear_grad(dy, hidden_low),
            linear_grad(branch_grad, project_low),
            linear_grad(gate_logit_grad, group(inner_low, 3)),
        ],
        axis=1,
    )
    early = jnp.pad(early_lhs, ((0, 0), (0, 128 - 6 * RANK))).astype(bf16).reshape(dp, wide, 128)
    early_sum = by_adapter(to_owners(early))

    forget_piece = linear_grad(forget_grad_low, group(inner_low, 4))
    forget_piece = forget_piece.T
    late = jnp.concatenate(
        [
            linear_grad(first_norm, inner_low_grad),
            linear_grad(dq, group(inner_low, 0)),
            linear_grad(dk, group(inner_low, 1)),
            linear_grad(dv, group(inner_low, 2)),
        ],
        axis=1,
    ).astype(bf16)
    late_sum = by_adapter(to_owners(late.reshape(dp, wide, 128)))
    forget_sum = by_adapter(to_owners(jnp.broadcast_to(forget_piece.astype(bf16)[None], (dp, RANK, H))))

    turned = lambda v: jnp.swapaxes(v, 1, 2)
    at16 = lambda v, i: v[:, :, i * RANK : (i + 1) * RANK]
    per = ADAPTERS * RANK // dp
    return (
        outputs,
        input_grads,
        jnp.concatenate([late_sum[:, :, : 5 * RANK], early_sum[:, :, : 3 * RANK]], axis=2),
        turned(ff_sum[:, :RANK]),
        turned(
            jnp.concatenate([late_sum[:, :, 5 * RANK :], at16(early_sum, 5), at16(early_sum, 3)], axis=2)
        ),
        turned(at16(early_sum, 4)),
        ff_sum[:, RANK:],
        lax.dynamic_slice_in_dim(forget_sum.reshape(ADAPTERS * RANK, H), me * per, per, 0),
    )


def solution(mesh):
    placed = (
        P("dp", "seq", None),
        P("dp", "seq", None),
        P("dp", None),
        P("dp"),
        P(),
        P("dp", None),
        P("dp", None),
        P(),
        P("dp", None),
        P(),
        P("dp", None),
        P("dp", None),
        P(None, "dp", None),
        P(None, "dp", None),
        P(None, None, "dp"),
        P(None, None, "dp"),
        P(None, None, "dp"),
        P("dp", None),
    )
    return jax.shard_map(
        functools.partial(body, (mesh.shape["dp"], mesh.shape["seq"])),
        mesh=mesh,
        in_specs=placed,
        out_specs=(
            P("dp", "seq", None),
            P("dp", "seq", None),
            P(None, "dp", None),
            P(None, "dp", None),
            P(None, None, "dp"),
            P(None, None, "dp"),
            P(None, None, "dp"),
            P("dp", None),
        ),
        check_vma=False,
    )
```

time: 2420 us -> 745 us (0.31)
  waiting for transfers between devices: 1460 us -> 10.7 us
  Pallas kernels: 0 us -> 447 us
  matrix products: 416 us -> 28.2 us
  blocking collectives: 146 us -> 0 us
  other arithmetic: 176 us -> 46.4 us
  starting transfers between devices: 1.28 us -> 105 us
  local copies, waits for them, and re-layouts: 179 us -> 77.1 us
    all_gather x20 -> x0, waiting for transfers between devices: 759 us -> none  [the longest x2 213 us: one_tree(): lax.all_gather(owned[3], 'dp', axis=0, tiled=True)]
    pallas_call x0 -> x13, Pallas kernels: none -> 447 us  [the longest x1 233 us: gather_all(): pl.pallas_call(functools.partial(gather_kernel, chunks), out_shape=tuple(...]
    reduce_scatter x6 -> x0, waiting for transfers between devices: 345 us -> none  [the longest x2 144 us: one_tree(): lax.psum_scatter(jnp.concatenate([key_part, value_part], axis=1).astype(j...]
    psum x3 -> x0, waiting for transfers between devices: 302 us -> none  [the longest x1 302 us: body(): lax.psum(accum[0].astype(jnp.bfloat16), 'seq').astype(jnp.float32)]
    dot_general x70 -> x16, matrix products: 283 us -> 8.6 us  [the longest x6 4.08 us: linear(): return jnp.dot(left, right, preferred_element_type=f32)]
    all_gather x8 -> x0, blocking collectives: 129 us -> none  [the longest x2 66.4 us: one_tree(): lax.all_gather(owned[8], 'dp', axis=2, tiled=True)]
    dot_general x24 -> x7, matrix products: 116 us -> 11.8 us  [linear_back(): lax.dot_general(left, right, (((1,), (1,)), ((), ())), preferred_element_...]
    ppermute x0 -> x24, starting transfers between devices: none -> 86.4 us  [the longest x12 64.6 us: to_owners(): found.append(lax.ppermute(trees, 'seq', [(i, i ^ k) for i in range(4)]))]
  transfers between devices with their start and end apart: 31 -> 28, of which waited for: 26 -> 5; matrix products, arithmetic and copies ran while one was open for 20% -> 9% of each run, Pallas kernels for 0% -> 6%
where the time goes in v1:
time: 745 us; the launch traced here: 732 us
  Pallas kernels  447 us (60%)
  starting transfers between devices  105 us (14%)
  local copies, waits for them, and re-layouts  77.1 us (10%)
  other arithmetic  46.4 us (6%)
  matrix products  28.2 us (4%)
  between operations  17.5 us (2%)
  waiting for transfers between devices  10.7 us (1%)
    pallas_call x1, Pallas kernels, gather_all(): pl.pallas_call(functools.partial(gather_kernel, chunks), out_shape=tuple(...  233 us
    ppermute x12, starting transfers between devices, to_owners(): found.append(lax.ppermute(trees, 'seq', [(i, i ^ k) for i in range(4)]))  64.6 us
    pallas_call x1, Pallas kernels, swiglu(): pl.pallas_call(swiglu_kernel, out_shape=tuple(state) + (jax.ShapeDtypeStr...  56.3 us
    pallas_call x1, Pallas kernels, attend(): pl.pallas_call(attend_kernel, out_shape=(jax.ShapeDtypeStruct((4 * BLOCK,...  41.7 us
    pallas_call x4, Pallas kernels, backward_mm(): pl.pallas_call(backward_kernel, out_shape=(jax.ShapeDtypeStruct((rows, de...  39.4 us
    pallas_call x1, Pallas kernels, attend_back(): pl.pallas_call(attend_back_kernel, out_shape=(jax.ShapeDtypeStruct((4 * B...  36.7 us
    pallas_call x4, Pallas kernels, forward_mm(): pl.pallas_call(forward_kernel, out_shape=jax.ShapeDtypeStruct((rows, coun...  32 us
    unnamed x186, local copies, waits for them, and re-layouts  22.3 us
  transfers between devices with their start and end apart: 28, of which 5 were waited for; matrix products, arithmetic and copies ran while one was open for 9% of the time, Pallas kernels for 6%

profile of v1, /device:TPU:0, one launch (start us, length us, event | category | flops | bytes accessed | tf_op | source)
XLA Modules:
  0.0 732.1 jit_solution(3318202913748186263)
XLA Ops:
  4.1 7.9 %share_facts.1 = (s32[8,8,128]{2,1,0:T(8,128)}, bf16[8,16,128]{2,1,0:T(8,128)(2,1)}) custom-call(s32[8,128]{1,0:T(8,128)} %pad.35.facts_ref, bf16[16,128]{1,0:T(8,128)(2,1)} %pad.36.forget_ref), custom_call_target="tpu_custom_call" | custom-call | tf_op jit(solution)/shard_map/share_facts/pallas_call | solution.py:340
  25.4 233.1 %gather_all.1 = (bf16[512,1536]{1,0:T(8,128)(2,1)}, bf16[512,1536]{1,0:T(8,128)(2,1)}, bf16[8,192,128]{2,1,0:T(8,128)(2,1)}, bf16[8,96,192]{2,1,0:T(8,128)(2,1)}...) custom-call(bf16[2,2,128,1536]{3,2,1,0:T(8,128)(2,1)} %bitcast.204, ...), custom_call_target="tpu_custom_call" | custom-call | tf_op jit(solution)/shard_map/gather_all/pallas_call | solution.py:542
  258.5 1.9 fusion.11
  267.4 10.8 %forward_mm.5 = bf16[512,3072]{1,0:T(8,128)(2,1)} custom-call(bf16[512,1536]{1,0:T(8,128)(2,1)} %copy-done.7, bf16[512,128]{1,0:T(8,128)(2,1)} %pad.38.low_ref, bf16[1536,6144]{1,0:T(8,128)(2,1)} %get-tuple-element.43.w_ref, bf16[128,6144]{1,0:T(8,128)(2,1)} %copy-done.6, f32[1,6144]{1,0:T(1,128)} %broadcast_in_dim.43.b_ref), custom_call_target="tpu_custom_call" | custom-call | flops 5234491392 | bytes 11010048 | tf_op jit(solution)/shard_map/forward_mm/pallas_call | solution.py:202
  278.4 7.2 forward_mm.6
  293.5 1.4 concatenate.121
  295.7 1.4 concatenate.117
  298.5 6.9 forward_mm.4.q_ref
  305.9 3.7 fusion.124
  317.0 3.8 fusion.123
  320.8 41.7 %attend.1 = (f32[512,1536]{1,0:T(8,128)}, bf16[24,128,2304]{2,1,0:T(8,128)(2,1)}) custom-call(s32[18]{0:T(128)} %broadcast_select_fusion.2.where_ref, bf16[512,1536]{1,0:T(8,128)(2,1)} %forward_mm.4.q_ref, bf16[512,1536]{1,0:T(8,128)(2,1)} %get-tuple-element.129.k_ref, bf16[512,1536]{1,0:T(8,128)(2,1)} %get-tuple-element.128.v_ref, ...), custom_call_target="tpu_custom_call" | custom-call | flops 8000000000 | bytes 25000000 | tf_op jit(solution)/shard_map/attend/pallas_call | solution.py:88
  362.5 2.8 multiply_convert_fusion.3.x_ref
  367.8 7.2 forward_mm.7
  374.9 3.0 multiply_reduce_fusion.1
  381.8 56.3 %swiglu.1 = (f32[512,1536]{1,0:T(8,128)}, f32[512,1536]{1,0:T(8,128)}, f32[512,16]{1,0:T(8,128)}, f32[512,16]{1,0:T(8,128)}, f32[512,16]{1,0:T(8,128)}, /*index=5*/bf16[48,4096]{1,0:T(8,128)(2,1)}) custom-call(bf16[512,1536]{1,0:T(8,128)(2,1)} %copy-done.24, bf16[512,16]{1,0:T(8,128)(2,1)} %get-tuple-element.155.lowg_ref, ...), custom_call_target="tpu_custom_call" | custom-call | flops 38654705664 | bytes 56623104 | tf_op jit(solution)/shard_map/swiglu/pallas_call | solution.py:284
  440.9 3.9 multiply_reduce_fusion
  447.8 2.3 fusion.48.acc_ref
  452.5 8.8 %backward_mm.4 = (f32[512,1536]{1,0:T(8,128)}, f32[512,128]{1,0:T(8,128)}) custom-call(bf16[512,1536]{1,0:T(8,128)(2,1)} %copy-done.15, bf16[1536,1536]{1,0:T(8,128)(2,1)} %get-tuple-element.48.w_ref, bf16[128,1536]{1,0:T(8,128)(2,1)} %broadcast_in_dim.48.e_ref, f32[512,1536]{1,0:T(8,128)} %fusion.48.acc_ref, f32[512,128]{1,0:T(8,128)} %broadcast_in_dim.49.acclow_ref), custom_call_target="tpu_custom_call" | custom-call | flops 2617245696 | bytes 11010048 | tf_op jit(solution)/shard_map/backward_mm/pallas_call | solution.py:233
  461.4 6.9 multiply_convert_fusion
  468.2 36.7 %attend_back.1 = (bf16[512,1536]{1,0:T(8,128)(2,1)}, bf16[1024,1536]{1,0:T(8,128)(2,1)}, bf16[1024,1536]{1,0:T(8,128)(2,1)}, f32[512,128]{1,0:T(8,128)}, f32[12,8,2,128]{3,2,1,0:T(2,128)}) custom-call(s32[18]{0:T(128)} %broadcast_select_fusion.2.where_ref, bf16[512,1536]{1,0:T(8,128)(2,1)} %forward_mm.4.q_ref, bf16[512,1536]{1,0:T(8,128)(2,1)} %get-tuple-element.129.k_ref, ...), custom_call_target="tpu_custom_call" | custom-call | flops 16000000000 | bytes 35000000 | tf_op jit(solution)/shard_map/attend_back/pallas_call | solution.py:165
  506.5 1.7 copy.275
  510.9 1.7 slice.234
  513.4 2.0 pad_maximum_fusion
  522.5 2.0 broadcast_in_dim.50.acc_ref
  524.5 9.0 %backward_mm.5 = (f32[512,1536]{1,0:T(8,128)}, f32[512,128]{1,0:T(8,128)}) custom-call(bf16[512,1536]{1,0:T(8,128)(2,1)} %get-tuple-element.122.g_ref, bf16[1536,6144]{1,0:T(8,128)(2,1)} %get-tuple-element.43.w_ref, bf16[128,6144]{1,0:T(8,128)(2,1)} %copy-done.6, f32[512,1536]{1,0:T(8,128)} %broadcast_in_dim.50.acc_ref, f32[512,128]{1,0:T(8,128)} %broadcast_in_dim.49.acclow_ref), custom_call_target="tpu_custom_call" | custom-call | flops 2617245696 | bytes 11010048 | tf_op jit(solution)/shard_map/backward_mm/pallas_call | solution.py:233
  533.6 1.9 copy.321
  535.5 1.9 pad.42.clone
  537.3 1.8 copy.332
  539.1 4.5 collective-permute-start.2
  545.9 3.3 all-to-all-start.3
  549.3 8.8 %backward_mm.6 = (f32[512,1536]{1,0:T(8,128)}, f32[512,128]{1,0:T(8,128)}) custom-call(bf16[512,1536]{1,0:T(8,128)(2,1)} %get-tuple-element.62.g_ref, bf16[1536,6144]{1,0:T(8,128)(2,1)} %get-tuple-element.43.w_ref, bf16[128,6144]{1,0:T(8,128)(2,1)} %copy-done.6, f32[512,1536]{1,0:T(8,128)} %get-tuple-element.63.acc_ref, f32[512,128]{1,0:T(8,128)} %get-tuple-element.64.acclow_ref), custom_call_target="tpu_custom_call" | custom-call | flops 2617245696 | bytes 11010048 | tf_op jit(solution)/shard_map/backward_mm/pallas_call | solution.py:233
  559.0 4.1 all-to-all-start.1
  563.5 2.5 collective-permute-start.22
  565.9 1.7 collective-permute-start.23
  568.7 1.9 collective-permute-start.4
  571.6 3.6 collective-permute-start.5
  576.9 4.2 all-to-all-start.2
  585.5 4.1 all-to-all-done.2
  591.5 3.2 collective-permute-start.19
  594.7 3.5 collective-permute-start.20
  598.9 1.5 pad_maximum_fusion.2
  603.2 16.0 %collective-permute-start.17 = (bf16[4,192,128]{2,0,1:T(4,128)(2,1)S(1)}, bf16[4,192,128]{2,0,1:T(4,128)(2,1)S(1)}, u32[]{:S(2)}, u32[]{:S(2)}) collective-permute-start(bf16[4,192,128]{2,0,1:T(4,128)(2,1)S(1)} %copy-done.57), channel_id=1, source_target_pairs={{0,3},{1,2},{2,1},{3,0},{4,7},{5,6},{6,5},{7,4},{8,11},{9,10},{10,... | collective-permute-start | bytes 589832 | tf_op jit(solution)/shard_map/ppermute | solution.py:809
  621.8 2.2 collective-permute-done.16
  624.1 1.5 fusion.29
  625.5 2.8 add_convert_fusion.1
  628.7 2.1 pad_maximum_fusion.1.g_ref
  631.8 12.8 %backward_mm.7 = (f32[512,1536]{1,0:T(8,128)}, f32[512,128]{1,0:T(8,128)}) custom-call(bf16[512,3072]{1,0:T(8,128)(2,1)} %pad_maximum_fusion.1.g_ref, bf16[1536,6144]{1,0:T(8,128)(2,1)} %get-tuple-element.43.w_ref, bf16[128,6144]{1,0:T(8,128)(2,1)} %copy-done.6, f32[512,1536]{1,0:T(8,128)} %get-tuple-element.65.acc_ref, f32[512,128]{1,0:T(8,128)} %get-tuple-element.66.acclow_ref), custom_call_target="tpu_custom_call" | custom-call | flops 5234491392 | bytes 15728640 | tf_op jit(solution)/shard_map/backward_mm/pallas_call | solution.py:233
  645.7 2.7 convolution_convert_fusion
  648.3 1.9 copy.314
  651.1 1.8 copy.317
  652.9 2.6 pad_maximum_fusion.6
  655.5 7.1 all-to-all-start
  662.6 2.8 convolution_add_fusion.1
  667.8 1.8 fusion.10
  670.9 1.6 collective-permute-start.8
  672.5 5.9 collective-permute-start.9
  678.4 3.0 collective-permute-start.11
  684.4 3.5 collective-permute-start.12
  687.9 17.4 %collective-permute-start.13 = (bf16[4,192,128]{2,0,1:T(4,128)(2,1)S(1)}, bf16[4,192,128]{2,0,1:T(4,128)(2,1)S(1)}, u32[]{:S(2)}, u32[]{:S(2)}) collective-permute-start(bf16[4,192,128]{2,0,1:T(4,128)(2,1)S(1)} %copy.286), channel_id=1, source_target_pairs={{0,2},{1,3},{2,0},{3,1},{4,6},{5,7},{6,4},{7,5},{8,10},{9,11},{10,... | collective-permute-start | bytes 589832 | tf_op jit(solution)/shard_map/ppermute | solution.py:809
  705.3 14.8 %collective-permute-start.14 = (bf16[4,192,128]{2,0,1:T(4,128)(2,1)S(1)}, bf16[4,192,128]{2,0,1:T(4,128)(2,1)S(1)}, u32[]{:S(2)}, u32[]{:S(2)}) collective-permute-start(bf16[4,192,128]{2,0,1:T(4,128)(2,1)S(1)} %copy.286), channel_id=1, source_target_pairs={{0,3},{1,2},{2,1},{3,0},{4,7},{5,6},{6,5},{7,4},{8,11},{9,10},{10,... | collective-permute-start | bytes 589832 | tf_op jit(solution)/shard_map/ppermute | solution.py:809
  720.1 1.4 pad_maximum_fusion.4
  721.7 1.9 maximum_convert_fusion
  723.6 2.3 collective-permute-done.13
  728.1 2.3 copy.304
  (379 shorter events, 86.0 us)
Async XLA Ops:
  0.6 22.7 %copy-start.22 = (bf16[8,512,16]{1,2,0:T(8,128)(2,1)S(1)}, bf16[8,512,16]{1,2,0:T(8,128)(2,1)}, u32[]{:S(2)}) copy-start(bf16[8,512,16]{1,2,0:T(8,128)(2,1)} %param.35) | copy-start | bytes 393220
  0.6 22.7 %copy-start.17 = (bf16[8,32,512]{2,1,0:T(8,128)(2,1)S(1)}, bf16[8,32,512]{2,1,0:T(8,128)(2,1)}, u32[]{:S(2)}) copy-start(bf16[8,32,512]{2,1,0:T(8,128)(2,1)} %param.38) | copy-start | bytes 786436
  264.2 50.3 %copy-start.52 = (bf16[512,24]{0,1:T(8,128)(2,1)}, bf16[512,24]{0,1:T(8,128)(2,1)S(1)}, u32[]{:S(2)}) copy-start(bf16[512,24]{0,1:T(8,128)(2,1)S(1)} %fusion.20) | copy-start | bytes 73732
  264.2 50.3 %collective-permute-start.1 = (bf16[512,24]{0,1:T(8,128)(2,1)S(1)}, bf16[512,24]{0,1:T(8,128)(2,1)S(1)}, u32[]{:S(2)}, u32[]{:S(2)}) collective-permute-start(bf16[512,24]{0,1:T(8,128)(2,1)S(1)} %fusion.20), channel_id=1, source_target_pairs={{0,4},{4,0},{8,12},{12,8},{16,20},{20,16},{24,28},{28,24},{1,5},{5... | collective-permute-start | bytes 73736 | tf_op jit(solution)/shard_map/ppermute | solution.py:585
  278.2 7.4 %copy-start.72 = (s32[2,4]{0,1:T(4,128)S(1)}, s32[2,4]{0,1:T(4,128)}, u32[]{:S(2)}) copy-start(s32[2,4]{0,1:T(4,128)} %constant.233.clone) | copy-start | bytes 100
  278.2 15.3 %copy-start.75 = (s32[6]{0:T(128)S(1)}, s32[6]{0:T(128)}, u32[]{:S(2)}) copy-start(s32[6]{0:T(128)} %constant.235.clone) | copy-start | bytes 76
  278.2 15.3 %copy-start.76 = (s32[6]{0:T(128)S(1)}, s32[6]{0:T(128)}, u32[]{:S(2)}) copy-start(s32[6]{0:T(128)} %constant.236.clone) | copy-start | bytes 76
  278.2 16.7 %copy-start.77 = (s32[8]{0:T(128)S(1)}, s32[8]{0:T(128)}, u32[]{:S(2)}) copy-start(s32[8]{0:T(128)} %constant.234.clone) | copy-start | bytes 100
  278.2 20.1 %copy-start.50 = (bf16[8,48,512]{2,1,0:T(8,128)(2,1)S(1)}, bf16[8,48,512]{2,1,0:T(8,128)(2,1)}, u32[]{:S(2)}) copy-start(bf16[8,48,512]{2,1,0:T(8,128)(2,1)} %get-tuple-element.51) | copy-start | bytes 1179652
  278.2 38.8 %collective-permute-start = (bf16[512,3072]{1,0:T(8,128)(2,1)}, bf16[512,3072]{1,0:T(8,128)(2,1)}, u32[]{:S(2)}, u32[]{:S(2)}) collective-permute-start(bf16[512,3072]{1,0:T(8,128)(2,1)} %forward_mm.5), channel_id=1, source_target_pairs={{0,4},{4,0},{8,12},{12,8},{16,20},{20,16},{24,28},{28,24},{1,5},{5... | collective-permute-start | bytes 9437192 | tf_op jit(solution)/shard_map/ppermute | solution.py:585
  297.8 7.6 %copy-start.43 = (bf16[16,1536]{1,0:T(8,128)(2,1)}, bf16[16,1536]{1,0:T(8,128)(2,1)S(1)}, u32[]{:S(2)}) copy-start(bf16[16,1536]{1,0:T(8,128)(2,1)S(1)} %slice.226) | copy-start | bytes 147460
  298.2 16.8 %copy-start.69 = (f32[8,8]{0,1:T(8,128)}, f32[8,8]{0,1:T(8,128)S(1)}, u32[]{:S(2)}) copy-start(f32[8,8]{0,1:T(8,128)S(1)} %fusion.78) | copy-start | bytes 772
  298.5 6.9 copy-start.11
  310.5 5.4 copy-start.45
  320.8 41.7 %copy-start.8 = (f32[512,1536]{1,0:T(8,128)S(1)}, f32[512,1536]{1,0:T(8,128)}, u32[]{:S(2)}) copy-start(f32[512,1536]{1,0:T(8,128)} %forward_mm.6) | copy-start | bytes 9437188
  362.5 3.9 copy-start.27
  367.8 10.2 %copy-start.62 = (f32[1536]{0:T(1024)S(1)}, f32[1536]{0:T(1024)}, u32[]{:S(2)}) copy-start(f32[1536]{0:T(1024)} %param.31) | copy-start | bytes 18436
  374.9 3.3 copy-start
  374.9 3.8 copy-start.2
  440.9 4.6 copy-start.3
  440.9 4.6 copy-start.12
  440.9 4.6 copy-start.60
  446.5 3.6 copy-start.15
  510.4 33.1 %collective-permute-start.7 = (f32[24,8,128]{2,0,1:T(8,128)}, f32[24,8,128]{2,0,1:T(8,128)}, u32[]{:S(2)}, u32[]{:S(2)}) collective-permute-start(f32[24,8,128]{2,0,1:T(8,128)} %pad_maximum_fusion.8), channel_id=1, source_target_pairs={{0,4},{4,0},{8,12},{12,8},{16,20},{20,16},{24,28},{28,24},{1,5},{5... | collective-permute-start | bytes 294920 | tf_op jit(solution)/shard_map/ppermute | solution.py:585
  513.4 3.1 copy-start.47
  513.4 5.9 copy-start.34
  515.4 110.1 %collective-permute-start.6 = (bf16[512,3072]{1,0:T(8,128)(2,1)}, bf16[512,3072]{1,0:T(8,128)(2,1)}, u32[]{:S(2)}, u32[]{:S(2)}) collective-permute-start(bf16[512,3072]{1,0:T(8,128)(2,1)} %pad_maximum_fusion), channel_id=1, source_target_pairs={{0,4},{4,0},{8,12},{12,8},{16,20},{20,16},{24,28},{28,24},{1,5},{5... | collective-permute-start | bytes 9437192 | tf_op jit(solution)/shard_map/ppermute | solution.py:585
  533.6 11.0 %copy-start.70 = (f32[8,8]{0,1:T(8,128)S(1)}, f32[8,8]{0,1:T(8,128)}, u32[]{:S(2)}) copy-start(f32[8,8]{0,1:T(8,128)} %copy-done.69) | copy-start | bytes 772
  533.6 11.3 %copy-start.53 = (bf16[512,24]{0,1:T(8,128)(2,1)S(1)}, bf16[512,24]{0,1:T(8,128)(2,1)}, u32[]{:S(2)}) copy-start(bf16[512,24]{0,1:T(8,128)(2,1)} %copy-done.52) | copy-start | bytes 73732
  539.1 51.7 %collective-permute-start.2 = (bf16[128,1536]{1,0:T(8,128)(2,1)}, bf16[128,1536]{1,0:T(8,128)(2,1)}, u32[]{:S(2)}, u32[]{:S(2)}) collective-permute-start(bf16[128,1536]{1,0:T(8,128)(2,1)} %get-tuple-element.138), channel_id=1, source_target_pairs={{0,0},{4,1},{1,2},{5,3},{2,4},{6,5},{3,6},{7,7},{8,8},{12,9},{9,10... | collective-permute-start | bytes 1179656 | tf_op jit(solution)/shard_map/ppermute | solution.py:612
  544.9 22.8 %copy-start.54 = (bf16[512,24]{0,1:T(8,128)(2,1)}, bf16[512,24]{0,1:T(8,128)(2,1)S(1)}, u32[]{:S(2)}) copy-start(bf16[512,24]{0,1:T(8,128)(2,1)S(1)} %fusion.74) | copy-start | bytes 73732
  545.9 13.0 %all-to-all-start.3 = ((bf16[8,2,192]{2,1,0:T(2,128)(2,1)}), bf16[8,2,192]{2,1,0:T(2,128)(2,1)S(1)}, u32[]{:S(2)}, u32[]{:S(2)}) async-start(bf16[8,2,192]{2,1,0:T(2,128)(2,1)} %reshape.518), calls=%async_computation.3 | async-start | bytes 16384 | tf_op jit(solution)/shard_map/all_to_all | solution.py:803
  549.3 8.8 %copy-start.56 = (bf16[1536,16]{0,1:T(8,128)(2,1)S(1)}, bf16[1536,16]{0,1:T(8,128)(2,1)}, u32[]{:S(2)}) copy-start(bf16[1536,16]{0,1:T(8,128)(2,1)} %convolution_convert_fusion.8) | copy-start | bytes 147460
  558.0 23.1 %copy-start.73 = (s32[16]{0:T(128)S(1)}, s32[16]{0:T(128)}, u32[]{:S(2)}) copy-start(s32[16]{0:T(128)} %gather_fusion.2) | copy-start | bytes 196
  559.0 17.9 %all-to-all-start.1 = ((bf16[8,192,128]{2,1,0:T(8,128)(2,1)}), bf16[8,192,128]{2,1,0:T(8,128)(2,1)}, u32[]{:S(2)}, u32[]{:S(2)}) async-start(bf16[8,192,128]{2,1,0:T(8,128)(2,1)} %bitcast.199), calls=%async_computation.1 | async-start | bytes 786432 | tf_op jit(solution)/shard_map/all_to_all | solution.py:803
  563.2 5.4 collective-permute-start.21
  563.5 5.2 collective-permute-start.22
  565.9 5.6 collective-permute-start.23
  568.6 77.1 %copy-start.37 = (bf16[512,16]{1,0:T(8,128)(2,1)}, bf16[512,16]{1,0:T(8,128)(2,1)S(1)}, u32[]{:S(2)}) copy-start(bf16[512,16]{1,0:T(8,128)(2,1)S(1)} %copy.278) | copy-start | bytes 49156
  568.6 22.8 %collective-permute-start.3 = (bf16[128,1536]{1,0:T(8,128)(2,1)}, bf16[128,1536]{1,0:T(8,128)(2,1)}, u32[]{:S(2)}, u32[]{:S(2)}) collective-permute-start(bf16[128,1536]{1,0:T(8,128)(2,1)} %get-tuple-element.141), channel_id=1, source_target_pairs={{4,0},{0,1},{5,2},{1,3},{6,4},{2,5},{7,6},{3,7},{12,8},{8,9},{13,1... | collective-permute-start | bytes 1179656 | tf_op jit(solution)/shard_map/ppermute | solution.py:612
  568.7 26.0 %collective-permute-start.4 = (bf16[128,1536]{1,0:T(8,128)(2,1)}, bf16[128,1536]{1,0:T(8,128)(2,1)}, u32[]{:S(2)}, u32[]{:S(2)}) collective-permute-start(bf16[128,1536]{1,0:T(8,128)(2,1)} %get-tuple-element.140), channel_id=1, source_target_pairs={{1,0},{5,1},{0,2},{4,3},{3,4},{7,5},{2,6},{6,7},{9,8},{13,9},{8,10... | collective-permute-start | bytes 1179656 | tf_op jit(solution)/shard_map/ppermute | solution.py:612
  571.6 26.7 %collective-permute-start.5 = (bf16[128,1536]{1,0:T(8,128)(2,1)}, bf16[128,1536]{1,0:T(8,128)(2,1)}, u32[]{:S(2)}, u32[]{:S(2)}) collective-permute-start(bf16[128,1536]{1,0:T(8,128)(2,1)} %get-tuple-element.139), channel_id=1, source_target_pairs={{5,0},{1,1},{4,2},{0,3},{7,4},{3,5},{6,6},{2,7},{13,8},{9,9},{12,1... | collective-permute-start | bytes 1179656 | tf_op jit(solution)/shard_map/ppermute | solution.py:612
  576.9 12.7 %all-to-all-start.2 = ((bf16[8,48,512]{2,1,0:T(8,128)(2,1)}), bf16[8,48,512]{2,1,0:T(8,128)(2,1)}, u32[]{:S(2)}, u32[]{:S(2)}) async-start(bf16[8,48,512]{2,1,0:T(8,128)(2,1)} %bitcast.198), calls=%async_computation.2 | async-start | bytes 786432 | tf_op jit(solution)/shard_map/all_to_all | solution.py:803
  590.8 12.1 %collective-permute-start.18 = (bf16[4,48,512]{2,0,1:T(4,128)(2,1)S(1)}, bf16[4,48,512]{2,0,1:T(4,128)(2,1)S(1)}, u32[]{:S(2)}, u32[]{:S(2)}) collective-permute-start(bf16[4,48,512]{2,0,1:T(4,128)(2,1)S(1)} %copy.296), channel_id=1, source_target_pairs={{0,1},{1,0},{2,3},{3,2},{4,5},{5,4},{6,7},{7,6},{8,9},{9,8},{10,11... | collective-permute-start | bytes 589832 | tf_op jit(solution)/shard_map/ppermute | solution.py:809
  591.5 11.8 %collective-permute-start.19 = (bf16[4,48,512]{2,0,1:T(4,128)(2,1)S(1)}, bf16[4,48,512]{2,0,1:T(4,128)(2,1)S(1)}, u32[]{:S(2)}, u32[]{:S(2)}) collective-permute-start(bf16[4,48,512]{2,0,1:T(4,128)(2,1)S(1)} %copy.296), channel_id=1, source_target_pairs={{0,2},{1,3},{2,0},{3,1},{4,6},{5,7},{6,4},{7,5},{8,10},{9,11},{10,... | collective-permute-start | bytes 589832 | tf_op jit(solution)/shard_map/ppermute | solution.py:809
  594.7 24.5 %collective-permute-start.20 = (bf16[4,48,512]{2,0,1:T(4,128)(2,1)S(1)}, bf16[4,48,512]{2,0,1:T(4,128)(2,1)S(1)}, u32[]{:S(2)}, u32[]{:S(2)}) collective-permute-start(bf16[4,48,512]{2,0,1:T(4,128)(2,1)S(1)} %copy.296), channel_id=1, source_target_pairs={{0,3},{1,2},{2,1},{3,0},{4,7},{5,6},{6,5},{7,4},{8,11},{9,10},{10,... | collective-permute-start | bytes 589832 | tf_op jit(solution)/shard_map/ppermute | solution.py:809
  598.2 23.6 %collective-permute-start.15 = (bf16[4,192,128]{2,0,1:T(4,128)(2,1)}, bf16[4,192,128]{2,0,1:T(4,128)(2,1)S(1)}, u32[]{:S(2)}, u32[]{:S(2)}) collective-permute-start(bf16[4,192,128]{2,0,1:T(4,128)(2,1)} %copy.291), channel_id=1, source_target_pairs={{0,1},{1,0},{2,3},{3,2},{4,5},{5,4},{6,7},{7,6},{8,9},{9,8},{10,11... | collective-permute-start | bytes 589832 | tf_op jit(solution)/shard_map/ppermute | solution.py:809
  602.9 21.2 %collective-permute-start.16 = (bf16[4,192,128]{2,0,1:T(4,128)(2,1)S(1)}, bf16[4,192,128]{2,0,1:T(4,128)(2,1)S(1)}, u32[]{:S(2)}, u32[]{:S(2)}) collective-permute-start(bf16[4,192,128]{2,0,1:T(4,128)(2,1)S(1)} %copy-done.57), channel_id=1, source_target_pairs={{0,2},{1,3},{2,0},{3,1},{4,6},{5,7},{6,4},{7,5},{8,10},{9,11},{10,... | collective-permute-start | bytes 589832 | tf_op jit(solution)/shard_map/ppermute | solution.py:809
  603.2 20.8 %collective-permute-start.17 = (bf16[4,192,128]{2,0,1:T(4,128)(2,1)S(1)}, bf16[4,192,128]{2,0,1:T(4,128)(2,1)S(1)}, u32[]{:S(2)}, u32[]{:S(2)}) collective-permute-start(bf16[4,192,128]{2,0,1:T(4,128)(2,1)S(1)} %copy-done.57), channel_id=1, source_target_pairs={{0,3},{1,2},{2,1},{3,0},{4,7},{5,6},{6,5},{7,4},{8,11},{9,10},{10,... | collective-permute-start | bytes 589832 | tf_op jit(solution)/shard_map/ppermute | solution.py:809
  619.2 6.3 copy-start.33
  621.0 4.6 copy-start.31
  645.6 4.5 copy-start.38
  651.1 11.5 %copy-start.30 = (bf16[8,192,128]{2,1,0:T(8,128)(2,1)S(1)}, bf16[8,192,128]{2,1,0:T(8,128)(2,1)}, u32[]{:S(2)}) copy-start(bf16[8,192,128]{2,1,0:T(8,128)(2,1)} %get-tuple-element.42) | copy-start | bytes 1179652
  655.5 27.6 %all-to-all-start = ((bf16[8,192,128]{2,1,0:T(8,128)(2,1)}), bf16[8,192,128]{2,1,0:T(8,128)(2,1)}, u32[]{:S(2)}, u32[]{:S(2)}) async-start(bf16[8,192,128]{2,1,0:T(8,128)(2,1)} %pad_maximum_fusion.6), calls=%async_computation | async-start | bytes 786432 | tf_op jit(solution)/shard_map/all_to_all | solution.py:803
  662.6 2.8 copy-start.5
  662.6 2.8 copy-start.36
  669.7 11.8 %copy-start.21 = (f32[8,192,128]{2,0,1:T(8,128)S(1)}, f32[8,192,128]{2,0,1:T(8,128)}, u32[]{:S(2)}) copy-start(f32[8,192,128]{2,0,1:T(8,128)} %fusion.29) | copy-start | bytes 2359300
  670.9 17.0 %collective-permute-start.8 = (bf16[128,1536]{1,0:T(8,128)(2,1)}, bf16[128,1536]{1,0:T(8,128)(2,1)S(1)}, u32[]{:S(2)}, u32[]{:S(2)}) collective-permute-start(bf16[128,1536]{1,0:T(8,128)(2,1)} %get-tuple-element.132), channel_id=1, source_target_pairs={{0,0},{4,1},{1,2},{5,3},{2,4},{6,5},{3,6},{7,7},{8,8},{12,9},{9,10... | collective-permute-start | bytes 1179656 | tf_op jit(solution)/shard_map/ppermute | solution.py:612
  672.5 32.8 %collective-permute-start.9 = (bf16[128,1536]{1,0:T(8,128)(2,1)}, bf16[128,1536]{1,0:T(8,128)(2,1)}, u32[]{:S(2)}, u32[]{:S(2)}) collective-permute-start(bf16[128,1536]{1,0:T(8,128)(2,1)} %get-tuple-element.135), channel_id=1, source_target_pairs={{4,0},{0,1},{5,2},{1,3},{6,4},{2,5},{7,6},{3,7},{12,8},{8,9},{13,1... | collective-permute-start | bytes 1179656 | tf_op jit(solution)/shard_map/ppermute | solution.py:612
  678.4 41.7 %collective-permute-start.10 = (bf16[128,1536]{1,0:T(8,128)(2,1)}, bf16[128,1536]{1,0:T(8,128)(2,1)}, u32[]{:S(2)}, u32[]{:S(2)}) collective-permute-start(bf16[128,1536]{1,0:T(8,128)(2,1)} %get-tuple-element.134), channel_id=1, source_target_pairs={{1,0},{5,1},{0,2},{4,3},{3,4},{7,5},{2,6},{6,7},{9,8},{13,9},{8,10... | collective-permute-start | bytes 1179656 | tf_op jit(solution)/shard_map/ppermute | solution.py:612
  678.4 41.7 %collective-permute-start.11 = (bf16[128,1536]{1,0:T(8,128)(2,1)}, bf16[128,1536]{1,0:T(8,128)(2,1)}, u32[]{:S(2)}, u32[]{:S(2)}) collective-permute-start(bf16[128,1536]{1,0:T(8,128)(2,1)} %get-tuple-element.133), channel_id=1, source_target_pairs={{5,0},{1,1},{4,2},{0,3},{7,4},{3,5},{6,6},{2,7},{13,8},{9,9},{12,1... | collective-permute-start | bytes 1179656 | tf_op jit(solution)/shard_map/ppermute | solution.py:612
  684.4 39.2 %collective-permute-start.12 = (bf16[4,192,128]{2,0,1:T(4,128)(2,1)S(1)}, bf16[4,192,128]{2,0,1:T(4,128)(2,1)S(1)}, u32[]{:S(2)}, u32[]{:S(2)}) collective-permute-start(bf16[4,192,128]{2,0,1:T(4,128)(2,1)S(1)} %copy.286), channel_id=1, source_target_pairs={{0,1},{1,0},{2,3},{3,2},{4,5},{5,4},{6,7},{7,6},{8,9},{9,8},{10,11... | collective-permute-start | bytes 589832 | tf_op jit(solution)/shard_map/ppermute | solution.py:809
  687.9 38.0 %collective-permute-start.13 = (bf16[4,192,128]{2,0,1:T(4,128)(2,1)S(1)}, bf16[4,192,128]{2,0,1:T(4,128)(2,1)S(1)}, u32[]{:S(2)}, u32[]{:S(2)}) collective-permute-start(bf16[4,192,128]{2,0,1:T(4,128)(2,1)S(1)} %copy.286), channel_id=1, source_target_pairs={{0,2},{1,3},{2,0},{3,1},{4,6},{5,7},{6,4},{7,5},{8,10},{9,11},{10,... | collective-permute-start | bytes 589832 | tf_op jit(solution)/shard_map/ppermute | solution.py:809
  705.3 20.6 %collective-permute-start.14 = (bf16[4,192,128]{2,0,1:T(4,128)(2,1)S(1)}, bf16[4,192,128]{2,0,1:T(4,128)(2,1)S(1)}, u32[]{:S(2)}, u32[]{:S(2)}) collective-permute-start(bf16[4,192,128]{2,0,1:T(4,128)(2,1)S(1)} %copy.286), channel_id=1, source_target_pairs={{0,3},{1,2},{2,1},{3,0},{4,7},{5,6},{6,5},{7,4},{8,11},{9,10},{10,... | collective-permute-start | bytes 589832 | tf_op jit(solution)/shard_map/ppermute | solution.py:809
  (42 other events, 74.5 us)

commit v2 on v1

--- a/solution.py
+++ b/solution.py
@@ -115,11 +115,11 @@
     vbuf[half:] = v2_ref[...]
     dkbuf[...] = jnp.zeros_like(dkbuf)
     dvbuf[...] = jnp.zeros_like(dvbuf)
-    ksum_ref[...] = jnp.zeros_like(ksum_ref)
 
     @pl.when(pair == 0)
     def _():
         qsum_ref[...] = jnp.zeros_like(qsum_ref)
+        ksum_ref[...] = jnp.zeros_like(ksum_ref)
 
     lane = lax.broadcasted_iota(jnp.int32, (BLOCK, BLOCK), 1)
     scale = HD ** (-0.5)
@@ -144,7 +144,7 @@
             wide = score_grad.astype(f32)
             col = jnp.sum(wide, axis=0, keepdims=True)
             for e in range(count):
-                ksum_ref[where_ref[first + e], a : a + 1, :] += col[:, e * BLOCK : (e + 1) * BLOCK]
+                ksum_ref[where_ref[first + e], pl.ds(2 * pair + a, 1), :] += col[:, e * BLOCK : (e + 1) * BLOCK]
             row_sums = row_sums + jnp.where(lane == 2 * pair + a, jnp.sum(wide, axis=1, keepdims=True), 0.0)
             dqs.append(linear(score_grad, keys))
             dks.append(linear_grad(score_grad, queries))
@@ -169,7 +169,7 @@
             jax.ShapeDtypeStruct((8 * BLOCK, D), bf16),
             jax.ShapeDtypeStruct((8 * BLOCK, D), bf16),
             jax.ShapeDtypeStruct((4 * BLOCK, BLOCK), f32),
-            jax.ShapeDtypeStruct((PAIRS, 8, 2, BLOCK), f32),
+            jax.ShapeDtypeStruct((8, BLOCK, BLOCK), f32),
         ),
         grid_spec=pltpu.PrefetchScalarGridSpec(
             num_scalar_prefetch=1,
@@ -180,7 +180,7 @@
                 full,
                 full,
                 pl.BlockSpec((4 * BLOCK, BLOCK), lambda g, w: (0, 0)),
-                pl.BlockSpec((None, 8, 2, BLOCK), lambda g, w: (g, 0, 0, 0)),
+                pl.BlockSpec((8, BLOCK, BLOCK), lambda g, w: (0, 0, 0)),
             ),
             scratch_shapes=[pltpu.VMEM((8 * BLOCK, 2 * HD), bf16)] * 2
             + [pltpu.VMEM((8 * BLOCK, 2 * HD), f32)] * 2,
@@ -351,206 +351,1206 @@
     )(facts, forget)
 
 
-def column_chunks(widths):
-    chunks = []
-    for index, (total, width) in enumerate(widths):
-        for first in range(0, total, width):
-            chunks.append((index, first, width))
-    return chunks
-
-
-def shared_rows(count):
-    return count // 4
-
-
-def gather_kernel(chunks, *refs):
-    (tok, cot, inner, model, ffp, mix, fg, out, dn, sw) = refs[:10]
-    (x_o, dy_o, inner_o, model_o, ff_o, mix_o, fg_o, out_o, dn_o, sw_o) = refs[10:20]
-    send, recv, own_sem, small_send, small_recv, row_send, row_recv = refs[20:]
-    me, z = lax.axis_index("dp"), lax.axis_index("seq")
-    core, odd = me & 1, z & 1
-    first_to = me ^ (2 + 2 * core)
-    second_to = me ^ (4 - 2 * core)
-
+def remote(src, dst, send, recv, to):
+    return pltpu.make_async_remote_copy(
+        src_ref=src, dst_ref=dst, send_sem=send, recv_sem=recv, device_id=to, device_id_type=MESH
+    )
+
+
+def peers_of(me, z):
+    return [(me ^ m, z) for m in range(1, 8)] + [(me ^ m, z ^ k) for m in (0, 1) for k in (1, 2, 3)]
+
+
+def greet(me, z):
     barrier = pltpu.get_barrier_semaphore()
-    peers = [(me ^ m, z) for m in range(1, 8)] + [(me ^ m, z ^ k) for m in (0, 1) for k in (1, 2, 3)]
+    peers = peers_of(me, z)
     for peer in peers:
         pl.semaphore_signal(barrier, inc=1, device_id=peer, device_id_type=MESH)
     pl.semaphore_wait(barrier, len(peers))
 
-    sources = (mix, fg, out, dn, sw)
-    targets = (mix_o, fg_o, out_o, dn_o, sw_o)
-    done = []
-
-    def remote(src, dst, s, r, to):
-        copy = pltpu.make_async_remote_copy(
-            src_ref=src, dst_ref=dst, send_sem=s, recv_sem=r, device_id=to, device_id_type=MESH
-        )
-        copy.start()
-        done.append(copy)
-        return copy
-
-    tree_core = z >> 1
-    rows = []
-    for kind, (src, dst) in enumerate(((tok, x_o), (cot, dy_o))):
-        for j in range(2):
-            for b in range(2):
-                to = ((me & ~1) | (b ^ odd), 2 * core + j)
-                self_copy = (to[0] == me) & (to[1] == z)
-                spot = dst.at[pl.ds(z * BLOCK, BLOCK)]
-                far = pltpu.make_async_remote_copy(
-                    src_ref=src.at[j, b],
-                    dst_ref=spot,
-                    send_sem=row_send.at[kind, 2 * j + b],
-                    recv_sem=row_recv.at[kind, z],
-                    device_id=to,
-                    device_id_type=MESH,
-                )
-                near = pltpu.make_async_copy(src.at[j, b], spot, row_send.at[kind, 2 * j + b])
-
-                @pl.when(self_copy)
-                def _(near=near):
-                    near.start()
-
-                @pl.when(jnp.logical_not(self_copy))
-                def _(far=far):
-                    far.start()
-
-                rows.append((self_copy, near, far))
-
+
+class Mover:
+    def __init__(self, plan, shards, full, sems):
+        self.plan, self.items = plan, []
+        self.send, self.recv, self.own = sems
+        for (target, first, width, step, shared), src in zip(plan, shards):
+            for at in range(0, width, step):
+                self.items.append((src, full[target], at, first + at, step, shared))
+        self.me, self.z = lax.axis_index("dp"), lax.axis_index("seq")
+        core = self.me & 1
+        self.odd = self.z & 1
+        self.near = self.me ^ (2 + 2 * core)
+        self.next = self.me ^ (4 - 2 * core)
+        self.far = self.me ^ 6
+
+    def sizes(self, i):
+        src, shared = self.items[i][0], self.items[i][5]
+        count = src.shape[0]
+        return count, shared, count - shared
+
+    def spot(self, i, owner, start, length):
+        src, dst, _, first, width, _ = self.items[i]
+        rows = pl.ds(pl.multiple_of(owner * src.shape[0] + start, 16), length)
+        return dst.at[rows, pl.ds(first, width)]
+
+    def copy(self, i, slot):
+        src, dst, at, _, width, _ = self.items[i]
+        count, shared, length = self.sizes(i)
+        low = self.odd * shared
+        cols = pl.ds(at, width)
+        owner = {2: self.near, 3: self.near, 4: self.next, 5: self.far, 7: self.near, 8: self.next, 9: self.far,
+                 10: self.near, 11: self.next, 12: self.far}
+        partner, above = (self.me ^ 1, self.z), (self.me, self.z ^ 1)
+        if slot in (0, 1):
+            here = src.at[pl.ds(pl.multiple_of(low, 16), length), cols]
+            there = self.spot(i, self.me, low, length)
+            to = (self.near if slot == 0 else self.next, self.z)
+        elif slot == 2:
+            here = there = self.spot(i, owner[2], low, length)
+            to = (self.next, self.z)
+        elif slot in (3, 4, 5):
+            here = there = self.spot(i, owner[slot], self.odd * (count - shared), shared)
+            to = above
+        elif slot == 6:
+            here, there, to = src.at[:, cols], self.spot(i, self.me, 0, count), partner
+        elif slot in (7, 8, 9):
+            here = there = self.spot(i, owner[slot], low, length)
+            to = partner
+        else:
+            here = there = self.spot(i, owner[slot], (1 - self.odd) * (count - shared), shared)
+            to = partner
+        return remote(here, there, self.send.at[i, slot], self.recv.at[i, slot], to)
+
+    def local(self, i):
+        src, _, at, _, width, _ = self.items[i]
+        return pltpu.make_async_copy(src.at[:, pl.ds(at, width)], self.spot(i, self.me, 0, src.shape[0]), self.own.at[i])
+
+    def phase(self, i, stage):
+        if stage == 0:
+            for slot in (0, 1, 6):
+                self.copy(i, slot).start()
+            self.local(i).start()
+        elif stage == 1:
+            self.copy(i, 0).wait_recv()
+            for slot in (2, 3, 7):
+                self.copy(i, slot).start()
+            self.copy(i, 1).wait_recv()
+            for slot in (4, 8):
+                self.copy(i, slot).start()
+        elif stage == 2:
+            self.copy(i, 2).wait_recv()
+            for slot in (5, 9):
+                self.copy(i, slot).start()
+        else:
+            for slot in (3, 4, 5):
+                self.copy(i, slot).wait_recv()
+                self.copy(i, slot + 7).start()
+
+    def polls(self, count):
+        n = len(self.items)
+        out = [[] for _ in range(count)]
+        out[0] = [(i, 0) for i in range(n)]
+        span = max(1, count - 3)
+        for stage in (1, 2, 3):
+            for i in range(n):
+                out[min(count - 1, i * span // n + stage)].append((i, stage))
+        return out
+
+    def run(self, poll):
+        for i, stage in poll:
+            self.phase(i, stage)
+
+    def finish(self):
+        for i in range(len(self.items)):
+            for slot in range(6, 13):
+                self.copy(i, slot).wait_recv()
+            for slot in range(13):
+                self.copy(i, slot).wait_send()
+            self.local(i).wait()
+
+
+def mover_scratch(plan):
+    dma = pltpu.SemaphoreType.DMA
+    count = sum(width // step for _, _, width, step, _ in plan)
+    return [dma((count, 13)), dma((count, 13)), dma((count,))]
+
+
+def shard_specs(pieces):
+    return [
+        pl.BlockSpec((v.shape[0], width), lambda *g, at=at: (0, at), pipeline_mode=pl.Buffered(1))
+        for v, at, width in pieces
+    ]
+
+
+def full_shapes(plan, pieces):
+    shapes = {}
+    for (target, first, width, _, _), (v, _, _) in zip(plan, pieces):
+        rows, cols = shapes.get(target, (8 * v.shape[0], 0))
+        shapes[target] = (rows, max(cols, first + width))
+    return tuple(jax.ShapeDtypeStruct(shapes[t], bf16) for t in sorted(shapes))
+
+
+def spread_rows(src, dst, send, recv):
+    me, z = lax.axis_index("dp"), lax.axis_index("seq")
+    core, odd, tree_core = me & 1, z & 1, z >> 1
+    for j in range(2):
+        for b in range(2):
+            to = ((me & ~1) | (b ^ odd), 2 * core + j)
+            same = (to[0] == me) & (to[1] == z)
+            spot = dst.at[pl.ds(pl.multiple_of(z * BLOCK, BLOCK), BLOCK)]
+
+            @pl.when(same)
+            def _():
+                pltpu.make_async_copy(src.at[j, b], spot, send.at[2 * j + b]).start()
+
+            @pl.when(jnp.logical_not(same))
+            def _():
+                remote(src.at[j, b], spot, send.at[2 * j + b], recv.at[z], to).start()
+
+
+def wait_rows(src, dst, send, recv):
+    me, z = lax.axis_index("dp"), lax.axis_index("seq")
+    core, odd, tree_core = me & 1, z & 1, z >> 1
+    for j in range(2):
+        for b in range(2):
+            to = ((me & ~1) | (b ^ odd), 2 * core + j)
+            same = (to[0] == me) & (to[1] == z)
+            spot = dst.at[pl.ds(pl.multiple_of(z * BLOCK, BLOCK), BLOCK)]
+
+            @pl.when(same)
+            def _():
+                pltpu.make_async_copy(src.at[j, b], spot, send.at[2 * j + b]).wait()
+
+            @pl.when(jnp.logical_not(same))
+            def _():
+                remote(src.at[j, b], spot, send.at[2 * j + b], recv.at[z], to).wait_send()
+
+    for p in range(4):
+        @pl.when(jnp.logical_not((p == z) & (core == tree_core)))
+        def _():
+            spot = dst.at[pl.ds(p * BLOCK, BLOCK)]
+            remote(src.at[0, 0], spot, send.at[p], recv.at[p], (me ^ 1, z)).wait_recv()
+
+
+def vmem_spec():
+    return pl.BlockSpec(memory_space=pltpu.VMEM)
+
+
+def hbm_spec():
+    return pl.BlockSpec(memory_space=pl.ANY)
+
+
+def full_shape(shard):
+    return jax.ShapeDtypeStruct((8 * shard.shape[0], shard.shape[1]), bf16)
+
+
+FIRST_PLAN = ((1, 0, EXTRA, EXTRA, 48), (0, 0, 4 * D, 512, 48))
+
+
+def first_kernel(tok, inner, model, ffp, fg, mix, x_o, inner_o, model_o, ff_o, mix_o, fg_o,
+                 send, recv, own, small_send, small_recv, row_send, row_recv):
+    me, z = lax.axis_index("dp"), lax.axis_index("seq")
+    greet(me, z)
+    mover = Mover(FIRST_PLAN, (fg, mix), (mix_o, fg_o), (send, recv, own))
+    n = len(mover.items)
+    for i in range(3):
+        mover.phase(i, 0)
+    spread_rows(tok, x_o, row_send, row_recv)
     small = []
     for kind, (src, dst) in enumerate(((inner, inner_o), (model, model_o), (ffp, ff_o))):
         for m in range(1, 8):
-            remote(src.at[me ^ m], dst.at[me], small_send.at[kind, m], small_recv.at[kind, m], (me ^ m, z))
-        copy = pltpu.make_async_copy(src.at[me], dst.at[me], small_send.at[kind, 0])
+            small.append(
+                remote(src.at[me ^ m], dst.at[me], small_send.at[kind, m], small_recv.at[kind, m], (me ^ m, z))
+            )
+        small.append(pltpu.make_async_copy(src.at[me], dst.at[me], small_send.at[kind, 0]))
+    for copy in small:
         copy.start()
-        small.append(copy)
-
-    own = []
-    for i, (index, first, width) in enumerate(chunks):
-        src, dst = sources[index], targets[index]
-        count = src.shape[0]
-        copy = pltpu.make_async_copy(
-            src.at[:, pl.ds(first, width)],
-            dst.at[pl.ds(pl.multiple_of(me * count, count), count), pl.ds(first, width)],
-            own_sem.at[i],
+    for t in range(n + 2):
+        if t + 3 < n:
+            mover.phase(t + 3, 0)
+        for stage in (1, 2, 3):
+            if 0 <= t - stage + 1 < n:
+                mover.phase(t - stage + 1, stage)
+    wait_rows(tok, x_o, row_send, row_recv)
+    for copy in small:
+        copy.wait()
+    mover.finish()
+
+
+def first(tokens, inner, model, ffp, mix, fg):
+    args = (tokens.reshape(2, 2, BLOCK, D), inner, model, ffp, fg, mix)
+    dma = pltpu.SemaphoreType.DMA
+    pieces = ((fg, 0, EXTRA), (mix, 0, 4 * D))
+    return pl.pallas_call(
+        first_kernel,
+        out_shape=(
+            jax.ShapeDtypeStruct((4 * BLOCK, D), bf16),
+            *(jax.ShapeDtypeStruct(v.shape, bf16) for v in (inner, model, ffp)),
+            *full_shapes(FIRST_PLAN, pieces),
+        ),
+        in_specs=[vmem_spec()] * 6,
+        out_specs=(hbm_spec(),) * 6,
+        scratch_shapes=mover_scratch(FIRST_PLAN) + [dma((3, 8)), dma((3, 8)), dma((4,)), dma((4,))],
+        compiler_params=pltpu.CompilerParams(collective_id=1, has_side_effects=True),
+        name="first",
+    )(*args)
+
+
+def lane_groups(shape):
+    return lax.broadcasted_iota(jnp.int32, shape, 1) // RANK
+
+
+def row_groups(shape):
+    return lax.broadcasted_iota(jnp.int32, shape, 0) // RANK
+
+
+def split_refs(plan, refs, outs, extra):
+    n = len(plan)
+    m = len({target for target, *_ in plan})
+    shards, outputs = refs[:n], refs[n : n + outs]
+    full, sems, rest = refs[n + outs : n + outs + m], refs[n + outs + m : n + outs + m + 3], refs[n + outs + m + 3 :]
+    assert len(rest) == extra
+    return shards, outputs, full, sems, rest
+
+
+def project_kernel(plan, x, gain, inner, got_model, w_ref, w_forget, forget_sel, bias, *refs):
+    shards, outputs, full, sems, (csend, crecv) = split_refs(plan, refs, 9, 2)
+    norm_o, low_o, kv_o, kv2_o, q_o, gate_o, forget_o, forget2_o, model = outputs
+    me, z = lax.axis_index("dp"), lax.axis_index("seq")
+    partner = (me ^ 1, z)
+    step = pl.program_id(0)
+    mover = Mover(plan, shards, full, sems)
+    polls = mover.polls(12)
+    place = jnp.where(step < 6, step + 3, jnp.where(step < 9, step - 6, step))
+    group = place // 3
+
+    def pass_kv(j):
+        cols = pl.ds(j * 512, 512)
+        return remote(kv_o.at[:, cols], kv2_o.at[:, cols], csend.at[j], crecv.at[j], partner)
+
+    pass_forget = remote(forget_o, forget2_o, csend.at[6], crecv.at[6], partner)
+
+    @pl.when(step == 0)
+    def _():
+        greet(me, z)
+        mover.run(polls[0])
+        model[6 * RANK :] = jnp.zeros_like(model[6 * RANK :])
+        for d in range(8):
+            model[: 6 * RANK, d * 192 : (d + 1) * 192] = got_model[d]
+        inputs = x[...].astype(f32)
+        norm = (inputs * rms_scale(inputs) * gain[...]).astype(bf16)
+        norm_o[...] = norm
+        low = linear(norm, inner[...])
+        low = jnp.where(lane_groups(low.shape) < 5, low, 0.0).astype(bf16)
+        low_o[...] = low
+        logit = linear(norm, w_forget[...]) + linear(low, forget_sel[...]) + bias[...]
+        forget_o[...] = logit.astype(bf16)
+
+    extra = model[:, pl.ds(pl.multiple_of((place - 3 * group) * 512, 512), 512)]
+    extra = jnp.where(row_groups(extra.shape) == group, extra, jnp.zeros_like(extra))
+    value = linear(norm_o[...], w_ref[...]) + linear(low_o[...], extra)
+
+    @pl.when(step < 6)
+    def _():
+        kv_o[:, pl.ds(pl.multiple_of((place - 3) * 512, 512), 512)] = value.astype(bf16)
+
+    @pl.when(group == 0)
+    def _():
+        q_o[:, pl.ds(pl.multiple_of(place * 512, 512), 512)] = value.astype(bf16)
+
+    @pl.when(group == 3)
+    def _():
+        gate_o[:, pl.ds(pl.multiple_of((place - 9) * 512, 512), 512)] = value
+
+    for s in range(1, 12):
+        @pl.when(step == s)
+        def _():
+            if s <= 6:
+                pass_kv(s - 1).start()
+            if s == 1:
+                pass_forget.start()
+            mover.run(polls[s])
+            if s == 11:
+                mover.finish()
+                pass_forget.wait()
+                for j in range(6):
+                    pass_kv(j).wait()
+
+
+def project(x, gain, inner, got_model, w_mix, w_forget, forget_sel, bias, plan, pieces):
+    rows = 4 * BLOCK
+    block = lambda j: jnp.where(j < 6, j + 3, jnp.where(j < 9, j - 6, j))
+    small = lambda v: pl.BlockSpec(v.shape, lambda j: (0,) * v.ndim, pipeline_mode=pl.Buffered(1))
+    keep = lambda *shape: pl.BlockSpec(shape, lambda j: (0,) * len(shape))
+    dma = pltpu.SemaphoreType.DMA
+    sds = jax.ShapeDtypeStruct
+    full = full_shapes(plan, pieces)
+    return pl.pallas_call(
+        functools.partial(project_kernel, plan),
+        out_shape=(
+            sds((rows, D), bf16), sds((rows, 128), bf16), sds((rows, 2 * D), bf16), sds((rows, 2 * D), bf16),
+            sds((rows, D), bf16), sds((rows, D), f32), sds((rows, 128), bf16), sds((rows, 128), bf16),
+            sds((128, D), bf16), *full,
+        ),
+        grid=(12,),
+        in_specs=[
+            small(x), small(gain), small(inner), small(got_model),
+            pl.BlockSpec((D, 512), lambda j: (0, block(j))),
+            small(w_forget), small(forget_sel), small(bias),
+        ]
+        + shard_specs(pieces),
+        out_specs=(
+            keep(rows, D), keep(rows, 128), keep(rows, 2 * D), hbm_spec(), keep(rows, D), keep(rows, D),
+            keep(rows, 128), hbm_spec(), keep(128, D),
         )
-        copy.start()
-        own.append(copy)
-
+        + (hbm_spec(),) * len(full),
+        scratch_shapes=mover_scratch(plan) + [dma((7,)), dma((7,))],
+        compiler_params=pltpu.CompilerParams(collective_id=3, has_side_effects=True),
+        name="project",
+    )(x, gain, inner, got_model, w_mix, w_forget, forget_sel, bias, *(v for v, _, _ in pieces))
+
+
+def paths_kernel_part(forget, forget2, strict, sums):
+    row = lax.broadcasted_iota(jnp.int32, (BLOCK, BLOCK), 0)
+    col = lax.broadcasted_iota(jnp.int32, (BLOCK, BLOCK), 1)
+    lower = (col <= row).astype(f32)
+    within, totals = [], []
+    for m in range(8):
+        ref = forget if m < 4 else forget2
+        logit = ref[(m % 4) * BLOCK : (m % 4 + 1) * BLOCK].astype(f32)
+        value = jnp.minimum(logit, 0.0) - jnp.log(1.0 + jnp.exp(-jnp.abs(logit)))
+        value = jnp.dot(lower, value, precision=highest, preferred_element_type=f32)
+        within.append(value)
+        totals.append(value[BLOCK - 1 :])
+    offsets = jnp.dot(strict[...], jnp.concatenate(totals, axis=0), precision=highest, preferred_element_type=f32)
+    for m in range(8):
+        sums[m] = -(within[m] + offsets[m : m + 1]).T
+
+
+UPS = (2, 3, 6, 7)
+
+
+def key_spots(place, core):
+    if place == 0:
+        return [4, 0]
+    if place == 1:
+        return [4 * core, 4 - 4 * core, 5, 1]
+    return [4 * core, 4 - 4 * core, 5 - 4 * core, 1 + 4 * core, None, place]
+
+
+def block_of(m):
+    return pl.ds(m * BLOCK if isinstance(m, int) else pl.multiple_of(m * BLOCK, BLOCK), BLOCK)
+
+
+def key_block(buf, spot, ups, place):
+    if spot is not None:
+        return buf[block_of(spot), :]
+    total = None
+    for i, m in enumerate(UPS):
+        line = ups[4 * (place - 2) + i : 4 * (place - 2) + i + 1, :].astype(buf.dtype)
+        part = buf[block_of(m), :] * line
+        total = part if total is None else total + part
+    return total
+
+
+def path_line(sums, spot, head, ups, place):
+    if spot is not None:
+        return sums[spot, pl.ds(head, 1), :]
+    total = None
+    for i, m in enumerate(UPS):
+        part = sums[m, pl.ds(head, 1), :] * ups[4 * (place - 2) + i : 4 * (place - 2) + i + 1, :]
+        total = part if total is None else total + part
+    return total
+
+
+def attend_move_kernel(plan, ups, closed, q_ref, k_ref, v_ref, k2_ref, v2_ref, gate_ref, forget, forget2, strict, cot,
+                       *refs):
+    shards, outputs, full, sems, rest = split_refs(plan, refs, 4, 5)
+    o_ref, gated_ref, p_ref, dy_o = outputs
+    kbuf, vbuf, sums, row_send, row_recv = rest
+    me, z = lax.axis_index("dp"), lax.axis_index("seq")
+    core = me & 1
+    step = pl.program_id(0)
+    mover = Mover(plan, shards, full, sems)
+    polls = mover.polls(PAIRS)
+
+    @pl.when(step == 0)
+    def _():
+        greet(me, z)
+        mover.run(polls[0])
+        spread_rows(cot, dy_o, row_send, row_recv)
+        paths_kernel_part(forget, forget2, strict, sums)
+
+    half = 4 * BLOCK
+    kbuf[:half] = k_ref[...]
+    kbuf[half:] = k2_ref[...]
+    vbuf[:half] = v_ref[...]
+    vbuf[half:] = v2_ref[...]
+    lane = lax.broadcasted_iota(jnp.int32, (BLOCK, BLOCK), 1)
+    row = lax.broadcasted_iota(jnp.int32, (BLOCK, BLOCK), 0)
+    later = jnp.where(lane > row, f32(-1e30), f32(0.0))
+    for place in range(4):
+        count, first = ENTRIES[place], FIRST[place]
+        queries = q_ref[place * BLOCK : (place + 1) * BLOCK, :]
+        spots = key_spots(place, core)
+        keys = jnp.concatenate([key_block(kbuf, s, ups, place) for s in spots], axis=0)
+        values = jnp.concatenate([key_block(vbuf, s, ups, place) for s in spots], axis=0)
+        outs = []
+        for a in range(2):
+            mine = jnp.where((lane < HD) == (a == 0), queries, jnp.zeros_like(queries))
+            scores = linear_back(mine, keys) * (HD ** (-0.5))
+            bias = [
+                path_line(sums, s, 2 * step + a, ups, place) + closed[first + e : first + e + 1, :]
+                for e, s in enumerate(spots)
+            ]
+            scores = scores + jnp.concatenate(bias, axis=1)
+            scores = jnp.concatenate(
+                [scores[:, : (count - 1) * BLOCK], scores[:, (count - 1) * BLOCK :] + later], axis=1
+            )
+            peak = jnp.max(scores, axis=1, keepdims=True)
+            expo = jnp.exp(scores - peak)
+            total = jnp.sum(expo, axis=1, keepdims=True)
+            probs = (expo * (1.0 / total)).astype(bf16)
+            p_ref[a, :, first * BLOCK : (first + count) * BLOCK] = probs
+            outs.append(linear(probs, values))
+        span = slice(place * BLOCK, (place + 1) * BLOCK)
+        attended = jnp.where(lane < HD, outs[0], outs[1])
+        o_ref[span, :] = attended
+        gated_ref[span, :] = (attended * jax.nn.sigmoid(gate_ref[span, :])).astype(bf16)
+
+    for s in range(1, PAIRS):
+        @pl.when(step == s)
+        def _():
+            mover.run(polls[s])
+            if s == PAIRS - 1:
+                mover.finish()
+                wait_rows(cot, dy_o, row_send, row_recv)
+
+
+def attend_move(ups, closed, q, kv, kv2, gate, forget, forget2, strict, cot, plan, pieces):
+    rows = pl.BlockSpec((4 * BLOCK, 2 * HD), lambda g: (0, g))
+    upper = pl.BlockSpec((4 * BLOCK, 2 * HD), lambda g: (0, PAIRS + g))
+    small = lambda v: pl.BlockSpec(v.shape, lambda g: (0,) * v.ndim, pipeline_mode=pl.Buffered(1))
+    dma = pltpu.SemaphoreType.DMA
+    sds = jax.ShapeDtypeStruct
+    cot = cot.reshape(2, 2, BLOCK, D)
+    full = full_shapes(plan, pieces)
+    return pl.pallas_call(
+        functools.partial(attend_move_kernel, plan),
+        out_shape=(
+            sds((4 * BLOCK, D), f32), sds((4 * BLOCK, D), bf16), sds((H, BLOCK, TOTAL * BLOCK), bf16),
+            sds((4 * BLOCK, D), bf16), *full,
+        ),
+        grid=(PAIRS,),
+        in_specs=[small(ups), small(closed), rows, rows, upper, rows, upper, rows]
+        + [small(v) for v in (forget, forget2, strict, cot)]
+        + shard_specs(pieces),
+        out_specs=(rows, rows, pl.BlockSpec((2, BLOCK, TOTAL * BLOCK), lambda g: (g, 0, 0)), hbm_spec())
+        + (hbm_spec(),) * len(full),
+        scratch_shapes=mover_scratch(plan)
+        + [pltpu.VMEM((8 * BLOCK, 2 * HD), bf16)] * 2
+        + [pltpu.VMEM((8, BLOCK, BLOCK), f32), dma((4,)), dma((4,))],
+        compiler_params=pltpu.CompilerParams(collective_id=4, has_side_effects=True),
+        name="attend_move",
+    )(ups, closed, q, kv, kv, kv2, kv2, gate, forget, forget2, strict, cot, *(v for v, _, _ in pieces))
+
+
+def middle_kernel(plan, x, gated, dy, gain, inner, model, w_ref, *refs):
+    shards, outputs, full, sems, _ = split_refs(plan, refs, 5, 0)
+    mid_o, norm_o, slow_o, plow_o, hlg_o = outputs
+    me, z = lax.axis_index("dp"), lax.axis_index("seq")
+    step = pl.program_id(0)
+    mover = Mover(plan, shards, full, sems)
+    polls = mover.polls(6)
+
+    for s in range(3):
+        @pl.when(step == s)
+        def _():
+            if s == 0:
+                greet(me, z)
+            mover.run(polls[2 * s])
+
+    @pl.when(step == 0)
+    def _():
+        low = linear(gated[...], inner[...])
+        plow_o[...] = jnp.where(lane_groups(low.shape) == 5, low, 0.0).astype(bf16)
+        low = linear_back(dy[...], model[...])
+        hlg_o[...] = jnp.where(lane_groups(low.shape) == 4, low, 0.0).astype(bf16)
+
+    cols = pl.ds(pl.multiple_of(step * 512, 512), 512)
+    mid_o[:, cols] = x[:, cols].astype(f32) + linear(gated[...], w_ref[...]) + linear(plow_o[...], model[:, cols])
+
+    @pl.when(step == 2)
+    def _():
+        value = mid_o[...]
+        norm = (value * rms_scale(value) * gain[...]).astype(bf16)
+        norm_o[...] = norm
+        low = linear(norm, inner[...])
+        slow_o[...] = jnp.where(lane_groups(low.shape) >= 6, low, 0.0).astype(bf16)
+
+    for s in range(3):
+        @pl.when(step == s)
+        def _():
+            mover.run(polls[2 * s + 1])
+            if s == 2:
+                mover.finish()
+
+
+def middle_step(x, gated, dy, gain, inner, model, w_out, plan, pieces):
+    rows = 4 * BLOCK
+    small = lambda v: pl.BlockSpec(v.shape, lambda j: (0,) * v.ndim, pipeline_mode=pl.Buffered(1))
+    keep = lambda *shape: pl.BlockSpec(shape, lambda j: (0,) * len(shape))
+    sds = jax.ShapeDtypeStruct
+    full = full_shapes(plan, pieces)
+    return pl.pallas_call(
+        functools.partial(middle_kernel, plan),
+        out_shape=(
+            sds((rows, D), f32), sds((rows, D), bf16), sds((rows, 128), bf16), sds((rows, 128), bf16),
+            sds((rows, 128), bf16), *full,
+        ),
+        grid=(3,),
+        in_specs=[small(v) for v in (x, gated, dy, gain, inner, model)]
+        + [pl.BlockSpec((D, 512), lambda j: (0, j))]
+        + shard_specs(pieces),
+        out_specs=(keep(rows, D), keep(rows, D), keep(rows, 128), keep(rows, 128), keep(rows, 128))
+        + (hbm_spec(),) * len(full),
+        scratch_shapes=mover_scratch(plan),
+        compiler_params=pltpu.CompilerParams(collective_id=5, has_side_effects=True),
+        name="middle_step",
+    )(x, gated, dy, gain, inner, model, w_out, *(v for v, _, _ in pieces))
+
+
+def feed_kernel(plan, steps, x_ref, slow, dy_ref, hlg, *refs):
+    g_ref, u_ref, low, dn_a, dn_b = refs[:5]
+    state_in, refs = refs[5:10], refs[10:]
+    step = pl.program_id(0)
+    if plan:
+        shards, outputs, full, sems, _ = split_refs(plan, refs, 6, 0)
+        me, z = lax.axis_index("dp"), lax.axis_index("seq")
+        mover = Mover(plan, shards, full, sems)
+        polls = mover.polls(3 * steps)
+    else:
+        outputs = refs
+    state, pack_ref = outputs[:5], outputs[5]
+    second_ref, down_ref, slg_ref, slu_ref, hl_ref = state
+
+    def poll(part):
+        if plan:
+            for s in range(steps):
+                @pl.when(step == s)
+                def _():
+                    if s == 0 and part == 0:
+                        greet(me, z)
+                    mover.run(polls[3 * s + part])
+                    if s == steps - 1 and part == 2:
+                        mover.finish()
+
+    poll(0)
+
+    @pl.when(step == 0)
+    def _():
+        for ref, old in zip(state, state_in):
+            ref[...] = old[...]
+
+    lowg, lowu, hidden = slow[:, 6 * RANK : 7 * RANK], slow[:, 7 * RANK :], hlg[:, 4 * RANK : 5 * RANK]
+    ah, bg, bu = low[:RANK], low[RANK : 2 * RANK], low[2 * RANK :]
+    edge = dn_a.shape[1]
+    gate = linear(x_ref[...], g_ref[...]) + linear(lowg, bg)
+    up = linear(x_ref[...], u_ref[...]) + linear(lowu, bu)
+    back = linear_back(dy_ref[:, :edge], dn_a[...]) + linear_back(dy_ref[:, edge:], dn_b[...]) + linear(hidden, ah)
+    poll(1)
+    sig = jax.nn.sigmoid(gate)
+    silu = gate * sig
+    activated = (silu * up).astype(bf16)
+    gate_grad = (back * up * (sig * (1.0 + gate * (1.0 - sig)))).astype(bf16)
+    up_grad = (back * silu).astype(bf16)
+    down_ref[:, :edge] += linear(activated, dn_a[...])
+    down_ref[:, edge:] += linear(activated, dn_b[...])
+    hl_ref[...] += linear_back(activated, ah)
+    second_ref[...] += linear_back(gate_grad, g_ref[...]) + linear_back(up_grad, u_ref[...])
+    slg_ref[...] += linear_back(gate_grad, bg)
+    slu_ref[...] += linear_back(up_grad, bu)
+    pack_ref[:RANK] = linear_grad(hidden, activated).astype(bf16)
+    pack_ref[RANK : 2 * RANK] = linear_grad(lowg, gate_grad).astype(bf16)
+    pack_ref[2 * RANK :] = linear_grad(lowu, up_grad).astype(bf16)
+    poll(2)
+
+
+def feed(x, slow, dy, hlg, weight, low, downs, chunk, state, plan, pieces, ident):
+    rows = 4 * BLOCK
+    steps, width = 2, 512
+    small = lambda v: pl.BlockSpec(v.shape, lambda j: (0,) * v.ndim, pipeline_mode=pl.Buffered(1))
+    keep = lambda v: pl.BlockSpec(v.shape, lambda j: (0,) * v.ndim)
+    owned = pl.BlockSpec((None, 3 * RANK, width), lambda j: (2 * chunk + j, 0, 0))
+    down = lambda v: pl.BlockSpec((width, v.shape[1]), lambda j: (2 * chunk + j, 0))
+    params = {}
+    if plan:
+        params["compiler_params"] = pltpu.CompilerParams(collective_id=ident, has_side_effects=True)
+    full = full_shapes(plan, pieces)
+    return pl.pallas_call(
+        functools.partial(feed_kernel, plan, steps),
+        out_shape=tuple(jax.ShapeDtypeStruct(v.shape, v.dtype) for v in state)
+        + (jax.ShapeDtypeStruct((steps, 3 * RANK, width), bf16),)
+        + full,
+        grid=(steps,),
+        in_specs=[small(v) for v in (x, slow, dy, hlg)]
+        + [
+            pl.BlockSpec((D, width), lambda j: (0, j)),
+            pl.BlockSpec((D, width), lambda j: (0, 2 + j)),
+            owned,
+            down(downs[0]),
+            down(downs[1]),
+        ]
+        + [small(v) for v in state]
+        + shard_specs(pieces),
+        out_specs=tuple(keep(v) for v in state)
+        + (pl.BlockSpec((None, 3 * RANK, width), lambda j: (j, 0, 0)),)
+        + (hbm_spec(),) * len(full),
+        scratch_shapes=mover_scratch(plan) if plan else [],
+        name="feed",
+        **params,
+    )(x, slow, dy, hlg, weight, weight, low, *downs, *state, *(v for v, _, _ in pieces))
+
+
+def attend_return_kernel(
+    ups, q_ref, k_ref, v_ref, k2_ref, v2_ref, g_ref, o_ref, p_ref,
+    dq_ref, dk_ref, dv_ref, qsum_ref, ksum_ref, kbuf, vbuf, dkbuf, dvbuf,
+):
+    core = lax.axis_index("dp") & 1
+    half = 4 * BLOCK
+    pair = pl.program_id(0)
+    kbuf[:half] = k_ref[...]
+    kbuf[half:] = k2_ref[...]
+    vbuf[:half] = v_ref[...]
+    vbuf[half:] = v2_ref[...]
+    dkbuf[...] = jnp.zeros_like(dkbuf)
+    dvbuf[...] = jnp.zeros_like(dvbuf)
+
+    @pl.when(pair == 0)
+    def _():
+        qsum_ref[...] = jnp.zeros_like(qsum_ref)
+        ksum_ref[...] = jnp.zeros_like(ksum_ref)
+
+    lane = lax.broadcasted_iota(jnp.int32, (BLOCK, BLOCK), 1)
+    scale = HD ** (-0.5)
+    for place in range(4):
+        count, first = ENTRIES[place], FIRST[place]
+        span = slice(place * BLOCK, (place + 1) * BLOCK)
+        queries = q_ref[span, :]
+        grads = g_ref[span, :]
+        product = grads.astype(f32) * o_ref[span, :]
+        spots = key_spots(place, core)
+        keys = jnp.concatenate([key_block(kbuf, s, ups, place) for s in spots], axis=0)
+        values = jnp.concatenate([key_block(vbuf, s, ups, place) for s in spots], axis=0)
+        dqs, dks, dvs = [], [], []
+        row_sums = qsum_ref[span, :]
+        for a in range(2):
+            own = (lane < HD) == (a == 0)
+            dot_row = jnp.sum(jnp.where(own, product, 0.0), axis=1, keepdims=True)
+            mine = jnp.where(own, grads, jnp.zeros_like(grads))
+            probs = p_ref[a, :, first * BLOCK : (first + count) * BLOCK]
+            prob_grad = linear_back(mine, values)
+            score_grad = (probs.astype(f32) * (prob_grad - dot_row)).astype(bf16)
+            wide = score_grad.astype(f32)
+            col = jnp.sum(wide, axis=0, keepdims=True)
+            head = pl.ds(2 * pair + a, 1)
+            for e, spot in enumerate(spots):
+                part = col[:, e * BLOCK : (e + 1) * BLOCK]
+                if spot is not None:
+                    ksum_ref[spot, head, :] += part
+                else:
+                    for i, m in enumerate(UPS):
+                        ksum_ref[m, head, :] += part * ups[4 * (place - 2) + i : 4 * (place - 2) + i + 1, :]
+            row_sums = row_sums + jnp.where(lane == 2 * pair + a, jnp.sum(wide, axis=1, keepdims=True), 0.0)
+            dqs.append(linear(score_grad, keys))
+            dks.append(linear_grad(score_grad, queries))
+            dvs.append(linear_grad(probs, grads))
+        qsum_ref[span, :] = row_sums
+        dq_ref[span, :] = (jnp.where(lane < HD, dqs[0], dqs[1]) * scale).astype(bf16)
+        for e, spot in enumerate(spots):
+            part = slice(e * BLOCK, (e + 1) * BLOCK)
+            dk_part = jnp.where(lane < HD, dks[0][part], dks[1][part])
+            dv_part = jnp.where(lane < HD, dvs[0][part], dvs[1][part])
+            if spot is not None:
+                dkbuf[block_of(spot), :] += dk_part
+                dvbuf[block_of(spot), :] += dv_part
+            else:
+                for i, m in enumerate(UPS):
+                    line = ups[4 * (place - 2) + i : 4 * (place - 2) + i + 1, :]
+                    dkbuf[block_of(m), :] += dk_part * line
+                    dvbuf[block_of(m), :] += dv_part * line
+    dk_ref[...] = (dkbuf[...] * scale).astype(bf16)
+    dv_ref[...] = dvbuf[...].astype(bf16)
+
+
+def attend_return(ups, queries, kv, kv2, grads, attended, probs):
+    rows = pl.BlockSpec((4 * BLOCK, 2 * HD), lambda g: (0, g))
+    upper = pl.BlockSpec((4 * BLOCK, 2 * HD), lambda g: (0, PAIRS + g))
+    full = pl.BlockSpec((8 * BLOCK, 2 * HD), lambda g: (0, g))
+    sds = jax.ShapeDtypeStruct
+    return pl.pallas_call(
+        attend_return_kernel,
+        out_shape=(
+            sds((4 * BLOCK, D), bf16), sds((8 * BLOCK, D), bf16), sds((8 * BLOCK, D), bf16),
+            sds((4 * BLOCK, BLOCK), f32), sds((8, BLOCK, BLOCK), f32),
+        ),
+        grid=(PAIRS,),
+        in_specs=[
+            pl.BlockSpec(ups.shape, lambda g: (0, 0)), rows, rows, upper, rows, upper, rows, rows,
+            pl.BlockSpec((2, BLOCK, TOTAL * BLOCK), lambda g: (g, 0, 0)),
+        ],
+        out_specs=(
+            rows, full, full, pl.BlockSpec((4 * BLOCK, BLOCK), lambda g: (0, 0)),
+            pl.BlockSpec((8, BLOCK, BLOCK), lambda g: (0, 0, 0)),
+        ),
+        scratch_shapes=[pltpu.VMEM((8 * BLOCK, 2 * HD), bf16)] * 2 + [pltpu.VMEM((8 * BLOCK, 2 * HD), f32)] * 2,
+        cost_estimate=pl.CostEstimate(flops=16_000_000_000, bytes_accessed=35_000_000, transcendentals=0),
+        name="attend_return",
+    )(ups, queries, kv, kv, kv2, kv2, grads, attended, probs)
+
+
+def turn_kernel(
+    qsum, ksum, logit, strict, dq, dg, dk, dv, dk2, dv2, w_ref, e_ref, low_ref, a_in, w_forget, forget_sel,
+    x_ref, gain, mgrad, ff, early,
+    dx_home, ff_trees, early_trees, late_trees,
+    grads, acc, lows, path, path2, got_k, got_v, dx, pack, late, ff_got, early_got, late_got,
+    ff_sum, early_sum, late_sum, csend, crecv, asend, arecv, zsend, zrecv, xsend, xrecv,
+):
+    me, z = lax.axis_index("dp"), lax.axis_index("seq")
+    core, odd, tree_core = me & 1, z & 1, z >> 1
+    step = pl.program_id(0)
+    rows = 4 * BLOCK
     partner = (me ^ 1, z)
-    above = (me, z ^ 1)
-    state = {}
-
-    def piece(i, owner, start, length):
-        index, first, width = chunks[i]
-        count = sources[index].shape[0]
-        return targets[index].at[
-            pl.ds(pl.multiple_of(owner * count + start, 16), length), pl.ds(first, width)
+
+    swaps = [
+        remote(src, dst, csend.at[i], crecv.at[i], partner)
+        for i, (src, dst) in enumerate(((path, path2), (dk2, got_k), (dv2, got_v)))
+    ]
+    packs = ((ff, ff_got, ff_sum, ff_trees), (early, early_got, early_sum, early_trees), (late, late_got, late_sum, late_trees))
+
+    def owners(kind):
+        src, dst = packs[kind][:2]
+        return [
+            remote(src.at[me ^ m], dst.at[me], asend.at[kind, m], arecv.at[kind, m], (me ^ m, z)) for m in range(1, 8)
         ]
 
-    def go(i, slot, src, dst, to):
-        state[i, slot] = remote(src, dst, send.at[i, slot], recv.at[i, slot], to)
-
-    def shape_of(i):
-        index, first, width = chunks[i]
-        count = sources[index].shape[0]
-        shared = shared_rows(count)
-        return count, shared, shared * odd, count - shared
-
-    def pass_on(i, slot, owner, start, length, target):
-        ref = piece(i, owner, start, length)
-        go(i, slot, ref, ref, target)
-
-    total = len(chunks)
-    for i in range(total + 3):
-        if i < total:
-            index, first, width = chunks[i]
-            count, shared, low, length = shape_of(i)
-            src = sources[index].at[pl.ds(pl.multiple_of(low, 16), length), pl.ds(first, width)]
-            go(i, 0, src, piece(i, me, low, length), (first_to, z))
-            go(i, 1, src, piece(i, me, low, length), (second_to, z))
-            go(i, 6, sources[index].at[:, pl.ds(first, width)], piece(i, me, 0, count), partner)
-        k = i - 1
-        if 0 <= k < total:
-            count, shared, low, length = shape_of(k)
-            state[k, 0].wait_recv()
-            pass_on(k, 2, first_to, low, length, (second_to, z))
-            pass_on(k, 7, first_to, low, length, partner)
-            pass_on(k, 3, first_to, odd * (count - shared), shared, above)
-            state[k, 1].wait_recv()
-            pass_on(k, 8, second_to, low, length, partner)
-            pass_on(k, 4, second_to, odd * (count - shared), shared, above)
-        k = i - 2
-        if 0 <= k < total:
-            count, shared, low, length = shape_of(k)
-            state[k, 2].wait_recv()
-            pass_on(k, 9, me ^ 6, low, length, partner)
-            pass_on(k, 5, me ^ 6, odd * (count - shared), shared, above)
-        k = i - 3
-        if 0 <= k < total:
-            count, shared, low, length = shape_of(k)
-            for n, owner in enumerate((first_to, second_to, me ^ 6)):
-                state[k, 3 + n].wait_recv()
-                pass_on(k, 10 + n, owner, (1 - odd) * (count - shared), shared, partner)
-    for i in range(total):
-        for slot in range(6, 13):
-            state[i, slot].wait_recv()
-    for copy in done:
-        copy.wait_send()
-    for kind in range(3):
-        for m in range(7):
-            done[kind * 7 + m].wait_recv()
-    for copy in own + small:
-        copy.wait()
-    for self_copy, near, far in rows:
-        @pl.when(self_copy)
-        def _(near=near):
-            near.wait()
-
-        @pl.when(jnp.logical_not(self_copy))
-        def _(far=far):
-            far.wait_send()
-
-    for kind, dst in enumerate((x_o, dy_o)):
+    def planes(kind):
+        src, dst = packs[kind][2:]
+        return [remote(src, dst.at[k], zsend.at[kind, k], zrecv.at[kind, k], (me, z ^ k)) for k in (1, 2, 3)]
+
+    def own_copy(kind):
+        src, dst = packs[kind][2:]
+        return pltpu.make_async_copy(src, dst.at[0], zsend.at[kind, 0])
+
+    def send_to_owners(kind):
+        for copy in owners(kind):
+            copy.start()
+
+    def sum_and_send(kind):
+        src, got, total = packs[kind][:3]
+        got[me] = src[me]
+        for copy in owners(kind):
+            copy.wait()
+        for q in range(4):
+            total[q] = (got[2 * q].astype(f32) + got[2 * q + 1].astype(f32)).astype(bf16)
+        for copy in planes(kind) + [own_copy(kind)]:
+            copy.start()
+
+    lane = lax.broadcasted_iota(jnp.int32, (rows, 128), 1)
+    low16 = lambda value, source, target: jnp.where(
+        lane // RANK == target, pltpu.roll(value, (target - source) * RANK % 128, 1), jnp.zeros_like(value)
+    )
+
+    @pl.when(step == 0)
+    def _():
+        greet(me, z)
+        swaps[1].start()
+        swaps[2].start()
+        send_to_owners(0)
+        send_to_owners(1)
+        for m in range(8):
+            sums = ksum[m].T
+            part = slice(m * BLOCK, (m + 1) * BLOCK)
+            path[part] = qsum[part] - sums if m < 4 else -sums
+        swaps[0].start()
+        grads[:, :D] = dq[...]
+        grads[:, 3 * D :] = dg[...]
+        acc[...] = jnp.zeros_like(acc)
+        lows[...] = jnp.zeros_like(lows)
+        pack[...] = jnp.zeros_like(pack)
+
+    @pl.when(step == 3)
+    def _():
+        sum_and_send(0)
+
+    @pl.when(step == 4)
+    def _():
+        sum_and_send(1)
+
+    @pl.when(step == 6)
+    def _():
+        swaps[1].wait()
+        swaps[2].wait()
+        grads[:, D : 2 * D] = (dk[...].astype(f32) + got_k[...].astype(f32)).astype(bf16)
+        grads[:, 2 * D : 3 * D] = (dv[...].astype(f32) + got_v[...].astype(f32)).astype(bf16)
+
+    place = jnp.where(step < 3, step, jnp.where(step < 6, step + 6, step - 3))
+    now = grads[:, pl.ds(pl.multiple_of(place * 512, 512), 512)]
+    acc[...] += linear_back(now, w_ref[...])
+    group = place // 3
+    extra = e_ref[...]
+    lows[...] += linear_back(now, jnp.where(row_groups(extra.shape) == group, extra, jnp.zeros_like(extra)))
+    low = low_ref[...]
+    moved = jnp.where(
+        group == 0, low16(low, 0, 4), jnp.where(group == 1, low16(low, 1, 5), low16(low, 2, 6))
+    )
+
+    @pl.when(group < 3)
+    def _():
+        spot = pl.ds(pl.multiple_of((place - 3 * group) * 512, 512), 512)
+        pack[spot, :] += linear_grad(now, moved)
+
+    @pl.when(step == 11)
+    def _():
+        swaps[0].wait()
+        row = lax.broadcasted_iota(jnp.int32, (BLOCK, BLOCK), 0)
+        col = lax.broadcasted_iota(jnp.int32, (BLOCK, BLOCK), 1)
+        upper = (row <= col).astype(f32)
+        totals = []
+        full = []
+        for m in range(8):
+            theirs = (m + 4) % 8
+            value = path[m * BLOCK : (m + 1) * BLOCK] + path2[theirs * BLOCK : (theirs + 1) * BLOCK]
+            full.append(value)
+            totals.append(jnp.sum(value, axis=0, keepdims=True))
+        below = lax.dot_general(
+            strict[...], jnp.concatenate(totals, axis=0), (((0,), (0,)), ((), ())), precision=highest,
+            preferred_element_type=f32,
+        )
+        suffix = jnp.concatenate(
+            [jnp.dot(upper, full[m], precision=highest, preferred_element_type=f32) + below[m : m + 1] for m in range(4)],
+            axis=0,
+        )
+        forget_low = (suffix * jax.nn.sigmoid(-logit[...].astype(f32))).astype(bf16)
+        inner_f = linear_back(forget_low, forget_sel[...])
+        ilg = jnp.where(lane < 4 * RANK, lows[...], pltpu.roll(inner_f, 4 * RANK, 1)).astype(bf16)
+        first_grad = acc[...] + linear_back(ilg, a_in[...]) + linear_back(forget_low, w_forget[...])
+        inputs = x_ref[...].astype(f32)
+        scale_rows = rms_scale(inputs)
+        unit = inputs * scale_rows
+        up = first_grad * gain[...]
+        back = scale_rows * (up - unit * jnp.mean(up * unit, axis=-1, keepdims=True))
+        dx[...] = (mgrad[...] + back).astype(bf16)
+        sends = []
         for p in range(4):
-            from_me = (p == z) & (core == tree_core)
-            arrived = pltpu.make_async_remote_copy(
-                src_ref=tok.at[0, 0],
-                dst_ref=dst.at[pl.ds(p * BLOCK, BLOCK)],
-                send_sem=row_send.at[kind, p],
-                recv_sem=row_recv.at[kind, p],
-                device_id=(me ^ 1, z),
-                device_id_type=MESH,
+            to = ((me & ~1) | tree_core, p)
+            b = core ^ (p & 1)
+            self_copy = (to[0] == me) & (p == z)
+            src = dx.at[pl.ds(p * BLOCK, BLOCK)]
+            dst = dx_home.at[odd, b]
+            far = remote(src, dst, xsend.at[p], xrecv.at[2 * odd + b], to)
+            near = pltpu.make_async_copy(src, dst, xsend.at[p])
+            sends.append((self_copy, near, far))
+        first_norm = (unit * gain[...]).astype(bf16)
+        keep = jnp.where(lane < 3 * RANK, ilg, low16(ilg, 4, 3))
+        body = pack[...] + linear_grad(first_norm, keep)
+        forget_piece = linear_grad(forget_low, low16(low_ref[...], 4, 7))
+        for d in range(8):
+            part = body[d * 192 : (d + 1) * 192]
+            late[d] = part.astype(bf16)
+            late[d, :32] = (part[:32] + forget_piece[:32]).astype(bf16)
+        for self_copy, near, far in sends:
+            @pl.when(self_copy)
+            def _(near=near):
+                near.start()
+
+            @pl.when(jnp.logical_not(self_copy))
+            def _(far=far):
+                far.start()
+
+        send_to_owners(2)
+        sum_and_send(2)
+        for kind in range(3):
+            own_copy(kind).wait()
+            for copy in planes(kind):
+                copy.wait()
+        for self_copy, near, far in sends:
+            @pl.when(self_copy)
+            def _(near=near):
+                near.wait()
+
+            @pl.when(jnp.logical_not(self_copy))
+            def _(far=far):
+                far.wait_send()
+
+        for j in range(2):
+            for b in range(2):
+                from_me = ((b ^ odd) == core) & (2 * core + j == z)
+                arrived = remote(
+                    dx.at[pl.ds(0, BLOCK)], dx_home.at[j, b], xsend.at[2 * j + b], xrecv.at[2 * j + b], partner
+                )
+
+                @pl.when(jnp.logical_not(from_me))
+                def _(arrived=arrived):
+                    arrived.wait_recv()
+
+
+def turn(qsum, ksum, logit, strict, dq, dg, dk_all, dv_all, weight, extra, low, a_in, w_forget, forget_sel, x, gain, mgrad, ff, early):
+    rows = 4 * BLOCK
+    block = lambda j: jnp.where(j < 3, j, jnp.where(j < 6, j + 6, j - 3))
+    one = lambda v: pl.BlockSpec(v.shape, lambda j: (0,) * v.ndim, pipeline_mode=pl.Buffered(1))
+    top = pl.BlockSpec((rows, D), lambda j: (0, 0), pipeline_mode=pl.Buffered(1))
+    bottom = pl.BlockSpec((rows, D), lambda j: (1, 0), pipeline_mode=pl.Buffered(1))
+    hbm = pl.BlockSpec(memory_space=pl.ANY)
+    dma = pltpu.SemaphoreType.DMA
+    vm = pltpu.VMEM
+    trees = lambda v: (4,) + v.shape[1:]
+    late_shape = (8, D // 8, 128)
+    return pl.pallas_call(
+        turn_kernel,
+        out_shape=(
+            jax.ShapeDtypeStruct((2, 2, BLOCK, D), bf16),
+            jax.ShapeDtypeStruct((4,) + trees(ff), bf16),
+            jax.ShapeDtypeStruct((4,) + trees(early), bf16),
+            jax.ShapeDtypeStruct((4, 4) + late_shape[1:], bf16),
+        ),
+        grid=(12,),
+        in_specs=[one(v) for v in (qsum, ksum, logit, strict, dq, dg)]
+        + [top, top, bottom, bottom]
+        + [
+            pl.BlockSpec((D, 512), lambda j: (0, block(j))),
+            pl.BlockSpec((128, 512), lambda j: (0, j % 3)),
+        ]
+        + [one(v) for v in (low, a_in, w_forget, forget_sel, x, gain, mgrad, ff, early)],
+        out_specs=(hbm,) * 4,
+        scratch_shapes=[
+            vm((rows, 4 * D), bf16),
+            vm((rows, D), f32),
+            vm((rows, 128), f32),
+            vm((2 * rows, 128), f32),
+            vm((2 * rows, 128), f32),
+            vm((rows, D), bf16),
+            vm((rows, D), bf16),
+            vm((rows, D), bf16),
+            vm((D, 128), f32),
+            vm(late_shape, bf16),
+            vm(ff.shape, bf16),
+            vm(early.shape, bf16),
+            vm(late_shape, bf16),
+            vm(trees(ff), bf16),
+            vm(trees(early), bf16),
+            vm((4,) + late_shape[1:], bf16),
+            dma((3,)),
+            dma((3,)),
+            dma((3, 8)),
+            dma((3, 8)),
+            dma((3, 4)),
+            dma((3, 4)),
+            dma((4,)),
+            dma((4,)),
+        ],
+        compiler_params=pltpu.CompilerParams(collective_id=2, has_side_effects=True),
+        name="turn",
+    )(
+        qsum, ksum, logit, strict, dq, dg, dk_all, dv_all, dk_all, dv_all, weight, extra, low, a_in, w_forget,
+        forget_sel, x, gain, mgrad, ff, early,
+    )
+
+
+def body_paired(
+    tokens,
+    cotangent,
+    parents,
+    adapter_ids,
+    attention_gain,
+    mixer_weight,
+    forget_weight,
+    forget_bias,
+    output_weight,
+    feedforward_gain,
+    swiglu_weight,
+    down_weight,
+    adapter_inner,
+    adapter_hidden,
+    adapter_model,
+    adapter_project,
+    adapter_swiglu,
+    adapter_forget,
+):
+    dp = 8
+    me = lax.axis_index("dp")
+    z = lax.axis_index("seq")
+    core = me & 1
+    tree_core, tree_slot = z >> 1, z & 1
+    rows = 4 * BLOCK
+    wide, tall = D // dp, FF // dp
+    part = tall // 4
+
+    def collect(value):
+        cut = value.reshape(4, BLOCK, D)
+        got = []
+        for step in range(4):
+            high, low = step >> 1, step & 1
+            pairs = []
+            for d in range(dp):
+                for s in range(4):
+                    target = ((d & ~1) | (low ^ (s & 1))) * 4 + 2 * (d & 1) + (high ^ (s >> 1))
+                    pairs.append((target, d * 4 + s))
+            piece = lax.dynamic_index_in_dim(cut, step ^ (2 * tree_slot + core), 0, keepdims=False)
+            got.append(lax.ppermute(piece, ("dp", "seq"), pairs))
+        stacked = jnp.stack(got).reshape(2, 2 * BLOCK, D)
+        return jnp.stack([lax.dynamic_index_in_dim(stacked, t ^ (z >> 1), 0, keepdims=False) for t in range(2)])
+
+    facts = jnp.concatenate([parents, adapter_ids[:, None]], axis=1)
+    facts, forget_all = share_facts(
+        jnp.pad(facts, ((0, 6), (0, 128 - 9))), jnp.pad(adapter_forget, ((0, 0), (0, EXTRA - H)))
+    )
+    facts = facts[:, :2, :9].reshape(2 * dp, 9)
+    all_ids = facts[:, 8]
+    tree = 2 * ((me & ~1) | tree_core) + tree_slot
+    parent_row = lax.dynamic_index_in_dim(facts, tree, 0, keepdims=False)[:8]
+    which = lax.dynamic_index_in_dim(all_ids, tree, 0, keepdims=False)
+    forget_sel = lax.dynamic_index_in_dim(forget_all, which, 0, keepdims=False)
+
+    def to_trees(value):
+        sent = []
+        for d in range(dp):
+            chosen = lax.dynamic_index_in_dim(
+                all_ids, 2 * ((d & ~1) | tree_core) + tree_slot, 0, keepdims=False
             )
-
-            @pl.when(jnp.logical_not(from_me))
-            def _(arrived=arrived):
-                arrived.wait_recv()
-
-
-def gather_all(tokens, cotangent, inner, model, ffp, mix, fg, out, dn, sw):
-    chunks = column_chunks(((4 * D, 1024), (EXTRA, EXTRA), (D, D), (D, 512), (2 * FF, 1024)))
-    vmem = pl.BlockSpec(memory_space=pltpu.VMEM)
-    hbm = pl.BlockSpec(memory_space=pl.ANY)
-    args = (tokens.reshape(2, 2, BLOCK, D), cotangent.reshape(2, 2, BLOCK, D), inner, model, ffp, mix, fg, out, dn, sw)
-    n = len(chunks)
-    shapes = [jax.ShapeDtypeStruct((4 * BLOCK, D), bf16)] * 2
-    shapes += [jax.ShapeDtypeStruct(v.shape, bf16) for v in (inner, model, ffp)]
-    shapes += [jax.ShapeDtypeStruct((8 * v.shape[0], v.shape[1]), bf16) for v in (mix, fg, out, dn, sw)]
-    dma = pltpu.SemaphoreType.DMA
-    return pl.pallas_call(
-        functools.partial(gather_kernel, chunks),
-        out_shape=tuple(shapes),
-        in_specs=[vmem] * len(args),
-        out_specs=(hbm,) * len(shapes),
-        scratch_shapes=[dma((n, 13)), dma((n, 13)), dma((n,)), dma((3, 8)), dma((3, 8)), dma((2, 4)), dma((2, 4))],
-        compiler_params=pltpu.CompilerParams(collective_id=1, has_side_effects=True),
-        name="gather_all",
-    )(*args)
-
-
-def body(
+            sent.append(lax.dynamic_index_in_dim(value, chosen, 0, keepdims=False))
+        return jnp.stack(sent)
+
+    own_inner = to_trees(adapter_inner)
+    own_model = to_trees(jnp.concatenate([adapter_model, adapter_project], axis=1))
+    own_ff = to_trees(jnp.concatenate([jnp.swapaxes(adapter_hidden, 1, 2), adapter_swiglu], axis=1))
+    padded_forget = jnp.pad(forget_weight, ((0, 0), (0, EXTRA - H)))
+    x, got_inner, got_model, got_ff, w_mix, w_forget = first(
+        tokens, own_inner, own_model, own_ff, mixer_weight, padded_forget
+    )
+    inner_sel = got_inner.reshape(D, 8 * RANK)
+    forget_low = jnp.pad(forget_sel, ((4 * RANK, 128 - 5 * RANK), (0, 0)))
+    forget_top = jnp.pad(forget_sel, ((0, 128 - RANK), (0, 0)))
+    bias = jnp.pad(forget_bias, (0, EXTRA - H))[None]
+    halves = lambda j: ((swiglu_weight, j, 1024), (swiglu_weight, 4 + j, 1024))
+
+    first_norm, low, kv, kv2, queries, gate_logit, forget, forget2, model_sel, w_out, down_a = project(
+        x, attention_gain[None], inner_sel, got_model, w_mix, w_forget, forget_low, bias,
+        ((0, 0, D, 512, 64), (1, 0, 512, 512, 176)), ((output_weight, 0, D), (down_weight, 0, 512)),
+    )
+
+    table = jnp.array([[0, 3, 4, 7], [1, 2, 5, 6]], dtype=jnp.int32)
+    ids = jnp.where(core == 0, table.reshape(8), table[::-1].reshape(8))
+    parent_of = jnp.sum(jnp.where(ids[:, None] == jnp.arange(8)[None, :], parent_row[None, :], 0), axis=1)
+    a, b = ids[:, None], ids[None, :]
+    linked = (a >= 4) & (b >= 4) & (parent_of[:, None] == b)
+    strict_local = (((b < 4) & (b < a)) | linked).astype(f32)
+    up = jnp.concatenate([linked[2, 2:4], linked[2, 6:8], linked[3, 2:4], linked[3, 6:8]]).astype(f32)
+    ups = jnp.broadcast_to(up[:, None], (8, BLOCK))
+    entry = jnp.arange(24)
+    no_up = jnp.where(entry < 12, jnp.sum(up[:4]), jnp.sum(up[4:])) < 0.5
+    shut = (
+        ((entry == 0) & (core == 0)) | ((entry == 4) & (core == 1)) | (((entry == 10) | (entry == 16)) & no_up)
+    )
+    closed = jnp.broadcast_to(jnp.where(shut, -1e30, 0.0).astype(f32)[:, None], (24, BLOCK))
+
+    attended, gated, probs, dy, down_b, w_sw0 = attend_move(
+        ups, closed, queries, kv, kv2, gate_logit, forget, forget2, strict_local, cotangent,
+        ((0, 0, 512, 512, 64), (0, 512, 512, 512, 64), (1, 0, 1024, 512, 32), (1, 1024, 1024, 512, 32)),
+        ((down_weight, 1, 512), (down_weight, 2, 512)) + halves(0),
+    )
+    both = ((0, 0, 1024, 512, 64), (0, 1024, 1024, 512, 64))
+    middle, second_norm, slow, plow, hlg, w_sw1 = middle_step(
+        x, gated, dy, feedforward_gain[None], inner_sel, model_sel, w_out, both, halves(1)
+    )
+    zeros = lambda n: jnp.zeros((rows, n), f32)
+    state = (zeros(D), zeros(D), zeros(RANK), zeros(RANK), zeros(RANK))
+    go = lambda w, j, st, plan, pieces, ident: feed(
+        second_norm, slow, dy, hlg, w, got_ff, (down_a, down_b), j, st, plan, pieces, ident
+    )
+    *state, pack0, w_sw2 = go(w_sw0, 0, state, both, halves(2), 6)
+    *state, pack1, w_sw3 = go(w_sw1, 1, state, both, halves(3), 7)
+    *state, pack2 = go(w_sw2, 2, state, (), (), None)
+    *state, pack3 = go(w_sw3, 3, state, (), (), None)
+    second_out, down_out, slg, slu, hidden_low = state
+
+    a_in = jnp.where(jnp.arange(128)[None, :] < 5 * RANK, inner_sel, 0).astype(bf16)
+    a_project = inner_sel[:, 5 * RANK : 6 * RANK]
+    a_swiglu = inner_sel[:, 6 * RANK :]
+    b_g, b_down, b_project = (model_sel[i * RANK : (i + 1) * RANK] for i in (3, 4, 5))
+    hidden_low = hidden_low.astype(bf16)
+    result = (middle + down_out + linear(hidden_low, b_down)).astype(bf16)
+
+    swiglu_low_grad = jnp.concatenate([slg, slu], axis=1).astype(bf16)
+    second_grad = second_out + linear_back(swiglu_low_grad, a_swiglu)
+    middle_grad = dy.astype(f32) + norm_back(middle, feedforward_gain, second_grad)
+    branch_grad = middle_grad.astype(bf16)
+    project_low_grad = linear_back(branch_grad, b_project).astype(bf16)
+    gated_grad = backward_mm(
+        branch_grad, w_out, jnp.zeros((EXTRA, D), bf16), 0, 3, 512, linear_back(project_low_grad, a_project), zeros(EXTRA)
+    )[0]
+    gate_open = jax.nn.sigmoid(gate_logit)
+    attended_grad = (gated_grad * gate_open).astype(bf16)
+    gate_logit_grad = (gated_grad * attended * gate_open * (1.0 - gate_open)).astype(bf16)
+
+    attended_grad, result = lax.optimization_barrier((attended_grad, result))
+    outputs = collect(result)
+    dq, dk_all, dv_all, query_sum, key_sum = attend_return(
+        ups, queries, kv, kv2, attended_grad, attended, probs
+    )
+    inner_g_grad = linear_back(gate_logit_grad, b_g).astype(bf16)
+    early = jnp.concatenate(
+        [
+            linear_grad(gated, project_low_grad),
+            linear_grad(second_norm, swiglu_low_grad),
+            linear_grad(first_norm, inner_g_grad),
+            linear_grad(dy, hidden_low),
+            linear_grad(branch_grad, plow[:, 5 * RANK : 6 * RANK]),
+            linear_grad(gate_logit_grad, low[:, 3 * RANK : 4 * RANK]),
+            jnp.zeros((D, RANK), f32),
+        ],
+        axis=1,
+    ).astype(bf16).reshape(dp, wide, 128)
+    ff_pack = jnp.concatenate([pack0, pack1, pack2, pack3], axis=0)
+    early, outputs = lax.optimization_barrier((early, outputs))
+    dx, ff_trees, early_trees, late_trees = turn(
+        query_sum, key_sum, forget, strict_local, dq, gate_logit_grad, dk_all, dv_all,
+        w_mix, model_sel, low, a_in, w_forget, forget_top, x, attention_gain[None], middle_grad, ff_pack, early,
+    )
+    input_grads = dx.reshape(2, 2 * BLOCK, D).astype(f32)
+    ff_trees, early_trees, late_trees = (
+        v.reshape((16,) + v.shape[2:]) for v in (ff_trees, early_trees, late_trees)
+    )
+
+    chip = jnp.arange(dp // 2, dtype=jnp.int32)
+    at = jnp.arange(4, dtype=jnp.int32) ^ z
+    tree_of = 2 * (2 * chip[None, :] + (at >> 1)[:, None]) + (at & 1)[:, None]
+    id_of = all_ids[tree_of.reshape(-1)]
+    one_hot = (jnp.arange(ADAPTERS, dtype=jnp.int32)[:, None] == id_of[None, :]).astype(bf16)
+
+    def by_adapter(value):
+        return jnp.einsum("at,trc->arc", one_hot, value, preferred_element_type=f32)
+
+    ff_sum, early_sum, late_sum = by_adapter(ff_trees), by_adapter(early_trees), by_adapter(late_trees)
+    turned = lambda v: jnp.swapaxes(v, 1, 2)
+    at16 = lambda v, i, n=1: v[:, :, i * RANK : (i + n) * RANK]
+    per = ADAPTERS * RANK // dp
+    forget_sum = turned(at16(late_sum, 7)[:, :H]).reshape(ADAPTERS * RANK, H)
+    return (
+        outputs,
+        input_grads,
+        jnp.concatenate(
+            [at16(late_sum, 0, 3), at16(early_sum, 3), at16(late_sum, 3), at16(early_sum, 0, 3)], axis=2
+        ),
+        turned(ff_sum[:, :RANK]),
+        turned(jnp.concatenate([at16(late_sum, 4, 3), at16(early_sum, 6), at16(early_sum, 4)], axis=2)),
+        turned(at16(early_sum, 5)),
+        ff_sum[:, RANK:],
+        lax.dynamic_slice_in_dim(forget_sum, me * per, per, 0),
+    )
+
+
+def body_plain(
     devices,
     tokens,
     cotangent,
@@ -572,7 +1572,6 @@
     adapter_forget,
 ):
     dp, seq = devices
-    paired = dp == 8
     me = lax.axis_index("dp")
     z = lax.axis_index("seq")
     core = me & 1
@@ -624,13 +1623,8 @@
         return value
 
     facts = jnp.concatenate([parents, adapter_ids[:, None]], axis=1)
-    if paired:
-        facts, forget_all = share_facts(jnp.pad(facts, ((0, 6), (0, 128 - 9))), jnp.pad(adapter_forget, ((0, 0), (0, EXTRA - H))))
-        facts = facts[:, :2, :9].reshape(2 * dp, 9)
-        forget_all = forget_all[:, :, :H].reshape(ADAPTERS * RANK, H)
-    else:
-        facts = gather_small(facts)
-        forget_all = gather_small(adapter_forget)
+    facts = gather_small(facts)
+    forget_all = gather_small(adapter_forget)
     all_ids = facts[:, 8]
     tree = 2 * ((me & ~1) | tree_core) + tree_slot
     parent_row = lax.dynamic_index_in_dim(facts, tree, 0, keepdims=False)[:8]
@@ -649,16 +1643,11 @@
     got_ff = to_trees(jnp.concatenate([jnp.swapaxes(adapter_hidden, 1, 2), adapter_swiglu], axis=1))
     padded_forget = jnp.pad(forget_weight, ((0, 0), (0, EXTRA - H)))
     shards = (mixer_weight, padded_forget, output_weight, down_weight, swiglu_weight)
-    if paired:
-        gathered = gather_all(tokens, cotangent, got_inner, got_model, got_ff, *shards)
-        x, dy, got_inner, got_model, got_ff = gathered[:5]
-        w_mix, w_forget, w_out, w_down, w_swiglu = gathered[5:]
-    else:
-        x, dy = spread(tokens), spread(cotangent)
-        got_inner, got_model, got_ff = (
-            lax.all_to_all(v, "dp", 0, 0, tiled=True) for v in (got_inner, got_model, got_ff)
-        )
-        w_mix, w_forget, w_out, w_down, w_swiglu = (lax.all_gather(v, "dp", axis=0, tiled=True) for v in shards)
+    x, dy = spread(tokens), spread(cotangent)
+    got_inner, got_model, got_ff = (
+        lax.all_to_all(v, "dp", 0, 0, tiled=True) for v in (got_inner, got_model, got_ff)
+    )
+    w_mix, w_forget, w_out, w_down, w_swiglu = (lax.all_gather(v, "dp", axis=0, tiled=True) for v in shards)
     inner_sel = got_inner.reshape(D, 8 * RANK)
     model_sel = jnp.swapaxes(got_model, 0, 1).reshape(6 * RANK, D)
     ff_sel = jnp.swapaxes(got_ff, 0, 1).reshape(3 * RANK, FF)
@@ -768,15 +1757,26 @@
     attended_grad = (gated_grad * gate_open).astype(bf16)
     gate_logit_grad = (gated_grad * attended * gate_open * (1.0 - gate_open)).astype(bf16)
 
-    first_out, first_low = backward_mm(
-        gate_logit_grad, w_mix, extra_mix, 9, 3, 512, jnp.zeros((rows, D), f32), none_low
-    )
     dq, dk_all, dv_all, query_sum, key_sum = attend_back(
         where, queries, keys, values, keys2, values2, attended_grad, attended, probs
     )
+    inner_g_grad = linear_back(gate_logit_grad, b_g).astype(bf16)
+    early = jnp.concatenate(
+        [
+            linear_grad(gated, project_low_grad),
+            linear_grad(second_norm, swiglu_low_grad),
+            linear_grad(first_norm, inner_g_grad),
+            linear_grad(dy, hidden_low),
+            linear_grad(branch_grad, project_low),
+            linear_grad(gate_logit_grad, group(inner_low, 3)),
+            jnp.zeros((D, RANK), f32),
+        ],
+        axis=1,
+    ).astype(bf16).reshape(dp, wide, 128)
+    ff_pack = jnp.swapaxes(ff_pack.reshape(3 * RANK, dp, tall), 0, 1)
     theirs = jnp.concatenate([dk_all[rows:], dv_all[rows:]], axis=1)
     back = swap(theirs, 1)
-    key_sum = jnp.transpose(key_sum, (0, 2, 1, 3)).reshape(H, 8, BLOCK)
+    key_sum = jnp.swapaxes(key_sum, 0, 1)[:H]
     query_part = query_sum[:, :H].T.reshape(H, 4, BLOCK)
     decay = jnp.concatenate([query_part - key_sum[:, :4], -key_sum[:, 4:]], axis=1)
     other = swap(decay, 1)
@@ -785,12 +1785,11 @@
     below = jnp.dot(jnp.sum(decay, axis=2), strict_local[:, :4], precision=highest)
     logf_grad = (suffix + below[:, :, None]).reshape(H, rows).T
     forget_grad_low = (logf_grad * jax.nn.sigmoid(-forget_logit.astype(f32))).astype(bf16)
-
-    first_out, first_low = backward_mm(dq, w_mix, extra_mix, 0, 3, 512, first_out, first_low)
     dk = (dk_all[:rows].astype(f32) + back[:, :D].astype(f32)).astype(bf16)
     dv = (dv_all[:rows].astype(f32) + back[:, D:].astype(f32)).astype(bf16)
     first_out, first_low = backward_mm(
-        jnp.concatenate([dk, dv], axis=1), w_mix, extra_mix, 3, 6, 512, first_out, first_low
+        jnp.concatenate([dq, dk, dv, gate_logit_grad], axis=1), w_mix, extra_mix, 0, 12, 512,
+        jnp.zeros((rows, D), f32), none_low,
     )
     inner_low_grad = jnp.concatenate(
         [first_low[:, : 4 * RANK], linear_back(forget_grad_low, forget_sel)], axis=1
@@ -798,76 +1797,60 @@
     first_grad = first_out + linear_back(inner_low_grad, a_in) + linear_back(pad_low(forget_grad_low), w_forget)
     input_grad = middle_grad + norm_back(inputs, attention_gain, first_grad)
     input_grads = collect(input_grad.astype(bf16)).astype(f32)
-
-    def to_owners(value):
-        taken = lax.all_to_all(value, "dp", 0, 0, tiled=True)
-        trees = jnp.sum(taken.astype(f32).reshape((dp // 2, 2) + value.shape[1:]), axis=1).astype(bf16)
-        if seq != 4:
-            return lax.all_gather(trees, "seq", axis=0, tiled=True)
-        found = [trees]
-        for k in (1, 2, 3):
-            found.append(lax.ppermute(trees, "seq", [(i, i ^ k) for i in range(4)]))
-        return jnp.concatenate(found, axis=0)
-
-    chip = jnp.arange(dp // 2, dtype=jnp.int32)
-    at = jnp.arange(seq, dtype=jnp.int32)
-    if seq == 4:
-        at = at ^ z
-    tree_of = 2 * (2 * chip[None, :] + (at >> 1)[:, None]) + (at & 1)[:, None]
-    id_of = all_ids[tree_of.reshape(-1)]
-    one_hot = (jnp.arange(ADAPTERS, dtype=jnp.int32)[:, None] == id_of[None, :]).astype(bf16)
-
-    def by_adapter(value):
-        return jnp.einsum("at,trc->arc", one_hot, value, preferred_element_type=f32)
-
-    ff_pack = jnp.swapaxes(ff_pack.reshape(3 * RANK, dp, tall), 0, 1)
-    ff_sum = by_adapter(to_owners(ff_pack))
-
-    early_lhs = jnp.concatenate(
-        [
-            linear_grad(gated, project_low_grad),
-            linear_grad(second_norm, swiglu_low_grad),
-            linear_grad(dy, hidden_low),
-            linear_grad(branch_grad, project_low),
-            linear_grad(gate_logit_grad, group(inner_low, 3)),
-        ],
-        axis=1,
-    )
-    early = jnp.pad(early_lhs, ((0, 0), (0, 128 - 6 * RANK))).astype(bf16).reshape(dp, wide, 128)
-    early_sum = by_adapter(to_owners(early))
-
     forget_piece = linear_grad(forget_grad_low, group(inner_low, 4))
-    forget_piece = forget_piece.T
+    forget_slab = jnp.broadcast_to(jnp.pad(forget_piece, ((0, -H % wide), (0, 0)))[None, :wide], (dp, wide, RANK))
     late = jnp.concatenate(
         [
-            linear_grad(first_norm, inner_low_grad),
+            linear_grad(first_norm, inner_low_grad[:, : 3 * RANK]),
+            linear_grad(first_norm, inner_low_grad[:, 4 * RANK :]),
             linear_grad(dq, group(inner_low, 0)),
             linear_grad(dk, group(inner_low, 1)),
             linear_grad(dv, group(inner_low, 2)),
         ],
         axis=1,
-    ).astype(bf16)
-    late_sum = by_adapter(to_owners(late.reshape(dp, wide, 128)))
-    forget_sum = by_adapter(to_owners(jnp.broadcast_to(forget_piece.astype(bf16)[None], (dp, RANK, H))))
-
+    ).reshape(dp, wide, 7 * RANK)
+    late = jnp.concatenate([late, forget_slab], axis=2).astype(bf16)
+
+    def to_owners(value):
+        taken = lax.all_to_all(value, "dp", 0, 0, tiled=True)
+        trees = jnp.sum(taken.astype(f32).reshape((dp // 2, 2) + value.shape[1:]), axis=1).astype(bf16)
+        found = [trees]
+        for k in (1, 2, 3):
+            found.append(lax.ppermute(trees, "seq", [(i, i ^ k) for i in range(4)]))
+        return jnp.concatenate(found, axis=0)
+
+    ff_trees, early_trees, late_trees = to_owners(ff_pack), to_owners(early), to_owners(late)
+
+    chip = jnp.arange(dp // 2, dtype=jnp.int32)
+    at = jnp.arange(seq, dtype=jnp.int32) ^ z
+    tree_of = 2 * (2 * chip[None, :] + (at >> 1)[:, None]) + (at & 1)[:, None]
+    id_of = all_ids[tree_of.reshape(-1)]
+    one_hot = (jnp.arange(ADAPTERS, dtype=jnp.int32)[:, None] == id_of[None, :]).astype(bf16)
+
+    def by_adapter(value):
+        return jnp.einsum("at,trc->arc", one_hot, value, preferred_element_type=f32)
+
+    ff_sum, early_sum, late_sum = by_adapter(ff_trees), by_adapter(early_trees), by_adapter(late_trees)
     turned = lambda v: jnp.swapaxes(v, 1, 2)
-    at16 = lambda v, i: v[:, :, i * RANK : (i + 1) * RANK]
+    at16 = lambda v, i, n=1: v[:, :, i * RANK : (i + n) * RANK]
     per = ADAPTERS * RANK // dp
+    forget_sum = turned(at16(late_sum, 7)[:, :H]).reshape(ADAPTERS * RANK, H)
     return (
         outputs,
         input_grads,
-        jnp.concatenate([late_sum[:, :, : 5 * RANK], early_sum[:, :, : 3 * RANK]], axis=2),
+        jnp.concatenate(
+            [at16(late_sum, 0, 3), at16(early_sum, 3), at16(late_sum, 3), at16(early_sum, 0, 3)], axis=2
+        ),
         turned(ff_sum[:, :RANK]),
-        turned(
-            jnp.concatenate([late_sum[:, :, 5 * RANK :], at16(early_sum, 5), at16(early_sum, 3)], axis=2)
-        ),
-        turned(at16(early_sum, 4)),
+        turned(jnp.concatenate([at16(late_sum, 4, 3), at16(early_sum, 6), at16(early_sum, 4)], axis=2)),
+        turned(at16(early_sum, 5)),
         ff_sum[:, RANK:],
-        lax.dynamic_slice_in_dim(forget_sum.reshape(ADAPTERS * RANK, H), me * per, per, 0),
+        lax.dynamic_slice_in_dim(forget_sum, me * per, per, 0),
     )
 
 
 def solution(mesh):
+    paired = mesh.shape["dp"] == 8 and mesh.shape["seq"] == 4
     placed = (
         P("dp", "seq", None),
         P("dp", "seq", None),
@@ -889,7 +1872,7 @@
         P("dp", None),
     )
     return jax.shard_map(
-        functools.partial(body, (mesh.shape["dp"], mesh.shape["seq"])),
+        body_paired if paired else functools.partial(body_plain, (mesh.shape["dp"], mesh.shape["seq"])),
         mesh=mesh,
         in_specs=placed,
         out_specs=(

time: 745 us -> 675 us (0.906)
  Pallas kernels: 447 us -> 547 us
  starting transfers between devices: 105 us -> 10.5 us
  local copies, waits for them, and re-layouts: 77.1 us -> 40.8 us
  other arithmetic: 46.4 us -> 30.1 us
  waiting for transfers between devices: 10.7 us -> 0.01 us
    pallas_call x8 -> x10, Pallas kernels: 400 us -> 530 us  [the longest x4 123 us: feed(): pl.pallas_call(functools.partial(feed_kernel, plan, steps), out_shape=tup...]
    ppermute x24 -> x4, starting transfers between devices: 86.4 us -> 10.5 us  [collect(): got.append(lax.ppermute(piece, ('dp', 'seq'), pairs))]
    pallas_call x4 -> x1, Pallas kernels: 39.4 us -> 8.85 us  [backward_mm(): pl.pallas_call(backward_kernel, out_shape=(jax.ShapeDtypeStruct((rows, de...]
    all_to_all x4 -> x0, starting transfers between devices: 18.7 us -> none  [to_owners(): taken = lax.all_to_all(value, 'dp', 0, 0, tiled=True)]
    slice x31 -> x6, local copies, waits for them, and re-layouts: 17.3 us -> 3.11 us  [the longest x2 2.26 us: body_paired(): at16 = lambda v, i, n=1: v[:, :, i * RANK:(i + n) * RANK]]
    unnamed x186 -> x95, local copies, waits for them, and re-layouts: 22.3 us -> 9.6 us
    another operation x4 -> x10, local copies, waits for them, and re-layouts: 0.9 us -> 10.5 us
    convert_element_type x9 -> x5, other arithmetic: 18.1 us -> 13.5 us  [the longest x1 6.87 us: body_paired(): attended_grad = (gated_grad * gate_open).astype(bf16)]
  transfers between devices with their start and end apart: 28 -> 4, of which waited for: 5 -> 0; matrix products, arithmetic and copies ran while one was open for 9% -> 3% of each run, Pallas kernels for 6% -> 6%
where the time goes in v2:
time: 675 us; the launch traced here: 663 us
  Pallas kernels  547 us (81%)
  local copies, waits for them, and re-layouts  40.8 us (6%)
  other arithmetic  30.1 us (4%)
  matrix products  23.4 us (3%)
  between operations  11.6 us (2%)
  starting transfers between devices  10.5 us (2%)
    pallas_call x4, Pallas kernels, feed(): pl.pallas_call(functools.partial(feed_kernel, plan, steps), out_shape=tup...  123 us
    pallas_call x1, Pallas kernels, turn(): pl.pallas_call(turn_kernel, out_shape=(jax.ShapeDtypeStruct((2, 2, BLOCK,...  98.4 us
    pallas_call x1, Pallas kernels, first(): pl.pallas_call(first_kernel, out_shape=(jax.ShapeDtypeStruct((4 * BLOCK,...  90.5 us
    pallas_call x1, Pallas kernels, attend_move(): pl.pallas_call(functools.partial(attend_move_kernel, plan), out_shape=(sd...  82.7 us
    pallas_call x1, Pallas kernels, project(): pl.pallas_call(functools.partial(project_kernel, plan), out_shape=(sds((r...  61.3 us
    pallas_call x1, Pallas kernels, attend_return(): pl.pallas_call(attend_return_kernel, out_shape=(sds((4 * BLOCK, D), bf16)...  37.2 us
    pallas_call x1, Pallas kernels, middle_step(): pl.pallas_call(functools.partial(middle_kernel, plan), out_shape=(sds((ro...  36.5 us
  transfers between devices with their start and end apart: 4, of which 0 were waited for; matrix products, arithmetic and copies ran while one was open for 3% of the time, Pallas kernels for 6%

profile of v2, /device:TPU:0, one launch (start us, length us, event | category | flops | bytes accessed | tf_op | source)
XLA Modules:
  0.0 663.3 jit_solution(2725069434651072871)
XLA Ops:
  0.7 0.8 copy.63
  1.5 0.8 pad_add_fusion
  2.9 1.3 pad.25.forget_ref
  4.2 7.9 %share_facts.1 = (s32[8,8,128]{2,1,0:T(8,128)}, bf16[8,16,128]{2,1,0:T(8,128)(2,1)}) custom-call(s32[8,128]{1,0:T(8,128)} %pad.24.facts_ref, bf16[16,128]{1,0:T(8,128)(2,1)} %pad.25.forget_ref), custom_call_target="tpu_custom_call" | custom-call | tf_op jit(solution)/shard_map/share_facts/pallas_call | solution.py:340
  12.0 0.8 slice.84
  20.1 1.0 constant_dynamic-update-slice_fusion.9
  21.8 0.8 constant_dynamic-update-slice_fusion.8
  24.7 0.8 constant_dynamic-update-slice_fusion.25
  25.5 0.8 constant_dynamic-update-slice_fusion.24
  26.3 0.8 constant_dynamic-update-slice_fusion.23
  33.7 1.3 or_select_fusion
  35.1 90.5 %first.1 = (bf16[512,1536]{1,0:T(8,128)(2,1)}, bf16[8,192,128]{2,1,0:T(8,128)(2,1)}, bf16[8,96,192]{2,1,0:T(8,128)(2,1)}, bf16[8,48,512]{2,1,0:T(8,128)(2,1)}, b...) custom-call(bf16[2,2,128,1536]{3,2,1,0:T(8,128)(2,1)} %bitcast.104, bf16[8,192,128]{2,1,0:T(8,128)(2,1)} %copy-done.17, ...), custom_call_target="tpu_custom_call" | custom-call | tf_op jit(solution)/shard_map/first/pallas_call | solution.py:584
  125.6 61.3 %project.1 = (bf16[512,1536]{1,0:T(8,128)(2,1)}, bf16[512,128]{1,0:T(8,128)(2,1)}, bf16[512,3072]{1,0:T(8,128)(2,1)}, bf16[512,3072]{1,0:T(8,128)(2,1)}, bf16[51...) custom-call(bf16[512,1536]{1,0:T(8,128)(2,1)} %get-tuple-element.80., ...), custom_call_target="tpu_custom_call" | custom-call | tf_op jit(solution)/shard_map/project/pallas_call | solution.py:688
  188.3 82.7 %attend_move.1 = (f32[512,1536]{1,0:T(8,128)}, bf16[512,1536]{1,0:T(8,128)(2,1)}, bf16[24,128,2304]{2,1,0:T(8,128)(2,1)}, bf16[512,1536]{1,0:T(8,128)(2,1)}, bf1...) custom-call(f32[8,128]{1,0:T(8,128)} %broadcast_in_dim.96.ups, f32[24,128]{1,0:T(8,128)} %broadcast_in_dim.101.closed, ...), custom_call_target="tpu_custom_call" | custom-call | tf_op jit(solution)/shard_map/attend_move/pallas_call | solution.py:838
  271.0 36.5 %middle_step.1 = (f32[512,1536]{1,0:T(8,128)}, bf16[512,1536]{1,0:T(8,128)(2,1)}, bf16[512,128]{1,0:T(8,128)(2,1)}, bf16[512,128]{1,0:T(8,128)(2,1)}, bf16[512,1...) custom-call(bf16[512,1536]{1,0:T(8,128)(2,1)} %get-tuple-element.80.x.x_ref, bf16[512,1536]{1,0:T(8,128)(2,1)} %get-tuple-element.92.gated, ...), custom_call_target="tpu_custom_call" | custom-call | tf_op jit(solution)/shard_map/middle_step/pallas_call | solution.py:905
  307.5 2.1 broadcast_25_refs_5__refs_6_.2.refs_5_.refs_6_
  310.2 41.2 %feed.4 = (f32[512,1536]{1,0:T(8,128)}, f32[512,1536]{1,0:T(8,128)}, f32[512,16]{1,0:T(8,128)}, f32[512,16]{1,0:T(8,128)}, f32[512,16]{1,0:T(8,128)}, /*index=5*...) custom-call(bf16[512,1536]{1,0:T(8,128)(2,1)} %get-tuple-element.97.x_ref, bf16[512,128]{1,0:T(8,128)(2,1)} %get-tuple-element.98.slow, ...), custom_call_target="tpu_custom_call" | custom-call | tf_op jit(solution)/shard_map/feed/pallas_call | solution.py:990
  351.4 41.1 %feed.5 = (f32[512,1536]{1,0:T(8,128)}, f32[512,1536]{1,0:T(8,128)}, f32[512,16]{1,0:T(8,128)}, f32[512,16]{1,0:T(8,128)}, f32[512,16]{1,0:T(8,128)}, /*index=5*...) custom-call(bf16[512,1536]{1,0:T(8,128)(2,1)} %get-tuple-element.97.x_ref, bf16[512,128]{1,0:T(8,128)(2,1)} %get-tuple-element.98.slow, ...), custom_call_target="tpu_custom_call" | custom-call | tf_op jit(solution)/shard_map/feed/pallas_call | solution.py:990
  392.6 20.4 %feed.6 = (f32[512,1536]{1,0:T(8,128)}, f32[512,1536]{1,0:T(8,128)}, f32[512,16]{1,0:T(8,128)}, f32[512,16]{1,0:T(8,128)}, f32[512,16]{1,0:T(8,128)}, /*index=5*/bf16[2,48,512]{2,1,0:T(8,128)(2,1)}) custom-call(bf16[512,1536]{1,0:T(8,128)(2,1)} %get-tuple-element.97.x_ref, bf16[512,128]{1,0:T(8,128)(2,1)} %get-tuple-element.98.slow, ...), custom_call_target="tpu_custom_call" | custom-call | tf_op jit(solution)/shard_map/feed/pallas_call | solution.py:990
  413.0 20.7 %feed.7 = (f32[512,1536]{1,0:T(8,128)}, f32[512,1536]{1,0:T(8,128)}, f32[512,16]{1,0:T(8,128)}, f32[512,16]{1,0:T(8,128)}, f32[512,16]{1,0:T(8,128)}, /*index=5*/bf16[2,48,512]{2,1,0:T(8,128)(2,1)}) custom-call(bf16[512,1536]{1,0:T(8,128)(2,1)} %get-tuple-element.97.x_ref, bf16[512,128]{1,0:T(8,128)(2,1)} %get-tuple-element.98.slow, ...), custom_call_target="tpu_custom_call" | custom-call | tf_op jit(solution)/shard_map/feed/pallas_call | solution.py:990
  433.7 1.7 convert.33
  435.4 1.6 copy.66
  437.0 1.6 convert.34
  438.6 1.6 copy.67
  440.5 1.6 copy-done.2
  442.1 3.1 multiply_reduce_fusion
  445.2 2.4 fusion.36
  447.6 1.5 convolution_convert_fusion.7
  449.8 2.4 fusion.8.acc_ref
  452.2 2.6 fusion.1
  454.7 0.8 broadcast_in_dim.105.e_ref
  456.2 8.8 %backward_mm.1 = (f32[512,1536]{1,0:T(8,128)}, f32[512,128]{1,0:T(8,128)}) custom-call(bf16[512,1536]{1,0:T(8,128)(2,1)} %copy-done.5, bf16[1536,1536]{1,0:T(8,128)(2,1)} %get-tuple-element.95.w_ref, bf16[128,1536]{1,0:T(8,128)(2,1)} %broadcast_in_dim.105.e_ref, f32[512,1536]{1,0:T(8,128)} %fusion.8.acc_ref, f32[512,128]{1,0:T(8,128)} %broadcast_in_dim.106.acclow_ref), custom_call_target="tpu_custom_call" | custom-call | flops 2617245696 | bytes 11010048 | tf_op jit(solution)/shard_map/backward_mm/pallas_call | solution.py:233
  465.1 6.9 %multiply_convert_fusion = (bf16[512,1536]{1,0:T(8,128)(2,1)}, bf16[512,1536]{1,0:T(8,128)(2,1)}) fusion(f32[512,1536]{1,0:T(8,128)} %get-tuple-element.126, f32[512,1536]{1,0:T(8,128)} %get-tuple-element.89.gate_ref, f32[512,1536]{1,0:T(8,128)} %get-tuple-element.127.o_ref), kind=kLoop, calls=%fused_computation.4 | loop fusion | flops 7864320 | bytes 12582912 | tf_op jit(solution)/shard_map/convert_element_type | solution.py:1493
  472.0 2.6 dynamic-slice_bitcast_fusion.3
  474.6 4.5 collective-permute-start
  479.1 1.2 collective-permute-start.2
  480.2 4.8 collective-permute-start.3
  485.1 2.1 convolution_convert_fusion.5
  487.2 1.9 convolution_convert_fusion
  489.1 0.9 convolution_convert_fusion.2
  490.5 1.9 convolution_convert_fusion.3
  492.5 1.7 copy.73
  494.2 1.9 convolution_convert_fusion.4
  496.2 1.1 copy.72
  497.3 1.1 copy.71
  498.3 2.2 convolution_convert_fusion.1
  501.6 37.2 %attend_return.1 = (bf16[512,1536]{1,0:T(8,128)(2,1)}, bf16[1024,1536]{1,0:T(8,128)(2,1)}, bf16[1024,1536]{1,0:T(8,128)(2,1)}, f32[512,128]{1,0:T(8,128)}, f32[8,128,128]{2,1,0:T(8,128)}) custom-call(f32[8,128]{1,0:T(8,128)} %broadcast_in_dim.96.ups, bf16[512,1536]{1,0:T(8,128)(2,1)} %get-tuple-element.86.q_ref, ...), custom_call_target="tpu_custom_call" | custom-call | flops 16000000000 | bytes 35000000 | tf_op jit(solution)/shard_map/attend_return/pallas_call | solution.py:1091
  539.5 0.8 pad_maximum_fusion.3.ff
  540.4 2.1 concatenate.69.early
  542.5 0.8 broadcast_select_fusion.a_in
  543.3 1.6 pad_maximum_fusion
  545.0 1.3 pad_maximum_fusion.1
  546.3 98.4 %turn.1 = (bf16[2,2,128,1536]{3,2,1,0:T(8,128)(2,1)}, bf16[4,4,48,512]{3,2,1,0:T(8,128)(2,1)}, bf16[4,4,192,128]{3,2,1,0:T(8,128)(2,1)}, bf16[4,4,192,128]{3,2,1,0:T(8,128)(2,1)}) custom-call(f32[512,128]{1,0:T(8,128)} %get-tuple-element.136.qsum, f32[8,128,128]{2,1,0:T(8,128)} %get-tuple-element.137.ksum, bf16[512,128]{1,0:T(8,128)(2,1)} %get-tuple-element.90.forget.logit, ...), custom_call_target="tpu_custom_call" | custom-call | tf_op jit(solution)/shard_map/turn/pallas_call | solution.py:1309
  644.7 1.7 fusion.6
  646.5 1.1 fusion.37
  647.6 1.1 slice.118
  649.9 0.9 slice_bitcast_fusion
  651.3 1.2 copy.79
  652.5 2.0 pad_maximum_fusion.2
  654.5 1.0 copy.77
  655.5 1.0 copy.80
  656.5 3.5 bitcast_convert_fusion
  660.0 1.1 copy.81
  661.1 0.9 copy.78
  (148 shorter events, 15.9 us)
Async XLA Ops:
  0.6 26.4 %copy-start.9 = (bf16[8,512,16]{1,2,0:T(8,128)(2,1)S(1)}, bf16[8,512,16]{1,2,0:T(8,128)(2,1)}, u32[]{:S(2)}) copy-start(bf16[8,512,16]{1,2,0:T(8,128)(2,1)} %param.32) | copy-start | bytes 393220
  0.6 26.4 %copy-start.7 = (bf16[8,32,512]{2,1,0:T(8,128)(2,1)S(1)}, bf16[8,32,512]{2,1,0:T(8,128)(2,1)}, u32[]{:S(2)}) copy-start(bf16[8,32,512]{2,1,0:T(8,128)(2,1)} %param.35) | copy-start | bytes 786436
  0.7 26.5 %copy-start.20 = (bf16[8,192,128]{2,1,0:T(8,128)(2,1)S(1)}, bf16[8,192,128]{2,1,0:T(8,128)(2,1)}, u32[]{:S(2)}) copy-start(bf16[8,192,128]{2,1,0:T(8,128)(2,1)} %param.31) | copy-start | bytes 1179652
  0.7 26.7 %copy-start.30 = (bf16[192,24]{0,1:T(8,128)(2,1)S(1)}, bf16[192,24]{0,1:T(8,128)(2,1)}, u32[]{:S(2)}) copy-start(bf16[192,24]{0,1:T(8,128)(2,1)} %param.25) | copy-start | bytes 27652
  12.0 18.1 %copy-start.31 = (f32[1536]{0:T(1024)S(1)}, f32[1536]{0:T(1024)}, u32[]{:S(2)}) copy-start(f32[1536]{0:T(1024)} %param.23) | copy-start | bytes 18436
  12.8 17.9 %copy-start.35 = (f32[24]{0:T(128)S(1)}, f32[24]{0:T(128)}, u32[]{:S(2)}) copy-start(f32[24]{0:T(128)} %param.26) | copy-start | bytes 292
  12.8 18.5 %copy-start.32 = (s32[2,4]{1,0:T(2,128)S(1)}, s32[2,4]{1,0:T(2,128)}, u32[]{:S(2)}) copy-start(s32[2,4]{1,0:T(2,128)} %constant.204.clone) | copy-start | bytes 100
  12.8 18.5 %copy-start.33 = (s32[2,4]{1,0:T(2,128)S(1)}, s32[2,4]{1,0:T(2,128)}, u32[]{:S(2)}) copy-start(s32[2,4]{1,0:T(2,128)} %constant.221) | copy-start | bytes 100
  13.6 19.6 %copy-start.29 = (f32[1536]{0:T(1024)S(1)}, f32[1536]{0:T(1024)}, u32[]{:S(2)}) copy-start(f32[1536]{0:T(1024)} %param.28) | copy-start | bytes 18436
  24.7 10.4 %copy-start.18 = (bf16[8,96,192]{2,1,0:T(8,128)(2,1)}, bf16[8,96,192]{2,1,0:T(8,128)(2,1)S(1)}, u32[]{:S(2)}) copy-start(bf16[8,96,192]{2,1,0:T(8,128)(2,1)S(1)} %constant_dynamic-update-slice_fusion.10.model) | copy-start | bytes 884740
  27.2 7.9 %copy-start.19 = (bf16[8,48,512]{2,1,0:T(8,128)(2,1)}, bf16[8,48,512]{2,1,0:T(8,128)(2,1)S(1)}, u32[]{:S(2)}) copy-start(bf16[8,48,512]{2,1,0:T(8,128)(2,1)S(1)} %constant_dynamic-update-slice_fusion.18.ffp) | copy-start | bytes 1179652
  27.4 7.7 %copy-start.17 = (bf16[8,192,128]{2,1,0:T(8,128)(2,1)}, bf16[8,192,128]{2,1,0:T(8,128)(2,1)S(1)}, u32[]{:S(2)}) copy-start(bf16[8,192,128]{2,1,0:T(8,128)(2,1)S(1)} %constant_dynamic-update-slice_fusion.inner) | copy-start | bytes 1179652
  413.0 27.2 %copy-start.1 = (f32[512,1536]{1,0:T(8,128)S(1)}, f32[512,1536]{1,0:T(8,128)}, u32[]{:S(2)}) copy-start(f32[512,1536]{1,0:T(8,128)} %get-tuple-element.96) | copy-start | bytes 9437188
  433.7 6.7 %copy-start.8 = (bf16[8,192,128]{2,1,0:T(8,128)(2,1)S(1)}, bf16[8,192,128]{2,1,0:T(8,128)(2,1)}, u32[]{:S(2)}) copy-start(bf16[8,192,128]{2,1,0:T(8,128)(2,1)} %get-tuple-element.81) | copy-start | bytes 1179652
  440.2 1.9 copy-start.2
  442.1 3.1 copy-start
  447.6 7.1 %copy-start.5 = (bf16[512,1536]{1,0:T(8,128)(2,1)}, bf16[512,1536]{1,0:T(8,128)(2,1)S(1)}, u32[]{:S(2)}) copy-start(bf16[512,1536]{1,0:T(8,128)(2,1)S(1)} %get-tuple-element.176.g_ref) | copy-start | bytes 4718596
  447.6 4.5 copy-start.12
  447.6 4.5 copy-start.14
  449.2 0.6 copy-start.23
  472.0 15.2 %copy-start.3 = (bf16[512,1536]{1,0:T(8,128)(2,1)S(1)}, bf16[512,1536]{1,0:T(8,128)(2,1)}, u32[]{:S(2)}) copy-start(bf16[512,1536]{1,0:T(8,128)(2,1)} %get-tuple-element.97.x_ref) | copy-start | bytes 4718596
  474.6 68.7 %collective-permute-start = (bf16[128,1536]{1,0:T(8,128)(2,1)}, bf16[128,1536]{1,0:T(8,128)(2,1)}, u32[]{:S(2)}, u32[]{:S(2)}) collective-permute-start(bf16[128,1536]{1,0:T(8,128)(2,1)} %get-tuple-element.182), channel_id=1, source_target_pairs={{0,0},{4,1},{1,2},{5,3},{2,4},{6,5},{3,6},{7,7},{8,8},{12,9},{9,10... | collective-permute-start | bytes 1179656 | tf_op jit(solution)/shard_map/ppermute | solution.py:1400
  479.0 64.2 %collective-permute-start.1 = (bf16[128,1536]{1,0:T(8,128)(2,1)}, bf16[128,1536]{1,0:T(8,128)(2,1)}, u32[]{:S(2)}, u32[]{:S(2)}) collective-permute-start(bf16[128,1536]{1,0:T(8,128)(2,1)} %get-tuple-element.185), channel_id=1, source_target_pairs={{4,0},{0,1},{5,2},{1,3},{6,4},{2,5},{7,6},{3,7},{12,8},{8,9},{13,1... | collective-permute-start | bytes 1179656 | tf_op jit(solution)/shard_map/ppermute | solution.py:1400
  479.1 64.2 %collective-permute-start.2 = (bf16[128,1536]{1,0:T(8,128)(2,1)}, bf16[128,1536]{1,0:T(8,128)(2,1)}, u32[]{:S(2)}, u32[]{:S(2)}) collective-permute-start(bf16[128,1536]{1,0:T(8,128)(2,1)} %get-tuple-element.184), channel_id=1, source_target_pairs={{1,0},{5,1},{0,2},{4,3},{3,4},{7,5},{2,6},{6,7},{9,8},{13,9},{8,10... | collective-permute-start | bytes 1179656 | tf_op jit(solution)/shard_map/ppermute | solution.py:1400
  480.2 63.0 %collective-permute-start.3 = (bf16[128,1536]{1,0:T(8,128)(2,1)}, bf16[128,1536]{1,0:T(8,128)(2,1)}, u32[]{:S(2)}, u32[]{:S(2)}) collective-permute-start(bf16[128,1536]{1,0:T(8,128)(2,1)} %get-tuple-element.183), channel_id=1, source_target_pairs={{5,0},{1,1},{4,2},{0,3},{7,4},{3,5},{6,6},{2,7},{13,8},{9,9},{12,1... | collective-permute-start | bytes 1179656 | tf_op jit(solution)/shard_map/ppermute | solution.py:1400
  485.1 4.0 copy-start.10
  485.1 3.9 copy-start.24
  487.2 3.4 copy-start.4
  489.1 5.1 copy-start.6
  496.2 4.7 copy-start.21
  496.2 4.9 copy-start.22
  501.5 37.9 %copy-start.25 = (bf16[2,48,512]{2,1,0:T(8,128)(2,1)S(1)}, bf16[2,48,512]{2,1,0:T(8,128)(2,1)}, u32[]{:S(2)}) copy-start(bf16[2,48,512]{2,1,0:T(8,128)(2,1)} %get-tuple-element.141) | copy-start | bytes 294916
  501.5 37.9 %copy-start.26 = (bf16[2,48,512]{2,1,0:T(8,128)(2,1)S(1)}, bf16[2,48,512]{2,1,0:T(8,128)(2,1)}, u32[]{:S(2)}) copy-start(bf16[2,48,512]{2,1,0:T(8,128)(2,1)} %get-tuple-element.142) | copy-start | bytes 294916
  501.5 37.9 %copy-start.27 = (bf16[2,48,512]{2,1,0:T(8,128)(2,1)S(1)}, bf16[2,48,512]{2,1,0:T(8,128)(2,1)}, u32[]{:S(2)}) copy-start(bf16[2,48,512]{2,1,0:T(8,128)(2,1)} %get-tuple-element.143) | copy-start | bytes 294916
  501.5 37.9 %copy-start.28 = (bf16[2,48,512]{2,1,0:T(8,128)(2,1)S(1)}, bf16[2,48,512]{2,1,0:T(8,128)(2,1)}, u32[]{:S(2)}) copy-start(bf16[2,48,512]{2,1,0:T(8,128)(2,1)} %get-tuple-element.144) | copy-start | bytes 294916
  501.5 38.8 %copy-start.13 = (bf16[1536,16]{1,0:T(8,128)(2,1)S(1)}, bf16[1536,16]{1,0:T(8,128)(2,1)}, u32[]{:S(2)}) copy-start(bf16[1536,16]{1,0:T(8,128)(2,1)} %copy.73) | copy-start | bytes 147460
  538.8 3.7 copy-start.34
  644.7 4.0 copy-start.16
  647.6 1.8 copy-start.15
  649.3 1.5 copy-start.11
  655.5 4.5 slice-start
